TPU v7x, 32 devices: a whole 2x2x4 slice. The times are simulated.
32 devices in a mesh: fsdp: 8 (over y, x, core), context: 4 (over z).
Axes of the slice: x: 2, y: 2, z: 4, core: 2. Of those that a mesh axis runs over, the one named last changes fastest.
Arguments:
- hidden_in: bfloat16 [8, 1024, 1536], P('fsdp', 'context'), may hold values from -6 to 6
- cotangent: bfloat16 [8, 1024, 1536], P('fsdp', 'context'), may hold values from -6 to 6
- seq_lengths: int32 [8], P('fsdp'), may hold values from 1 to 1024, 6144 in all
- tile_place: int32 [8, 8], P('fsdp'), may hold values from 0 to 7, each once within a row
- norm_attn: bfloat16 [2, 1536], P(None, 'fsdp'), may hold values from 0.25 to 1.75
- w_qkv: bfloat16 [2, 1536, 2048], P(None, 'fsdp'), may hold values from -0.15625 to 0.15625
- b_qkv: bfloat16 [2, 2048], P(None, 'fsdp'), may hold values from -3 to 3
- w_out: bfloat16 [2, 1536, 1536], P(None, 'fsdp'), may hold values from -0.625 to 0.625
- norm_mlp: bfloat16 [2, 1536], P(None, 'fsdp'), may hold values from 0.25 to 1.75
- w_gate: bfloat16 [2, 1536, 8960], P(None, 'fsdp', 'context'), may hold values from -0.15625 to 0.15625
- w_up: bfloat16 [2, 1536, 8960], P(None, 'fsdp', 'context'), may hold values from -0.15625 to 0.15625
- w_down: bfloat16 [2, 8960, 1536], P(None, 'context', 'fsdp'), may hold values from -0.0625 to 0.0625
Outputs:
- layer_out: bfloat16 [8, 1024, 1536], P('fsdp', 'context')
- grad_in: float32 [8, 1024, 1536], P('fsdp', 'context')
- grad_norm_attn: float32 [2, 1536], P(None, 'fsdp')
- grad_w_qkv: float32 [2, 1536, 2048], P(None, 'fsdp')
- grad_b_qkv: float32 [2, 2048], P(None, 'fsdp')
- grad_w_out: float32 [2, 1536, 1536], P(None, 'fsdp')
- grad_norm_mlp: float32 [2, 1536], P(None, 'fsdp')
- grad_w_gate: float32 [2, 1536, 8960], P(None, 'fsdp', 'context')
- grad_w_up: float32 [2, 1536, 8960], P(None, 'fsdp', 'context')
- grad_w_down: float32 [2, 8960, 1536], P(None, 'context', 'fsdp')
Inputs may be any that keep to these rules, and one draw needn't show every extreme that they name: `seq_lengths`: each index of fsdp holds one sequence of this many tokens, padded to 1024 rows; some sequence has exactly 1024. For each index of fsdp a permutation: rows 128 * j to 128 * j + 127 hold tile tile_place[j] of the sequence.
All inputs are finite; a program needn't handle non-finite values. No bound on the sum of `seq_lengths` on one device may be relied on, other than what follows from the above.
Results may differ from a plain program's by a relative error of at most 0.022.
Values may be sent and summed in bfloat16 or wider, within the bound.
A program may use at most 320 MiB of HBM per device.

v0:
```python
import math

import jax
import jax.numpy as jnp
from jax import lax
from jax.sharding import PartitionSpec as P

QUERY_HEADS = 12
KEY_VALUE_HEADS = 2
HEAD_SIZE = 128
LAYERS = 2
TILE = 128


EPSILON = 1e-06
ROPE_BASE = 1000000.0


def normalize(stream, gain):
    return stream * lax.rsqrt(jnp.mean(stream * stream, axis=-1, keepdims=True) + EPSILON) * gain


def apply_rotation(heads, cosine_table, sine_values):
    half_width = heads.shape[-1] // 2
    first_half = heads[..., :half_width]
    second = heads[..., half_width:]
    return jnp.concatenate(
        [
            first_half * cosine_table - second * sine_values,
            second * cosine_table + first_half * sine_values,
        ],
        axis=-1,
    )


def unrotate(grads, cosine_table, sine_values):
    half_width = grads.shape[-1] // 2
    first_half = grads[..., :half_width]
    second = grads[..., half_width:]
    return jnp.concatenate(
        [
            first_half * cosine_table + second * sine_values,
            second * cosine_table - first_half * sine_values,
        ],
        axis=-1,
    )


def frequencies():
    return jnp.power(ROPE_BASE, -(jnp.arange(HEAD_SIZE // 2, dtype=jnp.float32) * 2.0 / HEAD_SIZE))


def fetch_layer(norm_attn, w_qkv, b_qkv, w_out, norm_mlp, w_gate, w_up, w_down, layer_index):
    fetched = (
        lax.all_gather(norm_attn[layer_index], "fsdp", axis=0, tiled=True),
        lax.all_gather(w_qkv[layer_index], "fsdp", axis=0, tiled=True),
        lax.all_gather(b_qkv[layer_index], "fsdp", axis=0, tiled=True),
        lax.all_gather(w_out[layer_index], "fsdp", axis=0, tiled=True),
        lax.all_gather(norm_mlp[layer_index], "fsdp", axis=0, tiled=True),
        lax.all_gather(w_gate[layer_index], "fsdp", axis=0, tiled=True),
        lax.all_gather(w_up[layer_index], "fsdp", axis=0, tiled=True),
        lax.all_gather(w_down[layer_index], "fsdp", axis=1, tiled=True),
    )
    return (fetched[:5], fetched[5:])


def fetch_layer_again(norm_attn, w_qkv, b_qkv, w_out, norm_mlp, w_gate, w_up, w_down, layer_index):
    fetched = (
        lax.all_gather(norm_attn[layer_index], "fsdp", axis=0, tiled=True),
        lax.all_gather(w_qkv[layer_index], "fsdp", axis=0, tiled=True),
        lax.all_gather(b_qkv[layer_index], "fsdp", axis=0, tiled=True),
        lax.all_gather(w_out[layer_index], "fsdp", axis=0, tiled=True),
        lax.all_gather(norm_mlp[layer_index], "fsdp", axis=0, tiled=True),
        lax.all_gather(w_gate[layer_index], "fsdp", axis=0, tiled=True),
        lax.all_gather(w_up[layer_index], "fsdp", axis=0, tiled=True),
        lax.all_gather(w_down[layer_index], "fsdp", axis=1, tiled=True),
    )
    return (fetched[:5], fetched[5:])


def split_kv(grouped_key_value):
    key_value_width = KEY_VALUE_HEADS * HEAD_SIZE
    gathered_keys = grouped_key_value[:, :key_value_width].reshape(
        grouped_key_value.shape[0], KEY_VALUE_HEADS, HEAD_SIZE
    )
    gathered_values = grouped_key_value[:, key_value_width:].reshape(
        grouped_key_value.shape[0], KEY_VALUE_HEADS, HEAD_SIZE
    )
    return (gathered_keys, gathered_values)


def score_table(query_rows, gathered_keys, allowed):
    inv_root = 1.0 / math.sqrt(HEAD_SIZE)
    scores = (
        jnp.einsum("tgrd,kgd->grtk", query_rows, gathered_keys, preferred_element_type=jnp.float32)
        * inv_root
    )
    return jnp.where(allowed, scores, -1e30)


def forward_layer(stream, attn_set, ffn_set, allowed, cosine_table, sine_values):
    gain_one, qkv_w, qkv_b, out_w, gain_two = attn_set
    gate_w, up_w, down_w = ffn_set
    resident_rows = stream.shape[0]
    query_heads_width = QUERY_HEADS * HEAD_SIZE
    key_value_width = KEY_VALUE_HEADS * HEAD_SIZE
    normed = normalize(stream, gain_one.astype(jnp.float32)).astype(jnp.bfloat16)
    projected_output = jnp.dot(normed, qkv_w, preferred_element_type=jnp.float32) + qkv_b.astype(
        jnp.float32
    )
    query_rows = apply_rotation(
        projected_output[:, :query_heads_width].reshape(resident_rows, QUERY_HEADS, HEAD_SIZE),
        cosine_table,
        sine_values,
    ).astype(jnp.bfloat16)
    keys_local = apply_rotation(
        projected_output[:, query_heads_width : query_heads_width + key_value_width].reshape(
            resident_rows, KEY_VALUE_HEADS, HEAD_SIZE
        ),
        cosine_table,
        sine_values,
    ).astype(jnp.bfloat16)
    values_local = projected_output[:, query_heads_width + key_value_width :].astype(jnp.bfloat16)
    local_kv = jnp.concatenate(
        [keys_local.reshape(resident_rows, key_value_width), values_local], axis=1
    )
    grouped_key_value = lax.all_gather(local_kv, "context", axis=0, tiled=True)
    gathered_keys, gathered_values = split_kv(grouped_key_value)
    query_rows = query_rows.reshape(
        resident_rows, KEY_VALUE_HEADS, QUERY_HEADS // KEY_VALUE_HEADS, HEAD_SIZE
    )
    scores = score_table(query_rows, gathered_keys, allowed)
    peak_score = jnp.max(scores, axis=-1, keepdims=True)
    exponents = jnp.exp(scores - peak_score)
    denominator = jnp.sum(exponents, axis=-1, keepdims=True)
    softmax_weights = exponents / denominator
    log_total = peak_score + jnp.log(denominator)
    attended_output = jnp.einsum(
        "grtk,kgd->tgrd", softmax_weights, gathered_values.astype(jnp.float32)
    ).reshape(resident_rows, query_heads_width)
    attn_mixed = attended_output.astype(jnp.bfloat16)
    middle = stream + jnp.dot(attn_mixed, out_w, preferred_element_type=jnp.float32)
    normed_two = normalize(middle, gain_two.astype(jnp.float32)).astype(jnp.bfloat16)
    block_rows = lax.all_gather(normed_two, "context", axis=0, tiled=True)
    gate_value = jnp.dot(block_rows, gate_w, preferred_element_type=jnp.float32)
    up_value = jnp.dot(block_rows, up_w, preferred_element_type=jnp.float32)
    expand_hidden = (jax.nn.silu(gate_value) * up_value).astype(jnp.bfloat16)
    normed_all, gate_value, up_value, hidden = (block_rows, gate_value, up_value, expand_hidden)
    result = middle + lax.psum_scatter(
        jnp.dot(hidden, down_w, preferred_element_type=jnp.float32).astype(jnp.bfloat16),
        "context",
        scatter_dimension=0,
        tiled=True,
    ).astype(jnp.float32)
    stored = (
        stream,
        normed,
        query_rows,
        grouped_key_value,
        attended_output,
        log_total,
        middle,
        normed_all,
        gate_value,
        up_value,
        hidden,
    )
    return (result, stored)


def backward_layer(gradient, stored, attn_set, ffn_set, allowed, cosine_table, sine_values):
    (
        stream,
        normed,
        query_rows,
        grouped_key_value,
        attended_output,
        log_total,
        middle,
        normed_all,
        gate_value,
        up_value,
        hidden,
    ) = stored
    gain_one, qkv_w, qkv_b, out_w, gain_two = attn_set
    gate_w, up_w, down_w = ffn_set
    resident_rows = gradient.shape[0]
    query_heads_width = QUERY_HEADS * HEAD_SIZE
    key_value_width = KEY_VALUE_HEADS * HEAD_SIZE
    inv_root = 1.0 / math.sqrt(HEAD_SIZE)
    grad_low = gradient.astype(jnp.bfloat16)
    grad_all = lax.all_gather(grad_low, "context", axis=0, tiled=True)
    down_grad = jnp.einsum("tf,td->fd", hidden, grad_all, preferred_element_type=jnp.float32)
    hidden_grad = jnp.einsum("td,fd->tf", grad_all, down_w, preferred_element_type=jnp.float32)
    sigmoid_gate = jax.nn.sigmoid(gate_value)
    gate_grad = (
        hidden_grad * up_value * sigmoid_gate * (1.0 + gate_value * (1.0 - sigmoid_gate))
    ).astype(jnp.bfloat16)
    up_grad = (hidden_grad * gate_value * sigmoid_gate).astype(jnp.bfloat16)
    gate_w_grad = jnp.einsum("td,tf->df", normed_all, gate_grad, preferred_element_type=jnp.float32)
    up_w_grad = jnp.einsum("td,tf->df", normed_all, up_grad, preferred_element_type=jnp.float32)
    first_term = jnp.einsum("tf,df->td", gate_grad, gate_w, preferred_element_type=jnp.float32)
    normed_two_grad = lax.psum_scatter(
        (
            first_term + jnp.einsum("tf,df->td", up_grad, up_w, preferred_element_type=jnp.float32)
        ).astype(jnp.bfloat16),
        "context",
        scatter_dimension=0,
        tiled=True,
    ).astype(jnp.float32)
    ffn_grads = (
        lax.psum_scatter(
            gate_w_grad.astype(jnp.bfloat16), "fsdp", scatter_dimension=0, tiled=True
        ).astype(jnp.float32),
        lax.psum_scatter(
            up_w_grad.astype(jnp.bfloat16), "fsdp", scatter_dimension=0, tiled=True
        ).astype(jnp.float32),
        lax.psum_scatter(
            down_grad.astype(jnp.bfloat16), "fsdp", scatter_dimension=1, tiled=True
        ).astype(jnp.float32),
    )
    unused_two, norm_pullback = jax.vjp(normalize, middle, gain_two.astype(jnp.float32))
    middle_grad, gain_two_grad = norm_pullback(normed_two_grad)
    middle_grad = gradient + middle_grad
    middle_low = middle_grad.astype(jnp.bfloat16)
    attn_mixed = attended_output.astype(jnp.bfloat16)
    mixed_heads_gradient = jnp.einsum(
        "td,cd->tc", middle_low, out_w, preferred_element_type=jnp.float32
    ).astype(jnp.bfloat16)
    combined_heads = mixed_heads_gradient.reshape(
        resident_rows, KEY_VALUE_HEADS, QUERY_HEADS // KEY_VALUE_HEADS, HEAD_SIZE
    )
    mixed_heads_float = combined_heads.astype(jnp.float32)
    gathered_keys, gathered_values = split_kv(grouped_key_value)
    scores = score_table(query_rows, gathered_keys, allowed)
    softmax_weights = jnp.exp(scores - log_total)
    prob_grad = jnp.einsum(
        "tgrd,kgd->grtk", combined_heads, gathered_values, preferred_element_type=jnp.float32
    )
    row_dot = jnp.einsum(
        "ixou,ixou->xoi",
        mixed_heads_float,
        attended_output.reshape(
            resident_rows, KEY_VALUE_HEADS, QUERY_HEADS // KEY_VALUE_HEADS, HEAD_SIZE
        ),
    )[..., None]
    score_grad = softmax_weights * (prob_grad - row_dot) * inv_root
    query_grad = jnp.einsum("grtk,kgd->tgrd", score_grad, gathered_keys.astype(jnp.float32))
    key_grad = jnp.einsum("grtk,tgrd->kgd", score_grad, query_rows.astype(jnp.float32))
    value_grad = jnp.einsum("grtk,tgrd->kgd", softmax_weights, mixed_heads_float)
    group_rows = grouped_key_value.shape[0]
    key_value_gradient = jnp.concatenate(
        [
            key_grad.reshape(group_rows, key_value_width),
            value_grad.reshape(group_rows, key_value_width),
        ],
        axis=1,
    )
    key_value_gradient = lax.psum_scatter(
        key_value_gradient.astype(jnp.bfloat16), "context", scatter_dimension=0, tiled=True
    ).astype(jnp.float32)
    query_grad = unrotate(
        query_grad.reshape(resident_rows, QUERY_HEADS, HEAD_SIZE), cosine_table, sine_values
    )
    key_local_grad = unrotate(
        key_value_gradient[:, :key_value_width].reshape(resident_rows, KEY_VALUE_HEADS, HEAD_SIZE),
        cosine_table,
        sine_values,
    )
    projected_grad = jnp.concatenate(
        [
            query_grad.reshape(resident_rows, query_heads_width),
            key_local_grad.reshape(resident_rows, key_value_width),
            key_value_gradient[:, key_value_width:],
        ],
        axis=1,
    ).astype(jnp.bfloat16)
    qkv_b_grad = jnp.sum(projected_grad.astype(jnp.float32), axis=0)
    normed_grad = jnp.einsum("tc,dc->td", projected_grad, qkv_w, preferred_element_type=jnp.float32)
    unused_one, first_pullback = jax.vjp(normalize, stream, gain_one.astype(jnp.float32))
    stream_grad, gain_one_grad = first_pullback(normed_grad)
    qkv_w_grad = jnp.einsum("td,tc->dc", normed, projected_grad, preferred_element_type=jnp.float32)
    out_w_grad = jnp.einsum("tc,td->cd", attn_mixed, middle_low, preferred_element_type=jnp.float32)
    attn_grads = (
        lax.psum_scatter(
            gain_one_grad.astype(jnp.bfloat16), "fsdp", scatter_dimension=0, tiled=True
        ).astype(jnp.float32),
        lax.psum_scatter(
            qkv_w_grad.astype(jnp.bfloat16), "fsdp", scatter_dimension=0, tiled=True
        ).astype(jnp.float32),
        lax.psum_scatter(
            qkv_b_grad.astype(jnp.bfloat16), "fsdp", scatter_dimension=0, tiled=True
        ).astype(jnp.float32),
        lax.psum_scatter(
            out_w_grad.astype(jnp.bfloat16), "fsdp", scatter_dimension=0, tiled=True
        ).astype(jnp.float32),
        lax.psum_scatter(
            gain_two_grad.astype(jnp.bfloat16), "fsdp", scatter_dimension=0, tiled=True
        ).astype(jnp.float32),
    )
    attn_grads = (
        lax.psum(attn_grads[0].astype(jnp.bfloat16), "context").astype(jnp.float32),
        lax.psum(attn_grads[1].astype(jnp.bfloat16), "context").astype(jnp.float32),
        lax.psum(attn_grads[2].astype(jnp.bfloat16), "context").astype(jnp.float32),
        lax.psum(attn_grads[3].astype(jnp.bfloat16), "context").astype(jnp.float32),
        lax.psum(attn_grads[4].astype(jnp.bfloat16), "context").astype(jnp.float32),
    )
    return (middle_grad + stream_grad, attn_grads, ffn_grads)


def shards(
    hidden_in,
    cotangent,
    seq_lengths,
    tile_place,
    norm_attn,
    w_qkv,
    b_qkv,
    w_out,
    norm_mlp,
    w_gate,
    w_up,
    w_down,
):
    resident_rows = hidden_in.shape[1]
    group_rows = resident_rows * lax.axis_size("context")
    tile_order = tile_place[0]
    tile_count = tile_order.shape[0]
    row_index = jnp.arange(group_rows, dtype=jnp.int32)
    selector = (
        row_index[:, None] // TILE == jnp.arange(tile_count, dtype=jnp.int32)[None, :]
    ).astype(jnp.int32)
    tile_ids = jnp.sum(selector * tile_order[None, :], axis=1)
    position = tile_ids * TILE + row_index % TILE
    validity = position < seq_lengths[0]
    offset = lax.axis_index("context") * resident_rows
    my_position = lax.dynamic_slice_in_dim(position, offset, resident_rows)
    my_validity = lax.dynamic_slice_in_dim(validity, offset, resident_rows)
    allowed = (position[None, :] <= my_position[:, None]) & validity[None, :]
    angles = my_position.astype(jnp.float32)[:, None] * frequencies()
    cosine_table = jnp.cos(angles)[:, None, :]
    sine_values = jnp.sin(angles)[:, None, :]
    stream = hidden_in[0].astype(jnp.float32)
    stored_all = []
    attn_sets = []
    ffn_sets = []
    for layer_index in range(LAYERS):
        attn_set, ffn_set = fetch_layer(
            norm_attn, w_qkv, b_qkv, w_out, norm_mlp, w_gate, w_up, w_down, layer_index
        )
        stream, stored = forward_layer(
            stream, attn_set, ffn_set, allowed, cosine_table, sine_values
        )
        stored_all.append(stored)
        attn_sets.append(attn_set)
        ffn_sets.append(ffn_set)
    layer_out = stream.astype(jnp.bfloat16)[None]
    gradient = cotangent[0].astype(jnp.float32) * my_validity[:, None].astype(jnp.float32)
    attn_list = [None] * LAYERS
    ffn_list = [None] * LAYERS
    for layer_index in reversed(range(LAYERS)):
        attn_set, ffn_set = fetch_layer_again(
            norm_attn, w_qkv, b_qkv, w_out, norm_mlp, w_gate, w_up, w_down, layer_index
        )
        gradient, attn_grads, ffn_grads = backward_layer(
            gradient, stored_all[layer_index], attn_set, ffn_set, allowed, cosine_table, sine_values
        )
        attn_list[layer_index] = attn_grads
        ffn_list[layer_index] = ffn_grads
    grad_norm_attn = jnp.stack([attn_list[index][0] for index in range(LAYERS)])
    grad_w_qkv = jnp.stack([attn_list[index][1] for index in range(LAYERS)])
    grad_b_qkv = jnp.stack([attn_list[index][2] for index in range(LAYERS)])
    grad_w_out = jnp.stack([attn_list[index][3] for index in range(LAYERS)])
    grad_norm_mlp = jnp.stack([attn_list[index][4] for index in range(LAYERS)])
    grad_w_gate = jnp.stack([ffn_list[index][0] for index in range(LAYERS)])
    grad_w_up = jnp.stack([ffn_list[index][1] for index in range(LAYERS)])
    grad_w_down = jnp.stack([ffn_list[index][2] for index in range(LAYERS)])
    return (
        layer_out,
        gradient[None],
        grad_norm_attn,
        grad_w_qkv,
        grad_b_qkv,
        grad_w_out,
        grad_norm_mlp,
        grad_w_gate,
        grad_w_up,
        grad_w_down,
    )


def solution(mesh):
    return jax.shard_map(
        shards,
        mesh=mesh,
        in_specs=(
            P("fsdp", "context", None),
            P("fsdp", "context", None),
            P("fsdp"),
            P("fsdp", None),
            P(None, "fsdp"),
            P(None, "fsdp", None),
            P(None, "fsdp"),
            P(None, "fsdp", None),
            P(None, "fsdp"),
            P(None, "fsdp", "context"),
            P(None, "fsdp", "context"),
            P(None, "context", "fsdp"),
        ),
        out_specs=(
            P("fsdp", "context", None),
            P("fsdp", "context", None),
            P(None, "fsdp"),
            P(None, "fsdp", None),
            P(None, "fsdp"),
            P(None, "fsdp", None),
            P(None, "fsdp"),
            P(None, "fsdp", "context"),
            P(None, "fsdp", "context"),
            P(None, "context", "fsdp"),
        ),
        check_vma=False,
    )
```

profile of v0, /device:TPU:0, one launch (start us, length us, event | category | flops | bytes accessed | tf_op | source)
XLA Modules:
  0.0 2065.3 jit_solution(15504401212442406134)
XLA Ops:
  12.5 26.8 %all-reduce.11 = (bf16[1536]{0:T(1024)(128)(2,1)S(1)}, bf16[1536]{0:T(1024)(128)(2,1)S(1)}, bf16[1536]{0:T(1024)(128)(2,1)}, bf16[1536]{0:T(1024)(128)(2,1)}) all-reduce(bf16[1536]{0:T(1024)(128)(2,1)S(1)} %dynamic-update-slice, bf16[1536]{0:T(1024)(128)(2,1)S(1)} %dynamic-update-slice.1, ...), channel_id=2, replica_groups=mesh['fsdp'=8,'context'=4] {'fsdp'}, use_global_device_ids=true, to_apply=%add | all-reduce | flops 6144 | bytes 24576
  80.6 14.1 all-gather.33.cloned.1.call-done
  113.0 22.4 %all-gather.47.cloned.1.call-done = bf16[1,1536,1536]{2,1,0:T(8,128)(2,1)} async-done(((bf16[1,192,1536]{2,1,0:T(8,128)(2,1)}), bf16[1,1536,1536]{2,1,0:T(8,128)(2,1)}) %all-gather.47.cloned.1.call-update) | async-done | bytes 4718608 | tf_op jit(solution)/shard_map/all_gather | solution.py:58
  147.1 39.4 %all-gather.49.cloned.1.call-done = bf16[1,1536,2240]{2,1,0:T(8,128)(2,1)} async-done(((bf16[1,192,2240]{2,1,0:T(8,128)(2,1)}), bf16[1,1536,2240]{2,1,0:T(8,128)(2,1)}) %all-gather.49.cloned.1.call-update) | async-done | bytes 6881296 | tf_op jit(solution)/shard_map/all_gather | solution.py:60
  186.5 64.9 %all-gather.35.cloned.1.call-done = bf16[1024,1536]{1,0:T(8,128)(2,1)} async-done(((bf16[256,1536]{1,0:T(8,128)(2,1)}), bf16[1024,1536]{1,0:T(8,128)(2,1)}) %all-gather.35.cloned.1.call-update) | async-done | bytes 3145744 | tf_op jit(solution)/shard_map/all_gather | solution.py:144
  251.4 13.3 fusion.34
  264.6 35.9 %all-gather.51.cloned.1.call-done = bf16[1,1536,2240]{2,1,0:T(8,128)(2,1)} async-done(((bf16[1,192,2240]{2,1,0:T(8,128)(2,1)}), bf16[1,1536,2240]{2,1,0:T(8,128)(2,1)}) %all-gather.51.cloned.1.call-update) | async-done | bytes 6881296 | tf_op jit(solution)/shard_map/all_gather | solution.py:61
  300.5 16.7 multiply_convert_fusion.5
  317.3 34.5 %all-gather.53.cloned.1.call-done = bf16[1,2240,1536]{1,2,0:T(8,128)(2,1)} async-done(((bf16[1,2240,192]{1,2,0:T(8,128)(2,1)}), bf16[1,2240,1536]{1,2,0:T(8,128)(2,1)}) %all-gather.53.cloned.1.call-update) | async-done | bytes 6881296 | tf_op jit(solution)/shard_map/all_gather | solution.py:62
  351.7 12.8 fusion.76
  374.2 50.8 %reduce-scatter.17.cloned.1.call-done = bf16[256,1536]{1,0:T(8,128)(2,1)} async-done(((bf16[1024,1536]{1,0:T(8,128)(2,1)}), bf16[256,1536]{1,0:T(8,128)(2,1)}) %reduce-scatter.17.cloned.1.call-update) | async-done | bytes 786448 | tf_op jit(solution)/shard_map/reduce_scatter | solution.py:149
  427.1 45.8 %all-gather.55.cloned.1.call-done = bf16[1,1536,2048]{2,1,0:T(8,128)(2,1)} async-done(((bf16[1,192,2048]{2,1,0:T(8,128)(2,1)}), bf16[1,1536,2048]{2,1,0:T(8,128)(2,1)}) %all-gather.55.cloned.1.call-update) | async-done | bytes 6291472 | tf_op jit(solution)/shard_map/all_gather | solution.py:56
  492.9 16.0 all-gather.37.cloned.1.call-done
  530.3 18.6 all-gather.57.cloned.1.call-done
  554.8 59.7 %all-gather.41.cloned.1.call-done = bf16[1024,1536]{1,0:T(8,128)(2,1)} async-done(((bf16[256,1536]{1,0:T(8,128)(2,1)}), bf16[1024,1536]{1,0:T(8,128)(2,1)}) %all-gather.41.cloned.1.call-update) | async-done | bytes 3145744 | tf_op jit(solution)/shard_map/all_gather | solution.py:192
  614.4 49.9 %all-gather.63.cloned.1.call-done = bf16[1,2240,1536]{1,2,0:T(8,128)(2,1)} async-done(((bf16[1,2240,192]{1,2,0:T(8,128)(2,1)}), bf16[1,2240,1536]{1,2,0:T(8,128)(2,1)}) %all-gather.63.cloned.1.call-update) | async-done | bytes 6881296 | tf_op jit(solution)/shard_map/all_gather | solution.py:62
  664.3 13.4 fusion.12
  677.6 37.1 %all-gather.61.cloned.1.call-done = bf16[1,1536,2240]{2,1,0:T(8,128)(2,1)} async-done(((bf16[1,192,2240]{2,1,0:T(8,128)(2,1)}), bf16[1,1536,2240]{2,1,0:T(8,128)(2,1)}) %all-gather.61.cloned.1.call-update) | async-done | bytes 6881296 | tf_op jit(solution)/shard_map/all_gather | solution.py:61
  714.8 65.5 %all-gather.39.cloned.1.call-done = bf16[1024,1536]{1,0:T(8,128)(2,1)} async-done(((bf16[256,1536]{1,0:T(8,128)(2,1)}), bf16[1024,1536]{1,0:T(8,128)(2,1)}) %all-gather.39.cloned.1.call-update) | async-done | bytes 3145744 | tf_op jit(solution)/shard_map/all_gather | solution.py:144
  780.2 13.2 fusion.18
  793.4 36.5 %all-gather.59.cloned.1.call-done = bf16[1,1536,2240]{2,1,0:T(8,128)(2,1)} async-done(((bf16[1,192,2240]{2,1,0:T(8,128)(2,1)}), bf16[1,1536,2240]{2,1,0:T(8,128)(2,1)}) %all-gather.59.cloned.1.call-update) | async-done | bytes 6881296 | tf_op jit(solution)/shard_map/all_gather | solution.py:60
  829.9 20.6 multiply_convert_fusion.3
  871.7 12.4 fusion.79
  884.3 47.9 %reduce-scatter.21.cloned.1.call-done = bf16[256,1536]{1,0:T(8,128)(2,1)} async-done(((bf16[1024,1536]{1,0:T(8,128)(2,1)}), bf16[256,1536]{1,0:T(8,128)(2,1)}) %reduce-scatter.21.cloned.1.call-update) | async-done | bytes 786448 | tf_op jit(solution)/shard_map/reduce_scatter | solution.py:203
  934.4 60.9 %reduce-scatter.19.cloned.1.call-done = bf16[256,1536]{1,0:T(8,128)(2,1)} async-done(((bf16[1024,1536]{1,0:T(8,128)(2,1)}), bf16[256,1536]{1,0:T(8,128)(2,1)}) %reduce-scatter.19.cloned.1.call-update) | async-done | bytes 786448 | tf_op jit(solution)/shard_map/reduce_scatter | solution.py:149
  1028.7 22.9 %reduce-scatter.23.cloned.1.call-done = bf16[256,512]{0,1:T(8,128)(2,1)} async-done(((bf16[1024,512]{0,1:T(8,128)(2,1)}), bf16[256,512]{0,1:T(8,128)(2,1)}) %reduce-scatter.23.cloned.1.call-update) | async-done | bytes 262160 | tf_op jit(solution)/shard_map/reduce_scatter | solution.py:259
  1062.8 62.0 %all-gather.43.cloned.1.call-done = bf16[1024,1536]{1,0:T(8,128)(2,1)} async-done(((bf16[256,1536]{1,0:T(8,128)(2,1)}), bf16[1024,1536]{1,0:T(8,128)(2,1)}) %all-gather.43.cloned.1.call-update) | async-done | bytes 3145744 | tf_op jit(solution)/shard_map/all_gather | solution.py:192
  1124.9 20.6 multiply_convert_fusion.1
  1156.8 11.5 add_convert_fusion
  1169.8 57.7 %reduce-scatter.25.cloned.1.call-done = bf16[256,1536]{1,0:T(8,128)(2,1)} async-done(((bf16[1024,1536]{1,0:T(8,128)(2,1)}), bf16[256,1536]{1,0:T(8,128)(2,1)}) %reduce-scatter.25.cloned.1.call-update) | async-done | bytes 786448 | tf_op jit(solution)/shard_map/reduce_scatter | solution.py:203
  1298.8 12.8 convolution_convert_fusion.4
  1311.7 12.3 convolution_convert_fusion.5
  1324.5 12.5 convolution_convert_fusion.2
  1337.1 12.4 convolution_convert_fusion.3
  1349.6 12.7 convolution_convert_fusion
  1362.6 12.4 convolution_convert_fusion.1
  1378.5 27.7 %reduce-scatter.31.cloned.1.call-done = bf16[192,2048]{1,0:T(8,128)(2,1)} async-done(((bf16[1536,2048]{1,0:T(8,128)(2,1)}), bf16[192,2048]{1,0:T(8,128)(2,1)}) %reduce-scatter.31.cloned.1.call-update) | async-done | bytes 786448 | tf_op jit(solution)/shard_map/reduce_scatter | solution.py:288
  1406.1 57.3 %reduce-scatter.33.cloned.1.call-done = bf16[192,1536]{1,0:T(8,128)(2,1)} async-done(((bf16[1536,1536]{1,0:T(8,128)(2,1)}), bf16[192,1536]{1,0:T(8,128)(2,1)}) %reduce-scatter.33.cloned.1.call-update) | async-done | bytes 589840 | tf_op jit(solution)/shard_map/reduce_scatter | solution.py:294
  1463.4 65.0 %reduce-scatter.29.cloned.1.call-done = bf16[192,2048]{1,0:T(8,128)(2,1)} async-done(((bf16[1536,2048]{1,0:T(8,128)(2,1)}), bf16[192,2048]{1,0:T(8,128)(2,1)}) %reduce-scatter.29.cloned.1.call-update) | async-done | bytes 786448 | tf_op jit(solution)/shard_map/reduce_scatter | solution.py:288
  1534.9 22.9 %all-reduce.10 = (bf16[1536]{0:T(1024)(128)(2,1)S(1)}, bf16[1536]{0:T(1024)(128)(2,1)S(1)}, bf16[2048]{0:T(1024)(128)(2,1)S(1)}, bf16[2048]{0:T(1024)(128)(2,1)S...) all-reduce(bf16[1536]{0:T(1024)(128)(2,1)S(1)} %copy-done.89, ...), channel_id=25, replica_groups=mesh['fsdp'=8,'context'=4] {'fsdp'}, use_global_device_ids=true, to_apply=%region_23.24.clone | all-reduce | flops 10240 | bytes 40960
  1558.4 11.8 all-reduce.12
  1574.3 23.0 %reduce-scatter.39.cloned.1.call-done = bf16[192,2240]{1,0:T(8,128)(2,1)} async-done(((bf16[1536,2240]{1,0:T(8,128)(2,1)}), bf16[192,2240]{1,0:T(8,128)(2,1)}) %reduce-scatter.39.cloned.1.call-update) | async-done | bytes 860176 | tf_op jit(solution)/shard_map/reduce_scatter | solution.py:212
  1597.3 69.1 %reduce-scatter.37.cloned.1.call-done = bf16[192,2240]{1,0:T(8,128)(2,1)} async-done(((bf16[1536,2240]{1,0:T(8,128)(2,1)}), bf16[192,2240]{1,0:T(8,128)(2,1)}) %reduce-scatter.37.cloned.1.call-update) | async-done | bytes 860176 | tf_op jit(solution)/shard_map/reduce_scatter | solution.py:212
  1669.8 65.6 %reduce-scatter.43.cloned.1.call-done = bf16[192,2240]{1,0:T(8,128)(2,1)} async-done(((bf16[1536,2240]{1,0:T(8,128)(2,1)}), bf16[192,2240]{1,0:T(8,128)(2,1)}) %reduce-scatter.43.cloned.1.call-update) | async-done | bytes 860176 | tf_op jit(solution)/shard_map/reduce_scatter | solution.py:215
  1735.4 68.9 %reduce-scatter.41.cloned.1.call-done = bf16[192,2240]{1,0:T(8,128)(2,1)} async-done(((bf16[1536,2240]{1,0:T(8,128)(2,1)}), bf16[192,2240]{1,0:T(8,128)(2,1)}) %reduce-scatter.41.cloned.1.call-update) | async-done | bytes 860176 | tf_op jit(solution)/shard_map/reduce_scatter | solution.py:215
  1807.8 65.6 %reduce-scatter.47.cloned.1.call-done = bf16[2240,192]{0,1:T(8,128)(2,1)} async-done(((bf16[2240,1536]{0,1:T(8,128)(2,1)}), bf16[2240,192]{0,1:T(8,128)(2,1)}) %reduce-scatter.47.cloned.1.call-update) | async-done | bytes 860176 | tf_op jit(solution)/shard_map/reduce_scatter | solution.py:218
  1873.4 69.1 %reduce-scatter.45.cloned.1.call-done = bf16[2240,192]{0,1:T(8,128)(2,1)} async-done(((bf16[2240,1536]{0,1:T(8,128)(2,1)}), bf16[2240,192]{0,1:T(8,128)(2,1)}) %reduce-scatter.45.cloned.1.call-update) | async-done | bytes 860176 | tf_op jit(solution)/shard_map/reduce_scatter | solution.py:218
  1945.9 107.4 %all-reduce.16.cloned.1.call-done = (bf16[1,192,2048]{2,1,0:T(8,128)(2,1)}, bf16[1,192,2048]{2,1,0:T(8,128)(2,1)}, bf16[1,192,1536]{2,1,0:T(8,128)(2,1)}, bf16[1,192,1536]{2,1,0:T(8,128)(2,1)}) async-done(((bf16[1,192,2048]{2,1,0:T(8,128)(2,1)}, bf16[1,192,2048]{2,1,0:T(8,128)(2,1)}, bf16[1,192,1536]{2,1,0:T(8,128)(2,1)}, bf16[1,192,1536]{2,1,0:T(8,128)(2,1)}), (bf16[1,192,2048]{2,1,0:T(8,128)(2,1)}, ...) | async-done | bytes 2752528 | tf_op jit(solution)/shard_map/psum | solution.py:303
  (422 shorter events, 314.1 us)
Async XLA Ops:
  7.2 32.1 %copy-start.88 = (bf16[2,256]{1,0:T(2,128)(2,1)S(1)}, bf16[2,256]{1,0:T(2,128)(2,1)}, u32[]{:S(2)}) copy-start(bf16[2,256]{1,0:T(2,128)(2,1)} %param.18) | copy-start | bytes 3076
  7.2 39.7 %copy-start.91 = (s32[1,8]{1,0:T(1,128)S(1)}, s32[1,8]{1,0:T(1,128)}, u32[]{:S(2)}) copy-start(s32[1,8]{1,0:T(1,128)} %param.15) | copy-start | bytes 100
  7.2 40.4 %copy-start.6 = (bf16[1,256,1536]{2,1,0:T(8,128)(2,1)S(1)}, bf16[1,256,1536]{2,1,0:T(8,128)(2,1)}, u32[]{:S(2)}) copy-start(bf16[1,256,1536]{2,1,0:T(8,128)(2,1)} %param.12) | copy-start | bytes 2359300
  7.2 51.6 %all-gather.45.cloned.1.call-start = ((), (), s32[]{:S(2)}) async-start(), calls=%async_computation.38 | async-start | bytes 7077888 | tf_op jit(solution)/shard_map/all_gather | solution.py:56
  10.1 84.7 %all-gather.33.cloned.1.call-start = ((), (), s32[]{:S(2)}) async-start(), calls=%async_computation.16 | async-start | bytes 1310720 | tf_op jit(solution)/shard_map/all_gather | solution.py:127
  47.4 29.0 %copy-start.35 = (f32[256,64]{0,1:T(8,128)}, f32[256,64]{0,1:T(8,128)S(1)}, u32[]{:S(2)}) copy-start(f32[256,64]{0,1:T(8,128)S(1)} %get-tuple-element.93) | copy-start | bytes 196612
  47.5 29.0 %copy-start.39 = (f32[256,64]{0,1:T(8,128)}, f32[256,64]{0,1:T(8,128)S(1)}, u32[]{:S(2)}) copy-start(f32[256,64]{0,1:T(8,128)S(1)} %get-tuple-element.94) | copy-start | bytes 196612
  47.6 431.5 %copy-start.28 = (f32[256,64]{1,0:T(8,128)}, f32[256,64]{1,0:T(8,128)S(1)}, u32[]{:S(2)}) copy-start(f32[256,64]{1,0:T(8,128)S(1)} %copy.128) | copy-start | bytes 196612
  66.6 68.8 %all-gather.47.cloned.1.call-start = ((), (), s32[]{:S(2)}) async-start(), calls=%async_computation.39 | async-start | bytes 5308416 | tf_op jit(solution)/shard_map/all_gather | solution.py:58
  67.8 118.7 %all-gather.49.cloned.1.call-start = ((), (), s32[]{:S(2)}) async-start(), calls=%async_computation.40 | async-start | bytes 7962624 | tf_op jit(solution)/shard_map/all_gather | solution.py:60
  70.6 180.8 %all-gather.35.cloned.1.call-start = ((), (), s32[]{:S(2)}) async-start(), calls=%async_computation.17 | async-start | bytes 3932160 | tf_op jit(solution)/shard_map/all_gather | solution.py:144
  71.5 68.3 %copy-start.61 = (f32[1536]{0:T(1024)}, f32[1536]{0:T(1024)S(1)}, u32[]{:S(2)}) copy-start(f32[1536]{0:T(1024)S(1)} %convert_element_type.309) | copy-start | bytes 18436
  139.2 285.8 %copy-start.2 = (f32[256,1536]{1,0:T(8,128)}, f32[256,1536]{1,0:T(8,128)S(1)}, u32[]{:S(2)}) copy-start(f32[256,1536]{1,0:T(8,128)S(1)} %get-tuple-element.104) | copy-start | bytes 4718596
  140.9 159.6 %all-gather.51.cloned.1.call-start = ((), (), s32[]{:S(2)}) async-start(), calls=%async_computation.41 | async-start | bytes 7962624 | tf_op jit(solution)/shard_map/all_gather | solution.py:61
  143.8 207.9 %all-gather.53.cloned.1.call-start = ((), (), s32[]{:S(2)}) async-start(), calls=%async_computation.42 | async-start | bytes 7962624 | tf_op jit(solution)/shard_map/all_gather | solution.py:62
  146.8 278.2 %reduce-scatter.17.cloned.1.call-start = ((), (), s32[]{:S(2)}) async-start(), calls=%async_computation.18 | async-start | bytes 3932160 | tf_op jit(solution)/shard_map/reduce_scatter | solution.py:149
  364.5 108.3 %all-gather.55.cloned.1.call-start = ((), (), s32[]{:S(2)}) async-start(), calls=%async_computation.43 | async-start | bytes 7077888 | tf_op jit(solution)/shard_map/all_gather | solution.py:56
  365.3 143.6 %all-gather.37.cloned.1.call-start = ((), (), s32[]{:S(2)}) async-start(), calls=%async_computation.19 | async-start | bytes 1310720 | tf_op jit(solution)/shard_map/all_gather | solution.py:127
  374.2 103.3 %copy-start.64 = (f32[1536]{0:T(1024)}, f32[1536]{0:T(1024)S(1)}, u32[]{:S(2)}) copy-start(f32[1536]{0:T(1024)S(1)} %convert_element_type.310) | copy-start | bytes 18436
  427.1 45.8 %copy-start.74 = (f32[256]{0:T(256)}, f32[256]{0:T(256)S(1)}, u32[]{:S(2)}) copy-start(f32[256]{0:T(256)S(1)} %fusion.150) | copy-start | bytes 3076
  480.7 68.2 %all-gather.57.cloned.1.call-start = ((), (), s32[]{:S(2)}) async-start(), calls=%async_computation.44 | async-start | bytes 5308416 | tf_op jit(solution)/shard_map/all_gather | solution.py:58
  481.5 133.0 %all-gather.41.cloned.1.call-start = ((), (), s32[]{:S(2)}) async-start(), calls=%async_computation.22 | async-start | bytes 3932160 | tf_op jit(solution)/shard_map/all_gather | solution.py:192
  482.7 181.6 %all-gather.63.cloned.1.call-start = ((), (), s32[]{:S(2)}) async-start(), calls=%async_computation.47 | async-start | bytes 7962624 | tf_op jit(solution)/shard_map/all_gather | solution.py:62
  483.5 231.3 %all-gather.61.cloned.1.call-start = ((), (), s32[]{:S(2)}) async-start(), calls=%async_computation.46 | async-start | bytes 7962624 | tf_op jit(solution)/shard_map/all_gather | solution.py:61
  484.0 296.2 %all-gather.39.cloned.1.call-start = ((), (), s32[]{:S(2)}) async-start(), calls=%async_computation.20 | async-start | bytes 3932160 | tf_op jit(solution)/shard_map/all_gather | solution.py:144
  491.2 30.0 %copy-start.19 = (bf16[256,12,64]{2,0,1:T(8,128)(2,1)}, bf16[256,12,64]{2,0,1:T(8,128)(2,1)S(1)}, u32[]{:S(2)}) copy-start(bf16[256,12,64]{2,0,1:T(8,128)(2,1)S(1)} %copy.137) | copy-start | bytes 1179652
  492.9 28.3 %copy-start.21 = (bf16[256,12,64]{2,0,1:T(8,128)(2,1)}, bf16[256,12,64]{2,0,1:T(8,128)(2,1)S(1)}, u32[]{:S(2)}) copy-start(bf16[256,12,64]{2,0,1:T(8,128)(2,1)S(1)} %copy.138) | copy-start | bytes 1179652
  554.1 275.8 %all-gather.59.cloned.1.call-start = ((), (), s32[]{:S(2)}) async-start(), calls=%async_computation.45 | async-start | bytes 7962624 | tf_op jit(solution)/shard_map/all_gather | solution.py:60
  554.7 377.5 %reduce-scatter.21.cloned.1.call-start = ((), (), s32[]{:S(2)}) async-start(), calls=%async_computation.23 | async-start | bytes 3932160 | tf_op jit(solution)/shard_map/reduce_scatter | solution.py:203
  871.6 123.6 %reduce-scatter.19.cloned.1.call-start = ((), (), s32[]{:S(2)}) async-start(), calls=%async_computation.21 | async-start | bytes 3932160 | tf_op jit(solution)/shard_map/reduce_scatter | solution.py:149
  884.1 167.5 %reduce-scatter.23.cloned.1.call-start = ((), (), s32[]{:S(2)}) async-start(), calls=%async_computation.24 | async-start | bytes 1310720 | tf_op jit(solution)/shard_map/reduce_scatter | solution.py:259
  1024.3 100.6 %all-gather.43.cloned.1.call-start = ((), (), s32[]{:S(2)}) async-start(), calls=%async_computation.25 | async-start | bytes 3932160 | tf_op jit(solution)/shard_map/all_gather | solution.py:192
  1028.7 32.2 %copy-start.23 = (bf16[256,12,128]{0,2,1:T(8,128)(2,1)}, bf16[256,12,128]{0,2,1:T(8,128)(2,1)S(1)}, u32[]{:S(2)}) copy-start(bf16[256,12,128]{0,2,1:T(8,128)(2,1)S(1)} %pad_maximum_fusion.6) | copy-start | bytes 2359300
  1062.8 164.8 %reduce-scatter.25.cloned.1.call-start = ((), (), s32[]{:S(2)}) async-start(), calls=%async_computation.26 | async-start | bytes 3932160 | tf_op jit(solution)/shard_map/reduce_scatter | solution.py:203
  1168.3 59.2 %copy-start.3 = (f32[256,1536]{1,0:T(8,128)S(1)}, f32[256,1536]{1,0:T(8,128)}, u32[]{:S(2)}) copy-start(f32[256,1536]{1,0:T(8,128)} %copy-done.2) | copy-start | bytes 4718596
  1168.4 117.0 %reduce-scatter.27.cloned.1.call-start = ((), (), s32[]{:S(2)}) async-start(), calls=%async_computation.27 | async-start | bytes 1310720 | tf_op jit(solution)/shard_map/reduce_scatter | solution.py:259
  1258.0 120.5 %reduce-scatter.35.cloned.1.call-start = ((), (), s32[]{:S(2)}) async-start(), calls=%async_computation.31 | async-start | bytes 5308416 | tf_op jit(solution)/shard_map/reduce_scatter | solution.py:294
  1263.5 142.7 %reduce-scatter.31.cloned.1.call-start = ((), (), s32[]{:S(2)}) async-start(), calls=%async_computation.29 | async-start | bytes 7077888 | tf_op jit(solution)/shard_map/reduce_scatter | solution.py:288
  1269.2 194.2 %reduce-scatter.33.cloned.1.call-start = ((), (), s32[]{:S(2)}) async-start(), calls=%async_computation.30 | async-start | bytes 5308416 | tf_op jit(solution)/shard_map/reduce_scatter | solution.py:294
  1274.4 254.0 %reduce-scatter.29.cloned.1.call-start = ((), (), s32[]{:S(2)}) async-start(), calls=%async_computation.28 | async-start | bytes 7077888 | tf_op jit(solution)/shard_map/reduce_scatter | solution.py:288
  1298.7 298.6 %reduce-scatter.39.cloned.1.call-start = ((), (), s32[]{:S(2)}) async-start(), calls=%async_computation.33 | async-start | bytes 7962624 | tf_op jit(solution)/shard_map/reduce_scatter | solution.py:212
  1311.6 354.8 %reduce-scatter.37.cloned.1.call-start = ((), (), s32[]{:S(2)}) async-start(), calls=%async_computation.32 | async-start | bytes 7962624 | tf_op jit(solution)/shard_map/reduce_scatter | solution.py:212
  1324.1 411.4 %reduce-scatter.43.cloned.1.call-start = ((), (), s32[]{:S(2)}) async-start(), calls=%async_computation.35 | async-start | bytes 7962624 | tf_op jit(solution)/shard_map/reduce_scatter | solution.py:215
  1337.0 467.3 %reduce-scatter.41.cloned.1.call-start = ((), (), s32[]{:S(2)}) async-start(), calls=%async_computation.34 | async-start | bytes 7962624 | tf_op jit(solution)/shard_map/reduce_scatter | solution.py:215
  1349.5 523.9 %reduce-scatter.47.cloned.1.call-start = ((), (), s32[]{:S(2)}) async-start(), calls=%async_computation.37 | async-start | bytes 7962624 | tf_op jit(solution)/shard_map/reduce_scatter | solution.py:218
  1362.3 580.2 %reduce-scatter.45.cloned.1.call-start = ((), (), s32[]{:S(2)}) async-start(), calls=%async_computation.36 | async-start | bytes 7962624 | tf_op jit(solution)/shard_map/reduce_scatter | solution.py:218
  1375.0 678.4 %all-reduce.16.cloned.1.call-start = ((), (), s32[]{:S(2)}) async-start(), calls=%async_computation.48 | async-start | bytes 5505024 | tf_op jit(solution)/shard_map/psum | solution.py:303
  1528.5 42.9 %copy-start.78 = (f32[256]{0:T(256)S(1)}, f32[256]{0:T(256)}, u32[]{:S(2)}) copy-start(f32[256]{0:T(256)} %copy-done.77) | copy-start | bytes 3076
  (80 other events, 607.3 us)
Sparse Core Ops, SparseCore 0:
  10.5 48.2 all-gather.44
  66.7 27.9 all-gather.32
  97.2 38.1 all-gather.46
  137.7 48.7 all-gather.48
  187.9 63.4 all-gather.34
  253.1 47.3 all-gather.50
  303.0 48.7 all-gather.52
  364.6 60.3 reduce-scatter.16
  427.5 45.2 all-gather.54
  480.8 27.9 all-gather.36
  510.7 38.1 all-gather.56
  550.9 63.4 all-gather.40
  616.9 47.3 all-gather.62
  666.0 48.7 all-gather.60
  716.8 63.4 all-gather.38
  782.5 47.3 all-gather.58
  871.7 60.3 reduce-scatter.20
  934.9 60.3 reduce-scatter.18
  1024.4 27.1 reduce-scatter.22
  1062.9 61.9 all-gather.42
  1168.5 59.0 reduce-scatter.24
  1258.1 27.1 reduce-scatter.26
  1288.8 52.2 reduce-scatter.34
  1344.3 61.7 reduce-scatter.30
  1409.6 53.7 reduce-scatter.32
  1466.6 61.7 reduce-scatter.28
  1531.8 65.4 reduce-scatter.38
  1600.8 65.4 reduce-scatter.36
  1669.9 65.4 reduce-scatter.42
  1738.8 65.4 reduce-scatter.40
  1807.9 65.4 reduce-scatter.46
  1876.9 65.4 reduce-scatter.44
  1945.0 108.3 all-reduce.15
where the time goes:
time: 2070 us
  waiting for transfers between devices  1480 us (71%)
  matrix products  356 us (17%)
  blocking collectives  78 us (4%)
  local copies, waits for them, and re-layouts  68.9 us (3%)
  other arithmetic  59.3 us (3%)
    reduce_scatter x2, waiting for transfers between devices, backward_layer(): lax.psum_scatter(down_grad.astype(jnp.bfloat16), 'fsdp', scatter_dimensio...  135 us
    reduce_scatter x2, waiting for transfers between devices, backward_layer(): lax.psum_scatter(up_w_grad.astype(jnp.bfloat16), 'fsdp', scatter_dimensio...  135 us
    all_gather x2, waiting for transfers between devices, forward_layer(): block_rows = lax.all_gather(normed_two, 'context', axis=0, tiled=True)  130 us
    all_gather x2, waiting for transfers between devices, backward_layer(): grad_all = lax.all_gather(grad_low, 'context', axis=0, tiled=True)  122 us
    reduce_scatter x2, waiting for transfers between devices, forward_layer(): lax.psum_scatter(jnp.dot(hidden, down_w, preferred_element_type=jnp.float...  112 us
    psum x1, waiting for transfers between devices, backward_layer(): lax.psum(attn_grads[1].astype(jnp.bfloat16), 'context').astype(jnp.float32)  107 us
    reduce_scatter x2, waiting for transfers between devices, backward_layer(): lax.psum_scatter((first_term + jnp.einsum('tf,df->td', up_grad, up_w, pre...  106 us
    reduce_scatter x2, waiting for transfers between devices, backward_layer(): lax.psum_scatter(qkv_w_grad.astype(jnp.bfloat16), 'fsdp', scatter_dimensi...  92.7 us
  transfers between devices with their start and end apart: 33, of which 32 were waited for; matrix products, arithmetic and copies ran while one was open for 14% of the time, Pallas kernels for 0%

commit v1 on v0

v1 whole, which is shorter than its diff:
```python
import functools
import math

import jax
import jax.numpy as jnp
from jax import lax
from jax.experimental import pallas as pl
from jax.experimental.pallas import tpu as pltpu
from jax.sharding import PartitionSpec as P

QUERY_HEADS = 12
KV_HEADS = 2
HEAD = 128
LAYERS = 2
TILE = 128
Q_WIDTH = QUERY_HEADS * HEAD
KV_WIDTH = KV_HEADS * HEAD
PER_GROUP = QUERY_HEADS // KV_HEADS
SCALE = 1.0 / math.sqrt(HEAD)
EPSILON = 1e-06
ROPE_BASE = 1000000.0
BF = jnp.bfloat16
F32 = jnp.float32
MESH = pl.DeviceIdType.MESH
VMEM_LIMIT = 66 * 1024 * 1024
ANY = pl.BlockSpec(memory_space=pl.ANY)
VM = pl.BlockSpec(memory_space=pltpu.VMEM)


def dot_nn(a, b):
    return lax.dot_general(a, b, (((1,), (0,)), ((), ())), preferred_element_type=F32)


def dot_nt(a, b):
    return lax.dot_general(a, b, (((1,), (1,)), ((), ())), preferred_element_type=F32)


def dot_tn(a, b):
    return lax.dot_general(a, b, (((0,), (0,)), ((), ())), preferred_element_type=F32)


def lane_tile(width, most):
    best = 128
    for k in range(1, most // 128 + 1):
        if width % (128 * k) == 0:
            best = 128 * k
    return best


class Line:
    def __init__(self, n):
        self.n = n
        self.z = lax.axis_index("context")
        self.right = lax.rem(self.z + 1, n)
        self.left = lax.rem(self.z + n - 1, n)
        self.has_right = self.z < n - 1
        self.has_left = self.z > 0

    def barrier(self):
        bar = pltpu.get_barrier_semaphore()

        @pl.when(self.has_right)
        def _():
            pl.semaphore_signal(bar, inc=1, device_id={"context": self.right}, device_id_type=MESH)

        @pl.when(self.has_left)
        def _():
            pl.semaphore_signal(bar, inc=1, device_id={"context": self.left}, device_id_type=MESH)

        both = self.has_right & self.has_left

        @pl.when(both)
        def _():
            pl.semaphore_wait(bar, 2)

        @pl.when(jnp.logical_not(both))
        def _():
            pl.semaphore_wait(bar, 1)

    def order(self, i):
        z, n = self.z, self.n
        short = jnp.minimum(z, n - 1 - z)
        j = i - 1
        paired = j < 2 * short
        k = jnp.where(paired, j // 2 + 1, j - short + 1)
        goes_left = jnp.where(paired, lax.rem(j, 2) == 0, z > n - 1 - z)
        return jnp.where(i == 0, z, jnp.where(goes_left, z - k, z + k))


def remote(src, dst, send, recv, target):
    return pltpu.make_async_remote_copy(
        src_ref=src, dst_ref=dst, send_sem=send, recv_sem=recv,
        device_id={"context": target}, device_id_type=MESH,
    )


class Gather:
    def __init__(self, line, slots, send_r, send_l, recv):
        self.line, self.slots = line, slots
        self.send_r, self.send_l, self.recv = send_r, send_l, recv

    def _right(self, b, src):
        return remote(src, self.slots.at[b], self.send_r.at[b], self.recv.at[b], self.line.right)

    def _left(self, b, src):
        return remote(src, self.slots.at[b], self.send_l.at[b], self.recv.at[b], self.line.left)

    def start(self, own):
        line = self.line

        @pl.when(line.has_right)
        def _():
            self._right(line.z, own).start()

        @pl.when(line.has_left)
        def _():
            self._left(line.z, own).start()

    def arrive(self, b):
        line = self.line
        self._right(b, self.slots.at[b]).wait_recv()

        @pl.when((b < line.z) & line.has_right)
        def _():
            self._right(b, self.slots.at[b]).start()

        @pl.when((b > line.z) & line.has_left)
        def _():
            self._left(b, self.slots.at[b]).start()

    def finish(self):
        line = self.line
        for b in range(line.n):
            @pl.when((b <= line.z) & line.has_right)
            def _():
                self._right(b, self.slots.at[b]).wait_send()

            @pl.when((b >= line.z) & line.has_left)
            def _():
                self._left(b, self.slots.at[b]).wait_send()


class Scatter:
    def __init__(self, line, pieces, part, from_left, from_right, send_r, send_l, recv_l, recv_r):
        self.line, self.pieces, self.part = line, pieces, part
        self.from_left, self.from_right = from_left, from_right
        self.send_r, self.send_l, self.recv_l, self.recv_r = send_r, send_l, recv_l, recv_r

    def _right(self, b, p):
        return remote(self.part.at[b, p], self.from_left.at[b, p], self.send_r.at[b, p],
                      self.recv_l.at[b, p], self.line.right)

    def _left(self, b, p):
        return remote(self.part.at[b, p], self.from_right.at[b, p], self.send_l.at[b, p],
                      self.recv_r.at[b, p], self.line.left)

    def computed(self, b, p):
        line = self.line

        @pl.when((line.z == 0) & (b > 0))
        def _():
            self._right(b, p).start()

        @pl.when((line.z == line.n - 1) & (b < line.n - 1))
        def _():
            self._left(b, p).start()

    def steps(self):
        return range(1, 2 * (self.line.n - 1) + 1)

    def step(self, t, add_own):
        line = self.line
        n, z = line.n, line.z
        b_left = t - z

        @pl.when(line.has_left & (b_left >= z) & (b_left < n))
        def _():
            for p in range(self.pieces):
                self._right(b_left, p).wait_recv()

                @pl.when(b_left == z)
                def _():
                    add_own(p, self.from_left[b_left, p].astype(F32))

                @pl.when(b_left != z)
                def _():
                    self.part[b_left, p] = (
                        self.part[b_left, p].astype(F32) + self.from_left[b_left, p].astype(F32)
                    ).astype(BF)
                    self._right(b_left, p).start()

        b_right = 2 * (n - 1) - t - z

        @pl.when(line.has_right & (b_right >= 0) & (b_right <= z))
        def _():
            for p in range(self.pieces):
                self._left(b_right, p).wait_recv()

                @pl.when(b_right == z)
                def _():
                    add_own(p, self.from_right[b_right, p].astype(F32))

                @pl.when(b_right != z)
                def _():
                    self.part[b_right, p] = (
                        self.part[b_right, p].astype(F32) + self.from_right[b_right, p].astype(F32)
                    ).astype(BF)
                    self._left(b_right, p).start()

    def finish(self):
        line = self.line
        for b in range(line.n):
            @pl.when((b > line.z) & line.has_right)
            def _():
                for p in range(self.pieces):
                    self._right(b, p).wait_send()

            @pl.when((b < line.z) & line.has_left)
            def _():
                for p in range(self.pieces):
                    self._left(b, p).wait_send()


def gather_sems(n):
    return [pltpu.SemaphoreType.DMA((n,))] * 3


def scatter_sems(n, pieces):
    return [pltpu.SemaphoreType.DMA((n, pieces))] * 4


def params(cid):
    return pltpu.CompilerParams(
        collective_id=cid, has_side_effects=True, vmem_limit_bytes=VMEM_LIMIT
    )


def ffn_forward_kernel(n, pieces, x_ref, w_ref, xall_ref, gate_ref, up_ref, y_ref,
                       w_v, xbuf, gbuf, ubuf, hbuf, part, from_l, from_r,
                       w_sem, x_sem, out_sem, *sems):
    line = Line(n)
    z = line.z
    owners, _, rows, width = w_ref.shape
    d_model = x_ref.shape[1]
    tile = lane_tile(width, 256)
    piece = d_model // pieces
    gather = Gather(line, xbuf, *sems[:3])
    scatter = Scatter(line, pieces, part, from_l, from_r, *sems[3:])

    def w_copy(k, f):
        return pltpu.make_async_copy(
            w_ref.at[f, k], w_v.at[k, pl.ds(f * rows, rows)], w_sem.at[k, f]
        )

    def out_copies(b):
        slot = lax.rem(b, 2)
        return (
            pltpu.make_async_copy(gbuf.at[slot], gate_ref.at[b], out_sem.at[0, slot]),
            pltpu.make_async_copy(ubuf.at[slot], up_ref.at[b], out_sem.at[1, slot]),
        )

    def x_out(b):
        return pltpu.make_async_copy(xbuf.at[b], xall_ref.at[b], x_sem.at[b])

    line.barrier()
    gather.start(x_ref)
    for k in range(3):
        for f in range(owners):
            w_copy(k, f).start()
    xbuf[z] = x_ref[...]
    for k in range(3):
        for f in range(owners):
            w_copy(k, f).wait()

    @pl.loop(0, n)
    def _(i):
        b = line.order(i)

        @pl.when(i > 0)
        def _():
            gather.arrive(b)

        x_out(b).start()
        slot = lax.rem(i, 2)
        g_copy = pltpu.make_async_copy(gbuf.at[slot], gate_ref.at[b], out_sem.at[0, slot])
        u_copy = pltpu.make_async_copy(ubuf.at[slot], up_ref.at[b], out_sem.at[1, slot])

        @pl.when(i > 1)
        def _():
            g_copy.wait()
            u_copy.wait()

        @pl.loop(0, width // tile)
        def _(j):
            cols = pl.ds(pl.multiple_of(j * tile, tile), tile)
            xb = xbuf[b]
            gate = dot_nn(xb, w_v[0, :, cols])
            up = dot_nn(xb, w_v[1, :, cols])
            gbuf[slot, :, cols] = gate.astype(BF)
            ubuf[slot, :, cols] = up.astype(BF)
            hbuf[:, cols] = (gate * jax.nn.sigmoid(gate) * up).astype(BF)

        g_copy.start()
        u_copy.start()
        for p in range(pieces):
            out = dot_nt(hbuf[...], w_v[2, pl.ds(p * piece, piece)])

            @pl.when(b == z)
            def _():
                y_ref[:, p * piece:(p + 1) * piece] = out

            @pl.when(b != z)
            def _():
                part[b, p] = out.astype(BF)

            scatter.computed(b, p)

    def add_own(p, value):
        cols = slice(p * piece, (p + 1) * piece)
        y_ref[:, cols] = y_ref[:, cols] + value

    for t in scatter.steps():
        scatter.step(t, add_own)
    for i in range(max(0, n - 2), n):
        slot = i % 2
        pltpu.make_async_copy(gbuf.at[slot], gate_ref.at[0], out_sem.at[0, slot]).wait()
        pltpu.make_async_copy(ubuf.at[slot], up_ref.at[0], out_sem.at[1, slot]).wait()
    for b in range(n):
        x_out(b).wait()
    gather.finish()
    scatter.finish()


def ffn_forward(x, w, n):
    rows, d_model = x.shape
    owners, _, shard, width = w.shape
    pieces = 3
    piece = d_model // pieces
    return pl.pallas_call(
        functools.partial(ffn_forward_kernel, n, pieces),
        out_shape=(
            jax.ShapeDtypeStruct((n, rows, d_model), BF),
            jax.ShapeDtypeStruct((n, rows, width), BF),
            jax.ShapeDtypeStruct((n, rows, width), BF),
            jax.ShapeDtypeStruct((rows, d_model), F32),
        ),
        in_specs=[VM, ANY],
        out_specs=[ANY, ANY, ANY, VM],
        scratch_shapes=[
            pltpu.VMEM((3, d_model, width), BF),
            pltpu.VMEM((n, rows, d_model), BF),
            pltpu.VMEM((2, rows, width), BF),
            pltpu.VMEM((2, rows, width), BF),
            pltpu.VMEM((rows, width), BF),
            pltpu.VMEM((n, pieces, rows, piece), BF),
            pltpu.VMEM((n, pieces, rows, piece), BF),
            pltpu.VMEM((n, pieces, rows, piece), BF),
            pltpu.SemaphoreType.DMA((3, owners)),
            pltpu.SemaphoreType.DMA((n,)),
            pltpu.SemaphoreType.DMA((2, 2)),
        ] + gather_sems(n) + scatter_sems(n, pieces),
        compiler_params=params(1),
        cost_estimate=pl.CostEstimate(
            flops=6 * n * rows * d_model * width, transcendentals=n * rows * width,
            bytes_accessed=60 << 20),
        name="ffn_forward",
    )(x, w)


def ffn_backward_kernel(n, pieces, groups, g_ref, w_ref, xall_ref, gate_ref, up_ref, dw_ref, dx_ref,
                        w_v, gbuf, xv, gate_v, up_v, hid_v, part, from_l, from_r, stage,
                        w_sem, in_sem, out_sem, *sems):
    line = Line(n)
    z = line.z
    owners, _, shard, width = w_ref.shape
    rows, d_model = g_ref.shape
    tile = lane_tile(width, 256)
    piece = d_model // pieces
    gather = Gather(line, gbuf, *sems[:3])
    scatter = Scatter(line, pieces, part, from_l, from_r, *sems[3:])

    def w_copy(k, f):
        return pltpu.make_async_copy(
            w_ref.at[f, k], w_v.at[k, pl.ds(f * shard, shard)], w_sem.at[k, f]
        )

    def loads(b):
        return (
            pltpu.make_async_copy(gate_ref.at[b], gate_v.at[b], in_sem.at[0, b]),
            pltpu.make_async_copy(up_ref.at[b], up_v.at[b], in_sem.at[1, b]),
        )

    def x_load(b):
        return pltpu.make_async_copy(xall_ref.at[b], xv.at[b], in_sem.at[2, b])

    line.barrier()
    gather.start(g_ref)
    for f in range(owners):
        w_copy(2, f).start()
    for c in loads(z):
        c.start()
    for k in range(2):
        for f in range(owners):
            w_copy(k, f).start()
    for b in range(n):
        @pl.when(b != z)
        def _():
            for c in loads(b):
                c.start()
    for b in range(n):
        x_load(b).start()
    gbuf[z] = g_ref[...]
    for k in (2, 0, 1):
        for f in range(owners):
            w_copy(k, f).wait()

    @pl.loop(0, n)
    def _(i):
        b = line.order(i)

        @pl.when(i > 0)
        def _():
            gather.arrive(b)

        for c in loads(b):
            c.wait()

        @pl.loop(0, width // tile)
        def _(j):
            cols = pl.ds(pl.multiple_of(j * tile, tile), tile)
            d_hidden = dot_nn(gbuf[b], w_v[2, :, cols])
            gate = gate_v[b, :, cols].astype(F32)
            up = up_v[b, :, cols].astype(F32)
            sig = jax.nn.sigmoid(gate)
            act = gate * sig
            hid_v[b, :, cols] = (act * up).astype(BF)
            gate_v[b, :, cols] = (d_hidden * up * (sig + act * (1.0 - sig))).astype(BF)
            up_v[b, :, cols] = (d_hidden * act).astype(BF)

        for p in range(pieces):
            sl = pl.ds(p * piece, piece)
            out = dot_nt(gate_v[b], w_v[0, sl]) + dot_nt(up_v[b], w_v[1, sl])

            @pl.when(b == z)
            def _():
                dx_ref[:, p * piece:(p + 1) * piece] = out

            @pl.when(b != z)
            def _():
                part[b, p] = out.astype(BF)

            scatter.computed(b, p)

    def add_own(p, value):
        cols = slice(p * piece, (p + 1) * piece)
        dx_ref[:, cols] = dx_ref[:, cols] + value

    for b in range(n):
        x_load(b).wait()

    group = d_model // groups
    per = group // shard

    def dw_copies(k, q, slot):
        return [
            pltpu.make_async_copy(
                stage.at[slot, pl.ds(s * shard, shard)], dw_ref.at[q * per + s, k],
                out_sem.at[slot, s])
            for s in range(per)
        ]

    def weight_unit(unit):
        k, q = unit // groups, unit % groups
        slot = unit % 2
        left = (xv, xv, gbuf)[k]
        right = (gate_v, up_v, hid_v)[k]
        if unit >= 2:
            for c in dw_copies((unit - 2) // groups, (unit - 2) % groups, slot):
                c.wait()
        lt = left[:, :, q * group:(q + 1) * group].reshape(n * rows, group)

        @pl.loop(0, width // tile)
        def _(j):
            cols = pl.ds(pl.multiple_of(j * tile, tile), tile)
            stage[slot, :, cols] = dot_tn(
                lt, right[:, :, cols].reshape(n * rows, tile)
            ).astype(BF)

        for c in dw_copies(k, q, slot):
            c.start()

    units = 3 * groups
    steps = list(scatter.steps())
    done = 0
    for index, t in enumerate(steps):
        scatter.step(t, add_own)
        until = units * (index + 1) // len(steps)
        while done < until:
            weight_unit(done)
            done += 1
    for unit in range(units - 2, units):
        for c in dw_copies(unit // groups, unit % groups, unit % 2):
            c.wait()
    gather.finish()
    scatter.finish()


def ffn_backward(g, w, xall, gate, up, n):
    rows, d_model = g.shape
    owners, _, shard, width = w.shape
    pieces, groups = 3, 4
    piece = d_model // pieces
    per = d_model // groups // shard
    return pl.pallas_call(
        functools.partial(ffn_backward_kernel, n, pieces, groups),
        out_shape=(
            jax.ShapeDtypeStruct((owners, 3, shard, width), BF),
            jax.ShapeDtypeStruct((rows, d_model), F32),
        ),
        in_specs=[VM, ANY, ANY, ANY, ANY],
        out_specs=[ANY, VM],
        scratch_shapes=[
            pltpu.VMEM((3, d_model, width), BF),
            pltpu.VMEM((n, rows, d_model), BF),
            pltpu.VMEM((n, rows, d_model), BF),
            pltpu.VMEM((n, rows, width), BF),
            pltpu.VMEM((n, rows, width), BF),
            pltpu.VMEM((n, rows, width), BF),
            pltpu.VMEM((n, pieces, rows, piece), BF),
            pltpu.VMEM((n, pieces, rows, piece), BF),
            pltpu.VMEM((n, pieces, rows, piece), BF),
            pltpu.VMEM((2, d_model // groups, width), BF),
            pltpu.SemaphoreType.DMA((3, owners)),
            pltpu.SemaphoreType.DMA((3, n)),
            pltpu.SemaphoreType.DMA((2, per)),
        ] + gather_sems(n) + scatter_sems(n, pieces),
        compiler_params=params(2),
        cost_estimate=pl.CostEstimate(
            flops=12 * n * rows * d_model * width, transcendentals=n * rows * width,
            bytes_accessed=100 << 20),
        name="ffn_backward",
    )(g, w, xall, gate, up)


def attention_forward_kernel(n, q_ref, kv_ref, pq_ref, pk_ref, mixed_ref, lse_ref, kvall_ref,
                             kvbuf, vt, *sems):
    line = Line(n)
    z = line.z
    rows = q_ref.shape[0]
    total = n * rows
    gather = Gather(line, kvbuf, *sems)
    line.barrier()
    gather.start(kv_ref)
    kvbuf[z] = kv_ref[...]
    for i in range(1, n):
        gather.arrive(line.order(i))
    kvall_ref[...] = kvbuf[...]
    allowed = pk_ref[...] <= pq_ref[...]
    for g in range(KV_HEADS):
        v = kvbuf[:, :, KV_WIDTH + g * HEAD:KV_WIDTH + (g + 1) * HEAD].reshape(total, HEAD)
        vt[g] = v.T
    for g in range(KV_HEADS):
        for r in range(PER_GROUP):
            h = g * PER_GROUP + r
            k = kvbuf[:, :, g * HEAD:(g + 1) * HEAD].reshape(total, HEAD)
            s = dot_nt(k, q_ref[:, h * HEAD:(h + 1) * HEAD]) * SCALE
            s = jnp.where(allowed, s, -1e30)
            top = jnp.max(s, axis=0, keepdims=True)
            e = jnp.exp(s - top)
            den = jnp.sum(e, axis=0, keepdims=True)
            o = dot_nn(vt[g], e.astype(BF)) / den
            mixed_ref[:, h * HEAD:(h + 1) * HEAD] = o.T.astype(BF)
            lse_ref[h:h + 1, :] = top + jnp.log(den)
    gather.finish()


def attention_forward(q, kv, pos_q, pos_k, n):
    rows = q.shape[0]
    return pl.pallas_call(
        functools.partial(attention_forward_kernel, n),
        out_shape=(
            jax.ShapeDtypeStruct((rows, Q_WIDTH), BF),
            jax.ShapeDtypeStruct((16, rows), F32),
            jax.ShapeDtypeStruct((n, rows, 2 * KV_WIDTH), BF),
        ),
        in_specs=[VM] * 4,
        out_specs=[VM] * 3,
        scratch_shapes=[
            pltpu.VMEM((n, rows, 2 * KV_WIDTH), BF),
            pltpu.VMEM((KV_HEADS, HEAD, n * rows), BF),
        ] + gather_sems(n),
        compiler_params=params(3),
        cost_estimate=pl.CostEstimate(
            flops=4 * n * rows * rows * Q_WIDTH, transcendentals=n * rows * rows * QUERY_HEADS,
            bytes_accessed=16 << 20),
        name="attention_forward",
    )(q, kv, pos_q, pos_k)


def attention_backward_kernel(n, q_ref, kvall_ref, lse_ref, dm_ref, pq_ref, pk_ref,
                              dq_ref, dkv_ref, kt, dk_acc, dv_acc, part, from_l, from_r, *sems):
    line = Line(n)
    z = line.z
    rows = q_ref.shape[0]
    total = n * rows
    pieces = KV_HEADS
    scatter = Scatter(line, pieces, part, from_l, from_r, *sems)
    line.barrier()
    allowed = pk_ref[...] <= pq_ref[...]
    for g in range(KV_HEADS):
        k = kvall_ref[:, :, g * HEAD:(g + 1) * HEAD].reshape(total, HEAD)
        kt[g] = k.T
    for g in range(KV_HEADS):
        for r in range(PER_GROUP):
            h = g * PER_GROUP + r
            cols = slice(h * HEAD, (h + 1) * HEAD)
            k = kvall_ref[:, :, g * HEAD:(g + 1) * HEAD].reshape(total, HEAD)
            v = kvall_ref[:, :, KV_WIDTH + g * HEAD:KV_WIDTH + (g + 1) * HEAD].reshape(total, HEAD)
            q = q_ref[:, cols]
            dm = dm_ref[:, cols]
            s = dot_nt(k, q) * SCALE
            pr = jnp.where(allowed, jnp.exp(s - lse_ref[h:h + 1, :]), 0.0)
            dp = dot_nt(v, dm)
            delta = jnp.sum(pr * dp, axis=0, keepdims=True)
            ds = (pr * (dp - delta) * SCALE).astype(BF)
            dv = dot_nn(pr.astype(BF), dm)
            dk = dot_nn(ds, q)
            if r == 0:
                dk_acc[...] = dk
                dv_acc[...] = dv
            else:
                dk_acc[...] += dk
                dv_acc[...] += dv
            dq_ref[:, cols] = dot_nn(kt[g], ds).T
        for b in range(n):
            sl = slice(b * rows, (b + 1) * rows)

            @pl.when(b == z)
            def _():
                dkv_ref[:, g * HEAD:(g + 1) * HEAD] = dk_acc[sl]
                dkv_ref[:, KV_WIDTH + g * HEAD:KV_WIDTH + (g + 1) * HEAD] = dv_acc[sl]

            @pl.when(b != z)
            def _():
                part[b, g, :, 0:HEAD] = dk_acc[sl].astype(BF)
                part[b, g, :, HEAD:2 * HEAD] = dv_acc[sl].astype(BF)

            scatter.computed(b, g)

    def add_own(p, value):
        a = slice(p * HEAD, (p + 1) * HEAD)
        c = slice(KV_WIDTH + p * HEAD, KV_WIDTH + (p + 1) * HEAD)
        dkv_ref[:, a] = dkv_ref[:, a] + value[:, :HEAD]
        dkv_ref[:, c] = dkv_ref[:, c] + value[:, HEAD:]

    for t in scatter.steps():
        scatter.step(t, add_own)
    scatter.finish()


def attention_backward(q, kvall, lse, dm, pos_q, pos_k, n):
    rows = q.shape[0]
    return pl.pallas_call(
        functools.partial(attention_backward_kernel, n),
        out_shape=(
            jax.ShapeDtypeStruct((rows, Q_WIDTH), F32),
            jax.ShapeDtypeStruct((rows, 2 * KV_WIDTH), F32),
        ),
        in_specs=[VM] * 6,
        out_specs=[VM] * 2,
        scratch_shapes=[
            pltpu.VMEM((KV_HEADS, HEAD, n * rows), BF),
            pltpu.VMEM((n * rows, HEAD), F32),
            pltpu.VMEM((n * rows, HEAD), F32),
        ] + [pltpu.VMEM((n, KV_HEADS, rows, 2 * HEAD), BF)] * 3 + scatter_sems(n, KV_HEADS),
        compiler_params=params(4),
        cost_estimate=pl.CostEstimate(
            flops=10 * n * rows * rows * Q_WIDTH, transcendentals=n * rows * rows * QUERY_HEADS,
            bytes_accessed=16 << 20),
        name="attention_backward",
    )(q, kvall, lse, dm, pos_q, pos_k)


def normalize(stream, gain):
    return stream * lax.rsqrt(jnp.mean(stream * stream, axis=-1, keepdims=True) + EPSILON) * gain


def normalize_back(grad, stream, gain):
    r = lax.rsqrt(jnp.mean(stream * stream, axis=-1, keepdims=True) + EPSILON)
    u = grad * gain
    back = r * (u - stream * (r * r) * jnp.mean(u * stream, axis=-1, keepdims=True))
    return back, jnp.sum(grad * stream * r, axis=0)


def rotate(heads, cosine, sine):
    half = HEAD // 2
    a, b = heads[..., :half], heads[..., half:]
    return jnp.concatenate([a * cosine - b * sine, b * cosine + a * sine], axis=-1)


def frequencies():
    return jnp.power(ROPE_BASE, -(jnp.arange(HEAD // 2, dtype=F32) * 2.0 / HEAD))


def shards(hidden_in, cotangent, seq_lengths, tile_place, norm_attn, w_qkv, b_qkv, w_out,
           norm_mlp, w_gate, w_up, w_down):
    n = lax.axis_size("context")
    owners = lax.axis_size("fsdp")
    rows, d_model = hidden_in.shape[1:]
    hidden_units = w_gate.shape[2]
    width = -(-hidden_units // 128) * 128
    pad = width - hidden_units
    total = n * rows

    row_index = jnp.arange(total, dtype=jnp.int32)
    tile_order = tile_place[0]
    selector = (
        row_index[:, None] // TILE == jnp.arange(tile_order.shape[0], dtype=jnp.int32)[None, :]
    ).astype(jnp.int32)
    position = jnp.sum(selector * tile_order[None, :], axis=1) * TILE + row_index % TILE
    valid = position < seq_lengths[0]
    offset = lax.axis_index("context") * rows
    my_position = lax.dynamic_slice_in_dim(position, offset, rows)
    my_valid = lax.dynamic_slice_in_dim(valid, offset, rows)
    pos_q = my_position[None, :]
    pos_k = jnp.where(valid, position, 1 << 30)[:, None]
    angles = my_position.astype(F32)[:, None] * frequencies()
    cosine, sine = jnp.cos(angles)[:, None, :], jnp.sin(angles)[:, None, :]

    small = jnp.concatenate(
        [norm_attn.reshape(-1), norm_mlp.reshape(-1), b_qkv.reshape(-1)])[None, None]
    small = lax.all_gather(small, "fsdp", axis=0, tiled=True)
    small = small[:, 0].astype(F32)
    shard = norm_attn.shape[1]
    bias_shard = b_qkv.shape[1]
    gains_attn, gains_mlp, biases = [], [], []
    for l in range(LAYERS):
        gains_attn.append(small[:, l * shard:(l + 1) * shard].reshape(-1))
        gains_mlp.append(small[:, (LAYERS + l) * shard:(LAYERS + l + 1) * shard].reshape(-1))
        start = 2 * LAYERS * shard + l * bias_shard
        biases.append(small[:, start:start + bias_shard].reshape(-1))

    def ffn_shard(l):
        return jnp.stack([
            jnp.pad(m, ((0, 0), (0, pad))) for m in (w_gate[l], w_up[l], w_down[l].T)])

    stream = hidden_in[0].astype(F32)
    kept = []
    for l in range(LAYERS):
        qkv_w = lax.all_gather(w_qkv[l], "fsdp", axis=0, tiled=True)
        out_w = lax.all_gather(w_out[l], "fsdp", axis=0, tiled=True)
        ffn_w = lax.all_gather(ffn_shard(l), "fsdp", axis=0, tiled=False)
        normed = normalize(stream, gains_attn[l]).astype(BF)
        projected = jnp.dot(normed, qkv_w, preferred_element_type=F32) + biases[l]
        qk = rotate(
            projected[:, :Q_WIDTH + KV_WIDTH].reshape(rows, QUERY_HEADS + KV_HEADS, HEAD),
            cosine, sine).astype(BF).reshape(rows, Q_WIDTH + KV_WIDTH)
        q = qk[:, :Q_WIDTH]
        kv = jnp.concatenate([qk[:, Q_WIDTH:], projected[:, Q_WIDTH + KV_WIDTH:].astype(BF)], axis=1)
        mixed, lse, kvall = attention_forward(q, kv, pos_q, pos_k, n)
        middle = stream + jnp.dot(mixed, out_w, preferred_element_type=F32)
        normed_two = normalize(middle, gains_mlp[l]).astype(BF)
        xall, gate, up, y = ffn_forward(normed_two, ffn_w, n)
        kept.append((stream, normed, q, kvall, lse, mixed, middle, xall, gate, up,
                     qkv_w, out_w, ffn_w))
        stream = middle + y
    layer_out = stream.astype(BF)[None]

    gradient = cotangent[0].astype(F32) * my_valid[:, None].astype(F32)
    small_grads = [None] * LAYERS
    big_grads = [None] * LAYERS
    for l in reversed(range(LAYERS)):
        (stream, normed, q, kvall, lse, mixed, middle, xall, gate, up,
         qkv_w, out_w, ffn_w) = kept[l]
        dw, dx = ffn_backward(gradient.astype(BF), ffn_w, xall, gate, up, n)
        dw = lax.psum_scatter(dw, "fsdp", scatter_dimension=0, tiled=False)
        back, gain_two = normalize_back(dx, middle, gains_mlp[l])
        d_middle = gradient + back
        d_low = d_middle.astype(BF)
        d_mixed = jnp.einsum("td,cd->tc", d_low, out_w, preferred_element_type=F32).astype(BF)
        out_grad = jnp.einsum("tc,td->cd", mixed, d_low, preferred_element_type=F32).astype(BF)
        out_grad = lax.psum_scatter(out_grad, "fsdp", scatter_dimension=0, tiled=True)
        out_grad = lax.psum(out_grad, "context")
        dq, dkv = attention_backward(q, kvall, lse, d_mixed, pos_q, pos_k, n)
        d_qk = rotate(
            jnp.concatenate([dq, dkv[:, :KV_WIDTH]], axis=1).reshape(
                rows, QUERY_HEADS + KV_HEADS, HEAD),
            cosine, -sine).reshape(rows, Q_WIDTH + KV_WIDTH)
        d_projected = jnp.concatenate([d_qk, dkv[:, KV_WIDTH:]], axis=1).astype(BF)
        bias_grad = jnp.sum(d_projected.astype(F32), axis=0)
        d_normed = jnp.einsum("tc,dc->td", d_projected, qkv_w, preferred_element_type=F32)
        qkv_grad = jnp.einsum(
            "td,tc->dc", normed, d_projected, preferred_element_type=F32).astype(BF)
        qkv_grad = lax.psum_scatter(qkv_grad, "fsdp", scatter_dimension=0, tiled=True)
        qkv_grad = lax.psum(qkv_grad, "context")
        back, gain_one = normalize_back(d_normed, stream, gains_attn[l])
        gradient = d_middle + back
        small_grads[l] = (gain_one, gain_two, bias_grad)
        big_grads[l] = (qkv_grad, out_grad, dw)

    rows_small = [
        m.reshape(owners, -1)
        for k in range(3) for m in (small_grads[l][k] for l in range(LAYERS))]
    small = jnp.concatenate(rows_small, axis=1).astype(BF)[:, None]
    small = lax.psum_scatter(small, "fsdp", scatter_dimension=0, tiled=True)
    small = lax.psum(small, "context")[0, 0].astype(F32)
    grad_norm_attn = small[:LAYERS * shard].reshape(LAYERS, shard)
    grad_norm_mlp = small[LAYERS * shard:2 * LAYERS * shard].reshape(LAYERS, shard)
    grad_b_qkv = small[2 * LAYERS * shard:].reshape(LAYERS, bias_shard)

    def stacked(pick):
        return jnp.stack([pick(big_grads[l]).astype(F32) for l in range(LAYERS)])

    return (
        layer_out,
        gradient[None],
        grad_norm_attn,
        stacked(lambda m: m[0]),
        grad_b_qkv,
        stacked(lambda m: m[1]),
        grad_norm_mlp,
        stacked(lambda m: m[2][0, :, :hidden_units]),
        stacked(lambda m: m[2][1, :, :hidden_units]),
        stacked(lambda m: m[2][2, :, :hidden_units].T),
    )


def solution(mesh):
    return jax.shard_map(
        shards,
        mesh=mesh,
        in_specs=(
            P("fsdp", "context", None),
            P("fsdp", "context", None),
            P("fsdp"),
            P("fsdp", None),
            P(None, "fsdp"),
            P(None, "fsdp", None),
            P(None, "fsdp"),
            P(None, "fsdp", None),
            P(None, "fsdp"),
            P(None, "fsdp", "context"),
            P(None, "fsdp", "context"),
            P(None, "context", "fsdp"),
        ),
        out_specs=(
            P("fsdp", "context", None),
            P("fsdp", "context", None),
            P(None, "fsdp"),
            P(None, "fsdp", None),
            P(None, "fsdp"),
            P(None, "fsdp", None),
            P(None, "fsdp"),
            P(None, "fsdp", "context"),
            P(None, "fsdp", "context"),
            P(None, "context", "fsdp"),
        ),
        check_vma=False,
    )
```

time: 2070 us -> 1430 us (0.69)
  waiting for transfers between devices: 1480 us -> 614 us
  Pallas kernels: 0 us -> 592 us
  matrix products: 356 us -> 59.9 us
  blocking collectives: 78 us -> 48.2 us
  local copies, waits for them, and re-layouts: 68.9 us -> 40.8 us
    pallas_call x0 -> x8, Pallas kernels: none -> 592 us  [the longest x2 236 us: ffn_backward(): pl.pallas_call(functools.partial(ffn_backward_kernel, n, pieces, groups),...]
    all_gather x16 -> x6, waiting for transfers between devices: 613 us -> 158 us  [the longest x2 139 us: shards(): ffn_w = lax.all_gather(ffn_shard(l), 'fsdp', axis=0, tiled=False)]
    reduce_scatter x16 -> x6, waiting for transfers between devices: 757 us -> 394 us  [the longest x2 275 us: shards(): dw = lax.psum_scatter(dw, 'fsdp', scatter_dimension=0, tiled=False)]
    dot_general x42 -> x12, matrix products: 356 us -> 59.9 us  [the longest x2 12.5 us: shards(): jnp.einsum('tc,dc->td', d_projected, qkv_w, preferred_element_type=F32)]
    psum x1, waiting for transfers between devices: 107 us -> 59.3 us  [shards(): qkv_grad = lax.psum(qkv_grad, 'context')]
    unnamed x2 -> x1, blocking collectives: 49.8 us -> 24.5 us
  transfers between devices with their start and end apart: 33 -> 13, of which waited for: 32 -> 8; matrix products, arithmetic and copies ran while one was open for 14% -> 8% of each run, Pallas kernels for 0% -> 23%
where the time goes in v1:
time: 1430 us; the launch traced here: 1420 us
  waiting for transfers between devices  614 us (43%)
  Pallas kernels  592 us (41%)
  matrix products  59.9 us (4%)
  other arithmetic  51.7 us (4%)
  blocking collectives  48.2 us (3%)
  local copies, waits for them, and re-layouts  40.8 us (3%)
  between operations  15.8 us (1%)
    reduce_scatter x2, waiting for transfers between devices, shards(): dw = lax.psum_scatter(dw, 'fsdp', scatter_dimension=0, tiled=False)  275 us
    pallas_call x2, Pallas kernels, ffn_backward(): pl.pallas_call(functools.partial(ffn_backward_kernel, n, pieces, groups),...  236 us
    pallas_call x2, Pallas kernels, ffn_forward(): pl.pallas_call(functools.partial(ffn_forward_kernel, n, pieces), out_shap...  215 us
    all_gather x2, waiting for transfers between devices, shards(): ffn_w = lax.all_gather(ffn_shard(l), 'fsdp', axis=0, tiled=False)  139 us
    reduce_scatter x2, waiting for transfers between devices, shards(): lax.psum_scatter(qkv_grad, 'fsdp', scatter_dimension=0, tiled=True)  120 us
    pallas_call x2, Pallas kernels, attention_backward(): pl.pallas_call(functools.partial(attention_backward_kernel, n), out_shape...  75 us
    pallas_call x2, Pallas kernels, attention_forward(): pl.pallas_call(functools.partial(attention_forward_kernel, n), out_shape=...  66.5 us
    psum x1, waiting for transfers between devices, shards(): qkv_grad = lax.psum(qkv_grad, 'context')  59.3 us
  transfers between devices with their start and end apart: 13, of which 8 were waited for; matrix products, arithmetic and copies ran while one was open for 8% of the time, Pallas kernels for 23%

profile of v1, /device:TPU:0, one launch (start us, length us, event | category | flops | bytes accessed | tf_op | source)
XLA Modules:
  0.0 1423.7 jit_solution(17330592297353538350)
XLA Ops:
  7.2 2.8 fusion.79
  15.3 1.8 pad_maximum_fusion
  18.5 1.8 pad_maximum_fusion.1
  21.2 11.0 all-gather.7
  40.5 18.3 %all-gather.15.cloned.1.call-done = bf16[1,1536,2048]{2,1,0:T(8,128)(2,1)} async-done(((bf16[1,192,2048]{2,1,0:T(8,128)(2,1)}), bf16[1,1536,2048]{2,1,0:T(8,128)(2,1)}) %all-gather.15.cloned.1.call-update) | async-done | bytes 6291472 | tf_op jit(solution)/shard_map/all_gather | solution.py:750
  58.8 4.6 fusion.21
  69.2 35.1 %attention_forward.2 = (bf16[256,1536]{1,0:T(8,128)(2,1)}, f32[16,256]{1,0:T(8,128)}, bf16[4,256,512]{2,1,0:T(8,128)(2,1)}) custom-call(bf16[256,1536]{1,0:T(8,128)(2,1)} %copy.58.q_ref, bf16[256,512]{1,0:T(8,128)(2,1)} %pad_maximum_fusion.14.kv_ref, s32[1,256]{1,0:T(1,128)} %bitcast.162, s32[1024,1]{1,0:T(8,128)} %compare_select_fusion.pk_ref), custom_call_target="tpu_custom_call" | custom-call | flops 1610612736 | bytes 16777216 | tf_op jit(solution)/shard_map/attention_forward/pallas_call | solution.py:579
  104.3 4.3 multiply_reduce_fusion.8
  110.8 100.3 %all-gather.19.cloned.1.call-done = bf16[24,192,2304]{2,1,0:T(8,128)(2,1)} async-done(((bf16[3,192,2304]{2,1,0:T(8,128)(2,1)}), bf16[24,192,2304]{2,1,0:T(8,128)(2,1)}) %all-gather.19.cloned.1.call-update) | async-done | bytes 21233680 | tf_op jit(solution)/shard_map/all_gather | solution.py:752
  211.1 107.9 %ffn_forward.2 = (bf16[4,256,1536]{2,1,0:T(8,128)(2,1)}, bf16[4,256,2304]{2,1,0:T(8,128)(2,1)}, bf16[4,256,2304]{2,1,0:T(8,128)(2,1)}, f32[256,1536]{1,0:T(8,128)}) custom-call(bf16[256,1536]{1,0:T(8,128)(2,1)} %multiply_convert_fusion.2.x_ref, bf16[8,3,192,2304]{3,2,1,0:T(8,128)(2,1)} %bitcast.168), custom_call_target="tpu_custom_call" | custom-call | flops 21743271936 | bytes 62914560 | tf_op jit(solution)/shard_map/ffn_forward/pallas_call | solution.py:339
  319.1 2.1 multiply_reduce_fusion.7
  322.5 4.6 fusion.24
  332.9 31.4 %attention_forward.3 = (bf16[256,1536]{1,0:T(8,128)(2,1)}, f32[16,256]{1,0:T(8,128)}, bf16[4,256,512]{2,1,0:T(8,128)(2,1)}) custom-call(bf16[256,1536]{1,0:T(8,128)(2,1)} %copy.60.q_ref, bf16[256,512]{1,0:T(8,128)(2,1)} %pad_maximum_fusion.15.kv_ref, s32[1,256]{1,0:T(1,128)} %bitcast.163, s32[1024,1]{1,0:T(8,128)} %compare_select_fusion.pk_ref), custom_call_target="tpu_custom_call" | custom-call | flops 1610612736 | bytes 16777216 | tf_op jit(solution)/shard_map/attention_forward/pallas_call | solution.py:579
  364.3 4.9 multiply_reduce_fusion.6
  371.4 38.9 %all-gather.25.cloned.1.call-done = bf16[24,192,2304]{2,1,0:T(8,128)(2,1)} async-done(((bf16[3,192,2304]{2,1,0:T(8,128)(2,1)}), bf16[24,192,2304]{2,1,0:T(8,128)(2,1)}) %all-gather.25.cloned.1.call-update) | async-done | bytes 21233680 | tf_op jit(solution)/shard_map/all_gather | solution.py:752
  410.4 107.0 %ffn_forward.3 = (bf16[4,256,1536]{2,1,0:T(8,128)(2,1)}, bf16[4,256,2304]{2,1,0:T(8,128)(2,1)}, bf16[4,256,2304]{2,1,0:T(8,128)(2,1)}, f32[256,1536]{1,0:T(8,128)}) custom-call(bf16[256,1536]{1,0:T(8,128)(2,1)} %multiply_convert_fusion.x_ref, bf16[8,3,192,2304]{3,2,1,0:T(8,128)(2,1)} %bitcast.170), custom_call_target="tpu_custom_call" | custom-call | flops 21743271936 | bytes 62914560 | tf_op jit(solution)/shard_map/ffn_forward/pallas_call | solution.py:339
  517.3 119.1 %ffn_backward.2 = (bf16[8,3,192,2304]{3,2,1,0:T(8,128)(2,1)}, f32[256,1536]{1,0:T(8,128)}) custom-call(bf16[256,1536]{1,0:T(8,128)(2,1)} %fusion.45.g_ref, bf16[8,3,192,2304]{3,2,1,0:T(8,128)(2,1)} %bitcast.171, bf16[4,256,1536]{2,1,0:T(8,128)(2,1)} %get-tuple-element.36.xall_ref, bf16[4,256,2304]{2,1,0:T(8,128)(2,1)} %get-tuple-element.37.gate_ref, ...), custom_call_target="tpu_custom_call" | custom-call | flops 43486543872 | bytes 104857600 | tf_op jit(solution)/shard_map/ffn_backward/pallas_call | solution.py:514
  636.5 3.0 multiply_reduce_fusion
  639.5 3.0 fusion.44
  642.5 5.2 fusion.30.dm_ref
  647.7 38.1 %attention_backward.2 = (f32[256,1536]{1,0:T(8,128)}, f32[256,512]{1,0:T(8,128)}) custom-call(bf16[256,1536]{1,0:T(8,128)(2,1)} %copy.60.q_ref, bf16[4,256,512]{2,1,0:T(8,128)(2,1)} %get-tuple-element.40.kvall_ref, f32[16,256]{1,0:T(8,128)} %get-tuple-element.41.lse_ref, bf16[256,1536]{1,0:T(8,128)(2,1)} %fusion.30.dm_ref, s32[1,256]{1,0:T(1,128)} %bitcast.164, ...), custom_call_target="tpu_custom_call" | custom-call | flops 4026531840 | bytes 16777216 | tf_op jit(solution)/shard_map/attention_backward/pallas_call | solution.py:663
  688.5 5.1 convolution_convert_fusion.2
  700.3 6.4 multiply_reduce_fusion.2
  706.7 1.9 fusion.77
  708.6 117.0 %ffn_backward.3 = (bf16[8,3,192,2304]{3,2,1,0:T(8,128)(2,1)}, f32[256,1536]{1,0:T(8,128)}) custom-call(bf16[256,1536]{1,0:T(8,128)(2,1)} %get-tuple-element.68.g_ref, bf16[8,3,192,2304]{3,2,1,0:T(8,128)(2,1)} %bitcast.169, bf16[4,256,1536]{2,1,0:T(8,128)(2,1)} %get-tuple-element.44.xall_ref, bf16[4,256,2304]{2,1,0:T(8,128)(2,1)} %get-tuple-element.45.gate_ref, ...), custom_call_target="tpu_custom_call" | custom-call | flops 43486543872 | bytes 104857600 | tf_op jit(solution)/shard_map/ffn_backward/pallas_call | solution.py:514
  825.7 3.0 multiply_reduce_fusion.1
  828.8 2.0 multiply_add_fusion
  830.8 3.5 convolution_convert_fusion.3
  834.4 4.6 fusion.27.dm_ref
  839.1 37.0 %attention_backward.3 = (f32[256,1536]{1,0:T(8,128)}, f32[256,512]{1,0:T(8,128)}) custom-call(bf16[256,1536]{1,0:T(8,128)(2,1)} %copy.58.q_ref, bf16[4,256,512]{2,1,0:T(8,128)(2,1)} %get-tuple-element.48.kvall_ref, f32[16,256]{1,0:T(8,128)} %get-tuple-element.49.lse_ref, bf16[256,1536]{1,0:T(8,128)(2,1)} %fusion.27.dm_ref, s32[1,256]{1,0:T(1,128)} %bitcast.165, ...), custom_call_target="tpu_custom_call" | custom-call | flops 4026531840 | bytes 16777216 | tf_op jit(solution)/shard_map/attention_backward/pallas_call | solution.py:663
  884.2 4.6 convolution_convert_fusion.1
  890.3 5.9 convolution_convert_fusion
  896.3 54.7 %reduce-scatter.8.cloned.1.call-done = bf16[192,2048]{1,0:T(8,128)(2,1)} async-done(((bf16[1536,2048]{1,0:T(8,128)(2,1)}), bf16[192,2048]{1,0:T(8,128)(2,1)}) %reduce-scatter.8.cloned.1.call-update) | async-done | bytes 786448 | tf_op jit(solution)/shard_map/reduce_scatter | solution.py:794
  951.0 65.0 %reduce-scatter.10.cloned.1.call-done = bf16[192,2048]{1,0:T(8,128)(2,1)} async-done(((bf16[1536,2048]{1,0:T(8,128)(2,1)}), bf16[192,2048]{1,0:T(8,128)(2,1)}) %reduce-scatter.10.cloned.1.call-update) | async-done | bytes 786448 | tf_op jit(solution)/shard_map/reduce_scatter | solution.py:794
  1018.8 6.1 fusion.43
  1025.3 24.5 %all-reduce.6 = bf16[8,1,1280]{2,0,1:T(8,128)(2,1)S(1)} all-reduce(bf16[8,1,1280]{2,0,1:T(8,128)(2,1)S(1)} %concatenate.79), channel_id=9, replica_groups=mesh['fsdp'=8,'context'=4] {'fsdp'}, use_global_device_ids=true, to_apply=%region_15.16.clone | all-reduce | flops 10240 | bytes 40960
  1050.4 12.7 psum.35
  1065.1 3.1 fusion.40
  1068.2 59.3 %all-reduce.10.cloned.1.call-done = (bf16[1,192,2048]{2,1,0:T(8,128)(2,1)}, bf16[1,192,2048]{2,1,0:T(8,128)(2,1)}, bf16[1,192,1536]{2,1,0:T(8,128)(2,1)}, bf16[1,192,1536]{2,1,0:T(8,128)(2,1)}) async-done(((bf16[1,192,2048]{2,1,0:T(8,128)(2,1)}, bf16[1,192,2048]{2,1,0:T(8,128)(2,1)}, bf16[1,192,1536]{2,1,0:T(8,128)(2,1)}, bf16[1,192,1536]{2,1,0:T(8,128)(2,1)}), (bf16[1,192,2048]{2,1,0:T(8,128)(2,1)}, ...) | async-done | bytes 2752528 | tf_op jit(solution)/shard_map/psum | solution.py:795
  1127.6 2.9 maximum_convert_fusion.4
  1130.5 1.9 maximum_convert_fusion.3
  1132.3 135.4 %reduce-scatter.16.cloned.1.call-done = bf16[1,3,192,2304]{3,2,1,0:T(8,128)(2,1)} async-done(((bf16[8,3,192,2304]{3,2,1,0:T(8,128)(2,1)}), bf16[1,3,192,2304]{3,2,1,0:T(8,128)(2,1)}) %reduce-scatter.16.cloned.1.call-update) | async-done | bytes 2654224 | tf_op jit(solution)/shard_map/reduce_scatter | solution.py:776
  1267.7 1.9 slice_bitcast_fusion.1
  1269.6 139.4 %reduce-scatter.18.cloned.1.call-done = bf16[1,3,192,2304]{3,2,1,0:T(8,128)(2,1)} async-done(((bf16[8,3,192,2304]{3,2,1,0:T(8,128)(2,1)}), bf16[1,3,192,2304]{3,2,1,0:T(8,128)(2,1)}) %reduce-scatter.18.cloned.1.call-update) | async-done | bytes 2654224 | tf_op jit(solution)/shard_map/reduce_scatter | solution.py:776
  1409.0 1.9 slice_bitcast_fusion
  1410.8 2.0 maximum_convert_fusion.2
  1412.9 2.0 maximum_convert_fusion.1
  1414.9 2.0 maximum_convert_fusion
  (268 shorter events, 56.8 us)
Async XLA Ops:
  7.2 51.6 %all-gather.15.cloned.1.call-start = ((), (), s32[]{:S(2)}) async-start(), calls=%async_computation.12 | async-start | bytes 7077888 | tf_op jit(solution)/shard_map/all_gather | solution.py:750
  10.0 94.2 %all-gather.17.cloned.1.call-start = ((), (), s32[]{:S(2)}) async-start(), calls=%async_computation.13 | async-start | bytes 5308416 | tf_op jit(solution)/shard_map/all_gather | solution.py:751
  11.2 199.9 %all-gather.19.cloned.1.call-start = ((), (), s32[]{:S(2)}) async-start(), calls=%async_computation.14 | async-start | bytes 23887872 | tf_op jit(solution)/shard_map/all_gather | solution.py:752
  17.1 304.8 %all-gather.21.cloned.1.call-start = ((), (), s32[]{:S(2)}) async-start(), calls=%async_computation.15 | async-start | bytes 7077888 | tf_op jit(solution)/shard_map/all_gather | solution.py:750
  17.7 346.6 %all-gather.23.cloned.1.call-start = ((), (), s32[]{:S(2)}) async-start(), calls=%async_computation.16 | async-start | bytes 5308416 | tf_op jit(solution)/shard_map/all_gather | solution.py:751
  18.2 392.1 %all-gather.25.cloned.1.call-start = ((), (), s32[]{:S(2)}) async-start(), calls=%async_computation.17 | async-start | bytes 23887872 | tf_op jit(solution)/shard_map/all_gather | solution.py:752
  20.3 12.1 copy-start.69
  20.3 16.4 %copy-start.11 = (bf16[1,256,1536]{2,1,0:T(8,128)(2,1)S(1)}, bf16[1,256,1536]{2,1,0:T(8,128)(2,1)}, u32[]{:S(2)}) copy-start(bf16[1,256,1536]{2,1,0:T(8,128)(2,1)} %param.12) | copy-start | bytes 2359300
  20.3 19.1 %copy-start.18 = (bf16[1,256,1536]{2,1,0:T(8,128)(2,1)S(1)}, bf16[1,256,1536]{2,1,0:T(8,128)(2,1)}, u32[]{:S(2)}) copy-start(bf16[1,256,1536]{2,1,0:T(8,128)(2,1)} %param.13) | copy-start | bytes 2359300
  20.4 875.9 %reduce-scatter.14.cloned.1.call-start = ((), (), s32[]{:S(2)}) async-start(), calls=%async_computation.9 | async-start | bytes 5308416 | tf_op jit(solution)/shard_map/reduce_scatter | solution.py:782
  32.4 26.4 %copy-start.45 = (f32[1536]{0:T(1024)}, f32[1536]{0:T(1024)S(1)}, u32[]{:S(2)}) copy-start(f32[1536]{0:T(1024)S(1)} %mul.450) | copy-start | bytes 18436
  36.1 3.3 copy-start.58
  37.5 25.9 %copy-start.53 = (f32[256]{0:T(256)}, f32[256]{0:T(256)S(1)}, u32[]{:S(2)}) copy-start(f32[256]{0:T(256)S(1)} %get-tuple-element.112) | copy-start | bytes 3076
  38.5 26.8 %copy-start.24 = (f32[256,64]{0,1:T(8,128)}, f32[256,64]{0,1:T(8,128)S(1)}, u32[]{:S(2)}) copy-start(f32[256,64]{0,1:T(8,128)S(1)} %get-tuple-element.110) | copy-start | bytes 196612
  38.5 26.8 %copy-start.36 = (f32[256,64]{0,1:T(8,128)}, f32[256,64]{0,1:T(8,128)S(1)}, u32[]{:S(2)}) copy-start(f32[256,64]{0,1:T(8,128)S(1)} %get-tuple-element.109) | copy-start | bytes 196612
  104.3 5.5 copy-start.41
  319.1 3.4 copy-start.38
  319.1 3.4 copy-start.60
  321.2 5.9 copy-start.2
  364.3 6.1 copy-start.43
  636.4 3.1 copy-start.8
  636.4 3.1 copy-start.17
  636.4 3.1 copy-start.44
  636.4 3.1 copy-start.50
  636.4 3.1 copy-start.59
  636.5 3.1 copy-start.63
  642.5 5.2 copy-start.5
  688.5 5.1 copy-start.28
  696.6 199.7 %reduce-scatter.12.cloned.1.call-start = ((), (), s32[]{:S(2)}) async-start(), calls=%async_computation.8 | async-start | bytes 5308416 | tf_op jit(solution)/shard_map/reduce_scatter | solution.py:782
  698.4 8.2 copy-start.13
  700.2 6.4 copy-start.6
  700.2 6.4 copy-start.62
  825.6 3.1 copy-start.1
  825.7 3.1 copy-start.16
  825.7 3.1 copy-start.42
  825.7 3.1 copy-start.48
  830.8 3.6 copy-start.9
  834.4 116.6 %reduce-scatter.8.cloned.1.call-start = ((), (), s32[]{:S(2)}) async-start(), calls=%async_computation.6 | async-start | bytes 7077888 | tf_op jit(solution)/shard_map/reduce_scatter | solution.py:794
  888.9 127.1 %reduce-scatter.10.cloned.1.call-start = ((), (), s32[]{:S(2)}) async-start(), calls=%async_computation.7 | async-start | bytes 7077888 | tf_op jit(solution)/shard_map/reduce_scatter | solution.py:794
  896.2 231.3 %all-reduce.10.cloned.1.call-start = ((), (), s32[]{:S(2)}) async-start(), calls=%async_computation.18 | async-start | bytes 5505024 | tf_op jit(solution)/shard_map/psum | solution.py:795
  1016.0 251.7 %reduce-scatter.16.cloned.1.call-start = ((), (), s32[]{:S(2)}) async-start(), calls=%async_computation.10 | async-start | bytes 23887872 | tf_op jit(solution)/shard_map/reduce_scatter | solution.py:776
  1016.6 392.3 %reduce-scatter.18.cloned.1.call-start = ((), (), s32[]{:S(2)}) async-start(), calls=%async_computation.11 | async-start | bytes 23887872 | tf_op jit(solution)/shard_map/reduce_scatter | solution.py:776
  1018.7 6.2 copy-start.52
  1018.7 6.3 copy-start.64
  1018.7 6.4 copy-start.51
  1018.7 46.4 %copy-start.10 = (f32[256,1536]{1,0:T(8,128)S(1)}, f32[256,1536]{1,0:T(8,128)}, u32[]{:S(2)}) copy-start(f32[256,1536]{1,0:T(8,128)} %copy-done.9) | copy-start | bytes 4718596
  1018.8 46.4 %copy-start.55 = (f32[256]{0:T(256)S(1)}, f32[256]{0:T(256)}, u32[]{:S(2)}) copy-start(f32[256]{0:T(256)} %copy-done.53) | copy-start | bytes 3076
  1018.8 46.4 %copy-start.65 = (f32[256]{0:T(256)S(1)}, f32[256]{0:T(256)}, u32[]{:S(2)}) copy-start(f32[256]{0:T(256)} %get-tuple-element.111) | copy-start | bytes 3076
  (36 other events, 56.5 us)
Sparse Core Ops, SparseCore 0:
  10.5 48.2 all-gather.14
  61.2 38.7 all-gather.16
  102.5 108.5 all-gather.18
  213.4 45.4 all-gather.20
  260.6 38.7 all-gather.22
  301.8 108.5 all-gather.24
  696.7 51.0 reduce-scatter.13
  834.5 51.3 reduce-scatter.11
  889.3 61.7 reduce-scatter.7
  954.3 61.7 reduce-scatter.9
  1018.7 108.8 all-reduce.9
  1131.0 136.6 reduce-scatter.15
  1271.3 137.5 reduce-scatter.17

commit v2 on v1

--- a/solution.py
+++ b/solution.py
@@ -681,6 +681,295 @@
     )(q, kvall, lse, dm, pos_q, pos_k)
 
 
+def bits_of(owners):
+    return [1 << i for i in range(owners.bit_length() - 1)]
+
+
+class Cube:
+    def __init__(self, owners):
+        self.owners = owners
+        self.me = lax.axis_index("fsdp")
+        self.bits = bits_of(owners)
+        self.chip_bits = [b // 2 for b in self.bits[1:]]
+        self.chips = owners // 2
+
+    def flip(self, mask):
+        index = self.me
+        for b in self.bits:
+            if mask & b:
+                index = index + b - 2 * b * lax.rem(self.me // b, 2)
+        return index
+
+    def signal(self, bar):
+        for b in self.bits:
+            pl.semaphore_signal(bar, inc=1, device_id={"fsdp": self.flip(b)}, device_id_type=MESH)
+
+    def order(self, half):
+        return self.chip_bits[::-1] if half == 0 else self.chip_bits
+
+    def plan(self):
+        steps = {}
+        for half in (0, 1):
+            order, slot = self.order(half), 0
+            for stage, bit in enumerate(order):
+                rest = [0]
+                for other in order[stage + 1:]:
+                    rest = rest + [m | other for m in rest]
+                steps[half, stage] = (bit, rest, slot)
+                slot += len(rest)
+        return steps
+
+
+def joint_barrier(line, cube):
+    bar = pltpu.get_barrier_semaphore()
+    cube.signal(bar)
+    peers = len(cube.bits)
+
+    @pl.when(line.has_right)
+    def _():
+        pl.semaphore_signal(bar, inc=1, device_id={"context": line.right}, device_id_type=MESH)
+
+    @pl.when(line.has_left)
+    def _():
+        pl.semaphore_signal(bar, inc=1, device_id={"context": line.left}, device_id_type=MESH)
+
+    both = line.has_right & line.has_left
+
+    @pl.when(both)
+    def _():
+        pl.semaphore_wait(bar, peers + 2)
+
+    @pl.when(jnp.logical_not(both))
+    def _():
+        pl.semaphore_wait(bar, peers + 1)
+
+
+class Fold:
+    def __init__(self, cube, src, mine, first, later, load_sem, send1, recv1, send2, recv2):
+        self.cube, self.src = cube, src
+        self.mine, self.first, self.later = mine, first, later
+        self.load_sem, self.send1, self.recv1 = load_sem, send1, recv1
+        self.send2, self.recv2 = send2, recv2
+        self.rows = mine.shape[1]
+        self.half = self.rows // 2
+        self.steps = cube.plan()
+        self.stages = len(cube.chip_bits)
+
+    def _load(self, d):
+        return pltpu.make_async_copy(
+            self.src(self.cube.flip(2 * d)), self.mine.at[d], self.load_sem.at[d])
+
+    def _core(self, d):
+        return pltpu.make_async_remote_copy(
+            src_ref=self.src(self.cube.flip(2 * d | 1)), dst_ref=self.first.at[d],
+            send_sem=self.send1.at[d], recv_sem=self.recv1.at[d],
+            device_id={"fsdp": self.cube.flip(1)}, device_id_type=MESH)
+
+    def _hop(self, half, stage, index):
+        bit, rest, slot = self.steps[half, stage]
+        rows = pl.ds(half * self.half, self.half)
+        return pltpu.make_async_remote_copy(
+            src_ref=self.mine.at[bit | rest[index], rows],
+            dst_ref=self.later.at[half, slot + index],
+            send_sem=self.send2.at[half, slot + index],
+            recv_sem=self.recv2.at[half, slot + index],
+            device_id={"fsdp": self.cube.flip(2 * bit)}, device_id_type=MESH)
+
+    def _hops(self, stage):
+        return [self._hop(half, stage, i)
+                for half in (0, 1) for i in range(len(self.steps[half, stage][1]))]
+
+    def _add(self, d, base, size, other):
+        dtype = self.mine.dtype
+        strip = 48 if size % 48 == 0 else size
+
+        @pl.loop(0, size // strip)
+        def _(i):
+            into = pl.ds(pl.multiple_of(base + i * strip, 8), strip)
+            rows = pl.ds(pl.multiple_of(i * strip, 8), strip)
+            self.mine[d, into] = (
+                self.mine[d, into].astype(F32) + other(rows).astype(F32)).astype(dtype)
+
+    def start(self):
+        for d in range(self.cube.chips):
+            self._core(d).start()
+        for d in range(self.cube.chips):
+            self._load(d).start()
+
+    def phase(self, k):
+        if k == 0:
+            for d in range(self.cube.chips):
+                self._load(d).wait()
+                self._core(d).wait_recv()
+                self._add(d, 0, self.rows, lambda rows, d=d: self.first[d, rows])
+        else:
+            for half in (0, 1):
+                _, rest, slot = self.steps[half, k - 1]
+                for i, e in enumerate(rest):
+                    self._hop(half, k - 1, i).wait_recv()
+                    self._add(e, half * self.half, self.half,
+                              lambda rows, h=half, j=slot + i: self.later[h, j, rows])
+        if k < self.stages:
+            for c in self._hops(k):
+                c.start()
+
+    def finish(self):
+        for d in range(self.cube.chips):
+            self._core(d).wait_send()
+        for stage in range(self.stages):
+            for c in self._hops(stage):
+                c.wait_send()
+
+
+def fold_scratch(owners, rows, width, dtype):
+    chips = owners // 2
+    return [
+        pltpu.VMEM((chips, rows, width), dtype),
+        pltpu.VMEM((chips, rows, width), dtype),
+        pltpu.VMEM((2, chips - 1, rows // 2, width), dtype),
+        pltpu.SemaphoreType.DMA((chips,)),
+        pltpu.SemaphoreType.DMA((chips,)),
+        pltpu.SemaphoreType.DMA((chips,)),
+        pltpu.SemaphoreType.DMA((2, chips - 1)),
+        pltpu.SemaphoreType.DMA((2, chips - 1)),
+    ]
+
+
+FOLD_REFS = 8
+
+
+def reduce_kernel(n, owners, small_ref, out_ref, qkv_ref, dw_ref,
+                  small_o, out_o, qkv_o, dw_o, *refs):
+    line = Line(n)
+    cube = Cube(owners)
+    refs = list(refs)
+
+    def take(count):
+        taken = refs[:count]
+        del refs[:count]
+        return taken
+
+    sources = [
+        lambda q: small_ref.at[q],
+        lambda q: out_ref.at[q],
+        lambda q: qkv_ref.at[q],
+        lambda q: dw_ref.at[q, 0],
+        lambda q: dw_ref.at[q, 1],
+        lambda q: dw_ref.at[q, 2],
+    ]
+    folds = [Fold(cube, src, *take(FOLD_REFS)) for src in sources]
+    small_all, = take(1)
+    gather_small = Gather(line, small_all, *take(3))
+    shared = []
+    for _ in range(2):
+        part, from_l, from_r, total, own = take(5)
+        shared.append((Scatter(line, 1, part, from_l, from_r, *take(4)), part,
+                       Gather(line, total, *take(3)), total, own))
+    write_sem, = take(1)
+
+    joint_barrier(line, cube)
+    for f in folds:
+        f.start()
+    last = folds[0].stages
+
+    def after(index):
+        fold = folds[index]
+        if index == 0:
+            small_all[line.z] = fold.mine[0]
+            gather_small.start(small_all.at[line.z])
+        elif index <= 2:
+            scatter, part, _, _, own = shared[index - 1]
+            rows = part.shape[2]
+            for b in range(n):
+                @pl.when(b == line.z)
+                def _():
+                    own[...] = fold.mine[0, b * rows:(b + 1) * rows].astype(F32)
+
+                @pl.when(b != line.z)
+                def _():
+                    part[b, 0] = fold.mine[0, b * rows:(b + 1) * rows]
+
+                scatter.computed(b, 0)
+        else:
+            pltpu.make_async_copy(fold.mine.at[0], dw_o.at[index - 3], write_sem.at[index - 3]).start()
+
+    def along_line(index):
+        scatter, part, gather, total, own = shared[index]
+
+        def add_own(p, value):
+            own[...] = own[...] + value
+
+        for t in scatter.steps():
+            scatter.step(t, add_own)
+        total[line.z] = own[...].astype(BF)
+        gather.start(total.at[line.z])
+
+    def collect(index):
+        _, _, gather, total, _ = shared[index]
+        for i in range(1, n):
+            gather.arrive(line.order(i))
+        target = (out_o, qkv_o)[index]
+        target[...] = total[...].reshape(target.shape)
+
+    count = len(folds)
+    for t in range(count + last):
+        for k in range(last + 1):
+            if 0 <= t - k < count:
+                folds[t - k].phase(k)
+                if k == last:
+                    after(t - k)
+        if t == last + 2:
+            for i in range(1, n):
+                gather_small.arrive(line.order(i))
+            small_o[...] = jnp.sum(small_all[...], axis=0)
+            along_line(0)
+        if t == last + 3:
+            along_line(1)
+    collect(0)
+    collect(1)
+    for k in range(3):
+        pltpu.make_async_copy(folds[3 + k].mine.at[0], dw_o.at[k], write_sem.at[k]).wait()
+    for f in folds:
+        f.finish()
+    gather_small.finish()
+    for scatter, _, gather, _, _ in shared:
+        scatter.finish()
+        gather.finish()
+
+
+def reduce_all(small, out_g, qkv_g, dw, n):
+    owners, shard, d_model = out_g.shape
+    width = dw.shape[3]
+    qkv_width = qkv_g.shape[2]
+    scratch = fold_scratch(owners, small.shape[1], 128, F32)
+    scratch += fold_scratch(owners, shard, d_model, BF)
+    scratch += fold_scratch(owners, shard, qkv_width, BF)
+    for _ in range(3):
+        scratch += fold_scratch(owners, shard, width, BF)
+    scratch += [pltpu.VMEM((n, small.shape[1], 128), F32)] + gather_sems(n)
+    for w in (d_model, qkv_width):
+        scratch += [pltpu.VMEM((n, 1, shard // n, w), BF)] * 3
+        scratch += [pltpu.VMEM((n, shard // n, w), BF), pltpu.VMEM((shard // n, w), F32)]
+        scratch += scatter_sems(n, 1) + gather_sems(n)
+    scratch += [pltpu.SemaphoreType.DMA((3,))]
+    return pl.pallas_call(
+        functools.partial(reduce_kernel, n, owners),
+        out_shape=(
+            jax.ShapeDtypeStruct(small.shape[1:], F32),
+            jax.ShapeDtypeStruct((shard, d_model), BF),
+            jax.ShapeDtypeStruct((shard, qkv_width), BF),
+            jax.ShapeDtypeStruct((3, shard, width), BF),
+        ),
+        in_specs=[ANY] * 4,
+        out_specs=[VM, VM, VM, ANY],
+        scratch_shapes=scratch,
+        compiler_params=params(5),
+        cost_estimate=pl.CostEstimate(
+            flops=1 << 20, transcendentals=0, bytes_accessed=300 << 20),
+        name="reduce_all",
+    )(small, out_g, qkv_g, dw)
+
+
 def normalize(stream, gain):
     return stream * lax.rsqrt(jnp.mean(stream * stream, axis=-1, keepdims=True) + EPSILON) * gain
 
@@ -773,15 +1062,19 @@
         (stream, normed, q, kvall, lse, mixed, middle, xall, gate, up,
          qkv_w, out_w, ffn_w) = kept[l]
         dw, dx = ffn_backward(gradient.astype(BF), ffn_w, xall, gate, up, n)
-        dw = lax.psum_scatter(dw, "fsdp", scatter_dimension=0, tiled=False)
+        if l < LAYERS - 1:
+            out_sum, qkv_sum, dw_sum = big_grads[l + 1]
+            dx, dw_sum = lax.optimization_barrier((dx, dw_sum))
         back, gain_two = normalize_back(dx, middle, gains_mlp[l])
         d_middle = gradient + back
         d_low = d_middle.astype(BF)
         d_mixed = jnp.einsum("td,cd->tc", d_low, out_w, preferred_element_type=F32).astype(BF)
         out_grad = jnp.einsum("tc,td->cd", mixed, d_low, preferred_element_type=F32).astype(BF)
-        out_grad = lax.psum_scatter(out_grad, "fsdp", scatter_dimension=0, tiled=True)
-        out_grad = lax.psum(out_grad, "context")
         dq, dkv = attention_backward(q, kvall, lse, d_mixed, pos_q, pos_k, n)
+        if l < LAYERS - 1:
+            dq, out_sum, qkv_sum = lax.optimization_barrier((dq, out_sum, qkv_sum))
+            big_grads[l + 1] = (
+                lax.psum(out_sum, "context"), lax.psum(qkv_sum, "context"), dw_sum)
         d_qk = rotate(
             jnp.concatenate([dq, dkv[:, :KV_WIDTH]], axis=1).reshape(
                 rows, QUERY_HEADS + KV_HEADS, HEAD),
@@ -791,22 +1084,33 @@
         d_normed = jnp.einsum("tc,dc->td", d_projected, qkv_w, preferred_element_type=F32)
         qkv_grad = jnp.einsum(
             "td,tc->dc", normed, d_projected, preferred_element_type=F32).astype(BF)
-        qkv_grad = lax.psum_scatter(qkv_grad, "fsdp", scatter_dimension=0, tiled=True)
-        qkv_grad = lax.psum(qkv_grad, "context")
         back, gain_one = normalize_back(d_normed, stream, gains_attn[l])
         gradient = d_middle + back
         small_grads[l] = (gain_one, gain_two, bias_grad)
-        big_grads[l] = (qkv_grad, out_grad, dw)
-
-    rows_small = [
-        m.reshape(owners, -1)
-        for k in range(3) for m in (small_grads[l][k] for l in range(LAYERS))]
-    small = jnp.concatenate(rows_small, axis=1).astype(BF)[:, None]
-    small = lax.psum_scatter(small, "fsdp", scatter_dimension=0, tiled=True)
-    small = lax.psum(small, "context")[0, 0].astype(F32)
+        if l > 0:
+            big_grads[l] = (
+                lax.psum_scatter(out_grad, "fsdp", scatter_dimension=0, tiled=True),
+                lax.psum_scatter(qkv_grad, "fsdp", scatter_dimension=0, tiled=True),
+                lax.psum_scatter(dw, "fsdp", scatter_dimension=0, tiled=False))
+        else:
+            pieces = [
+                m.reshape(owners, -1)
+                for k in range(3) for m in (small_grads[i][k] for i in range(LAYERS))]
+            small = jnp.concatenate(pieces, axis=1)
+            used = small.shape[1]
+            small_rows = -(-used // (16 * 128)) * 16
+            small = jnp.pad(small, ((0, 0), (0, small_rows * 128 - used)))
+            small, out_sum, qkv_sum, dw_sum = reduce_all(
+                small.reshape(owners, small_rows, 128),
+                out_grad.reshape(owners, shard, d_model),
+                qkv_grad.reshape(owners, shard, qkv_grad.shape[1]), dw, n)
+            small = small.reshape(-1)
+            big_grads[l] = (out_sum, qkv_sum, dw_sum)
+
     grad_norm_attn = small[:LAYERS * shard].reshape(LAYERS, shard)
     grad_norm_mlp = small[LAYERS * shard:2 * LAYERS * shard].reshape(LAYERS, shard)
-    grad_b_qkv = small[2 * LAYERS * shard:].reshape(LAYERS, bias_shard)
+    start = 2 * LAYERS * shard
+    grad_b_qkv = small[start:start + LAYERS * bias_shard].reshape(LAYERS, bias_shard)
 
     def stacked(pick):
         return jnp.stack([pick(big_grads[l]).astype(F32) for l in range(LAYERS)])
@@ -815,9 +1119,9 @@
         layer_out,
         gradient[None],
         grad_norm_attn,
+        stacked(lambda m: m[1]),
+        grad_b_qkv,
         stacked(lambda m: m[0]),
-        grad_b_qkv,
-        stacked(lambda m: m[1]),
         grad_norm_mlp,
         stacked(lambda m: m[2][0, :, :hidden_units]),
         stacked(lambda m: m[2][1, :, :hidden_units]),

time: 1430 us -> 1150 us (0.80)
  waiting for transfers between devices: 614 us -> 210 us
  Pallas kernels: 592 us -> 753 us
  blocking collectives: 48.2 us -> 11.1 us
    reduce_scatter x2 -> x1, waiting for transfers between devices: 275 us -> 0.02 us  [shards(): lax.psum_scatter(dw, 'fsdp', scatter_dimension=0, tiled=False)]
    pallas_call x0 -> x1, Pallas kernels: none -> 160 us  [reduce_all(): pl.pallas_call(functools.partial(reduce_kernel, n, owners), out_shape=(ja...]
    reduce_scatter x2 -> x1, waiting for transfers between devices: 120 us -> 1.96 us  [shards(): lax.psum_scatter(qkv_grad, 'fsdp', scatter_dimension=0, tiled=True)]
    unnamed x1 -> x0, blocking collectives: 24.5 us -> none
  transfers between devices with their start and end apart: 13 -> 10, of which waited for: 8 -> 5; matrix products, arithmetic and copies ran while one was open for 8% -> 10% of each run, Pallas kernels for 23% -> 32%
where the time goes in v2:
time: 1150 us
  Pallas kernels  753 us (65%)
  waiting for transfers between devices  210 us (18%)
  matrix products  60.9 us (5%)
  other arithmetic  52.8 us (5%)
  local copies, waits for them, and re-layouts  43.4 us (4%)
  between operations  16.1 us (1%)
    pallas_call x2, Pallas kernels, ffn_backward(): pl.pallas_call(functools.partial(ffn_backward_kernel, n, pieces, groups),...  237 us
    pallas_call x2, Pallas kernels, ffn_forward(): pl.pallas_call(functools.partial(ffn_forward_kernel, n, pieces), out_shap...  215 us
    pallas_call x1, Pallas kernels, reduce_all(): pl.pallas_call(functools.partial(reduce_kernel, n, owners), out_shape=(ja...  160 us
    all_gather x2, waiting for transfers between devices, shards(): ffn_w = lax.all_gather(ffn_shard(l), 'fsdp', axis=0, tiled=False)  140 us
    pallas_call x2, Pallas kernels, attention_backward(): pl.pallas_call(functools.partial(attention_backward_kernel, n), out_shape...  74.3 us
    pallas_call x2, Pallas kernels, attention_forward(): pl.pallas_call(functools.partial(attention_forward_kernel, n), out_shape=...  66.5 us
    psum x1, waiting for transfers between devices, shards(): lax.psum(qkv_sum, 'context')  48.4 us
  transfers between devices with their start and end apart: 10, of which 5 were waited for; matrix products, arithmetic and copies ran while one was open for 10% of the time, Pallas kernels for 32%

profile of v2, /device:TPU:0, one launch (start us, length us, event | category | flops | bytes accessed | tf_op | source)
XLA Modules:
  0.0 1148.0 jit_solution(13360213800904916796)
XLA Ops:
  7.2 2.8 fusion.76
  15.3 1.8 pad_maximum_fusion
  18.5 1.8 pad_maximum_fusion.1
  21.5 11.1 all-gather.7
  40.1 18.7 %all-gather.15.cloned.1.call-done = bf16[1,1536,2048]{2,1,0:T(8,128)(2,1)} async-done(((bf16[1,192,2048]{2,1,0:T(8,128)(2,1)}), bf16[1,1536,2048]{2,1,0:T(8,128)(2,1)}) %all-gather.15.cloned.1.call-update) | async-done | bytes 6291472 | tf_op jit(solution)/shard_map/all_gather | solution.py:1039
  58.7 4.6 fusion.21
  63.5 1.7 copy.44
  65.2 1.7 subtract_convert_fusion.3
  69.1 35.2 %attention_forward.2 = (bf16[256,1536]{1,0:T(8,128)(2,1)}, f32[16,256]{1,0:T(8,128)}, bf16[4,256,512]{2,1,0:T(8,128)(2,1)}) custom-call(bf16[256,1536]{1,0:T(8,128)(2,1)} %copy.56.q_ref, bf16[256,512]{1,0:T(8,128)(2,1)} %pad_maximum_fusion.14.kv_ref, s32[1,256]{1,0:T(1,128)} %bitcast.169, s32[1024,1]{1,0:T(8,128)} %compare_select_fusion.pk_ref), custom_call_target="tpu_custom_call" | custom-call | flops 1610612736 | bytes 16777216 | tf_op jit(solution)/shard_map/attention_forward/pallas_call | solution.py:579
  104.3 4.3 multiply_reduce_fusion.8
  110.8 100.3 %all-gather.19.cloned.1.call-done = bf16[24,192,2304]{2,1,0:T(8,128)(2,1)} async-done(((bf16[3,192,2304]{2,1,0:T(8,128)(2,1)}), bf16[24,192,2304]{2,1,0:T(8,128)(2,1)}) %all-gather.19.cloned.1.call-update) | async-done | bytes 21233680 | tf_op jit(solution)/shard_map/all_gather | solution.py:1041
  211.1 107.8 %ffn_forward.2 = (bf16[4,256,1536]{2,1,0:T(8,128)(2,1)}, bf16[4,256,2304]{2,1,0:T(8,128)(2,1)}, bf16[4,256,2304]{2,1,0:T(8,128)(2,1)}, f32[256,1536]{1,0:T(8,128)}) custom-call(bf16[256,1536]{1,0:T(8,128)(2,1)} %multiply_convert_fusion.2.x_ref, bf16[8,3,192,2304]{3,2,1,0:T(8,128)(2,1)} %bitcast.175), custom_call_target="tpu_custom_call" | custom-call | flops 21743271936 | bytes 62914560 | tf_op jit(solution)/shard_map/ffn_forward/pallas_call | solution.py:339
  318.9 2.1 multiply_reduce_fusion.7
  321.7 4.6 fusion.24
  328.2 1.7 subtract_convert_fusion.2
  332.1 31.4 %attention_forward.3 = (bf16[256,1536]{1,0:T(8,128)(2,1)}, f32[16,256]{1,0:T(8,128)}, bf16[4,256,512]{2,1,0:T(8,128)(2,1)}) custom-call(bf16[256,1536]{1,0:T(8,128)(2,1)} %copy.58.q_ref, bf16[256,512]{1,0:T(8,128)(2,1)} %pad_maximum_fusion.15.kv_ref, s32[1,256]{1,0:T(1,128)} %bitcast.170, s32[1024,1]{1,0:T(8,128)} %compare_select_fusion.pk_ref), custom_call_target="tpu_custom_call" | custom-call | flops 1610612736 | bytes 16777216 | tf_op jit(solution)/shard_map/attention_forward/pallas_call | solution.py:579
  363.5 4.6 multiply_reduce_fusion.6
  370.4 39.9 %all-gather.25.cloned.1.call-done = bf16[24,192,2304]{2,1,0:T(8,128)(2,1)} async-done(((bf16[3,192,2304]{2,1,0:T(8,128)(2,1)}), bf16[24,192,2304]{2,1,0:T(8,128)(2,1)}) %all-gather.25.cloned.1.call-update) | async-done | bytes 21233680 | tf_op jit(solution)/shard_map/all_gather | solution.py:1041
  410.3 107.0 %ffn_forward.3 = (bf16[4,256,1536]{2,1,0:T(8,128)(2,1)}, bf16[4,256,2304]{2,1,0:T(8,128)(2,1)}, bf16[4,256,2304]{2,1,0:T(8,128)(2,1)}, f32[256,1536]{1,0:T(8,128)}) custom-call(bf16[256,1536]{1,0:T(8,128)(2,1)} %multiply_convert_fusion.x_ref, bf16[8,3,192,2304]{3,2,1,0:T(8,128)(2,1)} %bitcast.177), custom_call_target="tpu_custom_call" | custom-call | flops 21743271936 | bytes 62914560 | tf_op jit(solution)/shard_map/ffn_forward/pallas_call | solution.py:339
  517.3 118.9 %ffn_backward.2 = (bf16[8,3,192,2304]{3,2,1,0:T(8,128)(2,1)}, f32[256,1536]{1,0:T(8,128)}) custom-call(bf16[256,1536]{1,0:T(8,128)(2,1)} %fusion.45.g_ref, bf16[8,3,192,2304]{3,2,1,0:T(8,128)(2,1)} %bitcast.178, bf16[4,256,1536]{2,1,0:T(8,128)(2,1)} %get-tuple-element.45.xall_ref, bf16[4,256,2304]{2,1,0:T(8,128)(2,1)} %get-tuple-element.46.gate_ref, ...), custom_call_target="tpu_custom_call" | custom-call | flops 43486543872 | bytes 104857600 | tf_op jit(solution)/shard_map/ffn_backward/pallas_call | solution.py:514
  640.0 2.8 fusion.44
  642.8 4.2 convolution_convert_fusion.3
  647.1 5.7 fusion.30.dm_ref
  652.8 38.2 %attention_backward.2 = (f32[256,1536]{1,0:T(8,128)}, f32[256,512]{1,0:T(8,128)}) custom-call(bf16[256,1536]{1,0:T(8,128)(2,1)} %copy.58.q_ref, bf16[4,256,512]{2,1,0:T(8,128)(2,1)} %get-tuple-element.49.kvall_ref, f32[16,256]{1,0:T(8,128)} %get-tuple-element.50.lse_ref, bf16[256,1536]{1,0:T(8,128)(2,1)} %fusion.30.dm_ref, s32[1,256]{1,0:T(1,128)} %bitcast.171, ...), custom_call_target="tpu_custom_call" | custom-call | flops 4026531840 | bytes 16777216 | tf_op jit(solution)/shard_map/attention_backward/pallas_call | solution.py:663
  694.6 1.7 copy.51
  696.3 1.7 subtract_convert_fusion.1
  700.0 4.6 convolution_convert_fusion.1
  706.0 6.3 multiply_reduce_fusion.2
  715.2 3.3 fusion.74
  718.5 117.9 %ffn_backward.3 = (bf16[8,3,192,2304]{3,2,1,0:T(8,128)(2,1)}, f32[256,1536]{1,0:T(8,128)}) custom-call(bf16[256,1536]{1,0:T(8,128)(2,1)} %get-tuple-element.82.g_ref, bf16[8,3,192,2304]{3,2,1,0:T(8,128)(2,1)} %bitcast.176, bf16[4,256,1536]{2,1,0:T(8,128)(2,1)} %get-tuple-element.53.xall_ref, bf16[4,256,2304]{2,1,0:T(8,128)(2,1)} %get-tuple-element.54.gate_ref, ...), custom_call_target="tpu_custom_call" | custom-call | flops 43486543872 | bytes 104857600 | tf_op jit(solution)/shard_map/ffn_backward/pallas_call | solution.py:514
  836.5 3.5 multiply_reduce_fusion.1
  840.1 2.2 multiply_add_fusion
  842.3 5.9 fusion.27.dm_ref
  848.2 36.1 %attention_backward.3 = (f32[256,1536]{1,0:T(8,128)}, f32[256,512]{1,0:T(8,128)}) custom-call(bf16[256,1536]{1,0:T(8,128)(2,1)} %copy.56.q_ref, bf16[4,256,512]{2,1,0:T(8,128)(2,1)} %get-tuple-element.59.kvall_ref, f32[16,256]{1,0:T(8,128)} %get-tuple-element.60.lse_ref, bf16[256,1536]{1,0:T(8,128)(2,1)} %fusion.27.dm_ref, s32[1,256]{1,0:T(1,128)} %bitcast.172, ...), custom_call_target="tpu_custom_call" | custom-call | flops 4026531840 | bytes 16777216 | tf_op jit(solution)/shard_map/attention_backward/pallas_call | solution.py:663
  887.1 5.1 convolution_convert_fusion.2
  892.3 2.0 reduce-scatter.8.cloned.1.call-done
  897.0 1.7 subtract_convert_fusion
  899.9 4.6 convolution_convert_fusion
  906.1 6.4 fusion.43
  913.4 160.4 %reduce_all.1 = (f32[16,128]{1,0:T(8,128)}, bf16[192,1536]{1,0:T(8,128)(2,1)}, bf16[192,2048]{1,0:T(8,128)(2,1)}, bf16[3,192,2304]{2,1,0:T(8,128)(2,1)}) custom-call(f32[8,16,128]{2,1,0:T(8,128)} %bitcast.162, bf16[8,192,1536]{2,1,0:T(8,128)(2,1)} %bitcast.142, bf16[8,192,2048]{2,1,0:T(8,128)(2,1)} %bitcast.141, ...), custom_call_target="tpu_custom_call" | custom-call | flops 1048576 | bytes 314572800 | tf_op jit(solution)/shard_map/reduce_all/pallas_call | solution.py:955
  1073.8 1.9 slice_bitcast_fusion.1
  1076.8 2.0 maximum_convert_fusion.2
  1078.9 2.0 maximum_convert_fusion.1
  1082.9 2.0 maximum_convert_fusion
  1086.2 1.7 fusion.40
  1087.9 48.4 %all-reduce.10.cloned.1.call-done = (bf16[1,192,2048]{2,1,0:T(8,128)(2,1)}, bf16[1,192,1536]{2,1,0:T(8,128)(2,1)}) async-done(((bf16[1,192,2048]{2,1,0:T(8,128)(2,1)}, bf16[1,192,1536]{2,1,0:T(8,128)(2,1)}), (bf16[1,192,2048]{2,1,0:T(8,128)(2,1)}, bf16[1,192,1536]{2,1,0:T(8,128)(2,1)})) %all-reduce.10.cloned.1.call-update) | async-done | bytes 1376272 | tf_op jit(solution)/shard_map/psum | solution.py:1077
  1136.4 2.7 maximum_convert_fusion.4
  1139.1 1.9 maximum_convert_fusion.3
  (271 shorter events, 53.0 us)
Async XLA Ops:
  7.2 2.9 copy-start.34
  7.2 51.5 %all-gather.15.cloned.1.call-start = ((), (), s32[]{:S(2)}) async-start(), calls=%async_computation.6 | async-start | bytes 7077888 | tf_op jit(solution)/shard_map/all_gather | solution.py:1039
  10.0 94.3 %all-gather.17.cloned.1.call-start = ((), (), s32[]{:S(2)}) async-start(), calls=%async_computation.7 | async-start | bytes 5308416 | tf_op jit(solution)/shard_map/all_gather | solution.py:1040
  11.2 199.9 %all-gather.19.cloned.1.call-start = ((), (), s32[]{:S(2)}) async-start(), calls=%async_computation.8 | async-start | bytes 23887872 | tf_op jit(solution)/shard_map/all_gather | solution.py:1041
  17.1 304.6 %all-gather.21.cloned.1.call-start = ((), (), s32[]{:S(2)}) async-start(), calls=%async_computation.9 | async-start | bytes 7077888 | tf_op jit(solution)/shard_map/all_gather | solution.py:1039
  17.7 345.8 %all-gather.23.cloned.1.call-start = ((), (), s32[]{:S(2)}) async-start(), calls=%async_computation.10 | async-start | bytes 5308416 | tf_op jit(solution)/shard_map/all_gather | solution.py:1040
  18.2 392.1 %all-gather.25.cloned.1.call-start = ((), (), s32[]{:S(2)}) async-start(), calls=%async_computation.11 | async-start | bytes 23887872 | tf_op jit(solution)/shard_map/all_gather | solution.py:1041
  20.3 15.0 %copy-start.77 = (s32[1,8]{1,0:T(1,128)S(1)}, s32[1,8]{1,0:T(1,128)}, u32[]{:S(2)}) copy-start(s32[1,8]{1,0:T(1,128)} %param.15) | copy-start | bytes 100
  20.3 16.1 %copy-start.10 = (bf16[1,256,1536]{2,1,0:T(8,128)(2,1)S(1)}, bf16[1,256,1536]{2,1,0:T(8,128)(2,1)}, u32[]{:S(2)}) copy-start(bf16[1,256,1536]{2,1,0:T(8,128)(2,1)} %param.12) | copy-start | bytes 2359300
  20.3 18.6 %copy-start.20 = (bf16[1,256,1536]{2,1,0:T(8,128)(2,1)S(1)}, bf16[1,256,1536]{2,1,0:T(8,128)(2,1)}, u32[]{:S(2)}) copy-start(bf16[1,256,1536]{2,1,0:T(8,128)(2,1)} %param.13) | copy-start | bytes 2359300
  20.4 816.1 %reduce-scatter.4.cloned.1.call-start = ((), (), s32[]{:S(2)}) async-start(), calls=%async_computation.3 | async-start | bytes 23887872 | tf_op jit(solution)/shard_map/reduce_scatter | solution.py:1094
  34.6 24.1 %copy-start.48 = (f32[1536]{0:T(1024)}, f32[1536]{0:T(1024)S(1)}, u32[]{:S(2)}) copy-start(f32[1536]{0:T(1024)S(1)} %mul.450) | copy-start | bytes 18436
  35.8 3.2 copy-start.65
  37.1 26.2 %copy-start.60 = (f32[256]{0:T(256)}, f32[256]{0:T(256)S(1)}, u32[]{:S(2)}) copy-start(f32[256]{0:T(256)S(1)} %get-tuple-element.128) | copy-start | bytes 3076
  38.1 27.1 %copy-start.28 = (f32[256,64]{0,1:T(8,128)}, f32[256,64]{0,1:T(8,128)S(1)}, u32[]{:S(2)}) copy-start(f32[256,64]{0,1:T(8,128)S(1)} %get-tuple-element.126) | copy-start | bytes 196612
  38.1 27.1 %copy-start.40 = (f32[256,64]{0,1:T(8,128)}, f32[256,64]{0,1:T(8,128)S(1)}, u32[]{:S(2)}) copy-start(f32[256,64]{0,1:T(8,128)S(1)} %get-tuple-element.125) | copy-start | bytes 196612
  104.3 5.4 copy-start.42
  318.9 2.8 copy-start.44
  318.9 2.8 copy-start.67
  321.1 5.3 copy-start.2
  321.7 4.7 copy-start.63
  363.5 5.9 copy-start.46
  636.3 256.0 %reduce-scatter.6.cloned.1.call-start = ((), (), s32[]{:S(2)}) async-start(), calls=%async_computation.4 | async-start | bytes 5308416 | tf_op jit(solution)/shard_map/reduce_scatter | solution.py:1092
  640.0 2.8 copy-start.24
  642.8 4.3 copy-start.4
  647.0 247.2 %reduce-scatter.8.cloned.1.call-start = ((), (), s32[]{:S(2)}) async-start(), calls=%async_computation.5 | async-start | bytes 7077888 | tf_op jit(solution)/shard_map/reduce_scatter | solution.py:1093
  704.7 431.7 %all-reduce.10.cloned.1.call-start = ((), (), s32[]{:S(2)}) async-start(), calls=%async_computation.12 | async-start | bytes 2752512 | tf_op jit(solution)/shard_map/psum | solution.py:1077
  706.0 9.2 copy-start.5
  706.0 9.2 copy-start.70
  836.5 3.6 copy-start.1
  836.5 3.6 copy-start.14
  836.5 3.6 copy-start.43
  836.5 3.6 copy-start.57
  836.5 3.6 copy-start.69
  842.3 5.9 copy-start.8
  884.3 2.8 copy-start.23
  887.1 7.1 copy-start.32
  899.9 4.6 copy-start.22
  906.1 6.5 copy-start.53
  906.1 6.5 copy-start.54
  906.1 6.5 copy-start.55
  1078.8 4.0 copy-start.76
  1078.8 4.0 copy-start.17
  1082.8 3.4 copy-start.33
  1082.8 3.4 copy-start.50
  1082.9 3.4 copy-start.62
  1082.9 3.4 copy-start.72
  1086.2 50.1 %copy-start.37 = (bf16[192,1536]{1,0:T(8,128)(2,1)S(1)}, bf16[192,1536]{1,0:T(8,128)(2,1)}, u32[]{:S(2)}) copy-start(bf16[192,1536]{1,0:T(8,128)(2,1)} %get-tuple-element.68) | copy-start | bytes 1769476
  (40 other events, 63.4 us)
Sparse Core Ops, SparseCore 0:
  10.5 48.2 all-gather.14
  61.2 38.7 all-gather.16
  102.5 108.5 all-gather.18
  213.4 45.4 all-gather.20
  260.6 38.7 all-gather.22
  301.7 108.5 all-gather.24
  636.4 135.3 reduce-scatter.3
  775.2 53.7 reduce-scatter.5
  832.4 61.7 reduce-scatter.7
  1075.8 60.5 all-reduce.9

commit v3 on v2

--- a/solution.py
+++ b/solution.py
@@ -235,9 +235,202 @@
     )
 
 
-def ffn_forward_kernel(n, pieces, x_ref, w_ref, xall_ref, gate_ref, up_ref, y_ref,
-                       w_v, xbuf, gbuf, ubuf, hbuf, part, from_l, from_r,
-                       w_sem, x_sem, out_sem, *sems):
+def bits_of(owners):
+    return [1 << i for i in range(owners.bit_length() - 1)]
+
+
+class Cube:
+    def __init__(self, owners):
+        self.owners = owners
+        self.me = lax.axis_index("fsdp")
+        self.bits = bits_of(owners)
+        self.chip_bits = [b // 2 for b in self.bits[1:]]
+        self.chips = owners // 2
+
+    def flip(self, mask):
+        index = self.me
+        for b in self.bits:
+            if mask & b:
+                index = index + b - 2 * b * lax.rem(self.me // b, 2)
+        return index
+
+    def signal(self, bar):
+        for b in self.bits:
+            pl.semaphore_signal(bar, inc=1, device_id={"fsdp": self.flip(b)}, device_id_type=MESH)
+
+    def order(self, half):
+        return self.chip_bits[::-1] if half == 0 else self.chip_bits
+
+    def plan(self):
+        steps = {}
+        for half in (0, 1):
+            order, slot = self.order(half), 0
+            for stage, bit in enumerate(order):
+                rest = [0]
+                for other in order[stage + 1:]:
+                    rest = rest + [m | other for m in rest]
+                steps[half, stage] = (bit, rest, slot)
+                slot += len(rest)
+        return steps
+
+
+def joint_barrier(line, cube):
+    bar = pltpu.get_barrier_semaphore()
+    cube.signal(bar)
+    peers = len(cube.bits)
+
+    @pl.when(line.has_right)
+    def _():
+        pl.semaphore_signal(bar, inc=1, device_id={"context": line.right}, device_id_type=MESH)
+
+    @pl.when(line.has_left)
+    def _():
+        pl.semaphore_signal(bar, inc=1, device_id={"context": line.left}, device_id_type=MESH)
+
+    both = line.has_right & line.has_left
+
+    @pl.when(both)
+    def _():
+        pl.semaphore_wait(bar, peers + 2)
+
+    @pl.when(jnp.logical_not(both))
+    def _():
+        pl.semaphore_wait(bar, peers + 1)
+
+
+class Spread:
+    def __init__(self, cube, own, full, own_sem, send, recv, core_send, core_recv):
+        self.cube, self.own, self.full = cube, own, full
+        self.own_sem, self.send, self.recv = own_sem, send, recv
+        self.core_send, self.core_recv = core_send, core_recv
+        self.half = own.shape[0] // 2
+        self.stages = len(cube.chip_bits)
+
+    def _rows(self, half):
+        return pl.ds(half * self.half, self.half)
+
+    def _block(self, half, mask):
+        return self.full.at[self.cube.flip(mask), self._rows(half)]
+
+    def _source(self, half, mask):
+        return self._block(half, 2 * mask) if mask else self.own.at[self._rows(half)]
+
+    def _masks(self, half, stage):
+        masks = [0]
+        for bit in self.cube.order(half)[:stage]:
+            masks = masks + [m | bit for m in masks]
+        return masks
+
+    def _hop(self, half, stage, mask):
+        bit = self.cube.order(half)[stage]
+        return pltpu.make_async_remote_copy(
+            src_ref=self._source(half, mask), dst_ref=self._block(half, 2 * mask),
+            send_sem=self.send.at[half, mask | bit], recv_sem=self.recv.at[half, mask | bit],
+            device_id={"fsdp": self.cube.flip(2 * bit)}, device_id_type=MESH)
+
+    def _arrival(self, half, mask):
+        block = self._block(half, 2 * mask)
+        return pltpu.make_async_remote_copy(
+            src_ref=block, dst_ref=block,
+            send_sem=self.send.at[half, mask], recv_sem=self.recv.at[half, mask],
+            device_id={"fsdp": self.cube.flip(1)}, device_id_type=MESH)
+
+    def _core(self, half, mask):
+        return pltpu.make_async_remote_copy(
+            src_ref=self._source(half, mask), dst_ref=self._block(half, 2 * mask),
+            send_sem=self.core_send.at[half, mask], recv_sem=self.core_recv.at[half, mask],
+            device_id={"fsdp": self.cube.flip(1)}, device_id_type=MESH)
+
+    def _core_arrival(self, half, mask):
+        block = self._block(half, 2 * mask | 1)
+        return pltpu.make_async_remote_copy(
+            src_ref=block, dst_ref=block,
+            send_sem=self.core_send.at[half, mask], recv_sem=self.core_recv.at[half, mask],
+            device_id={"fsdp": self.cube.flip(1)}, device_id_type=MESH)
+
+    def _own_copy(self):
+        return pltpu.make_async_copy(self.own, self.full.at[self.cube.me], self.own_sem)
+
+    def start(self):
+        for stage in range(self.stages):
+            for half in (0, 1):
+                self._hop(half, stage, 0).start()
+        for half in (0, 1):
+            self._core(half, 0).start()
+        self._own_copy().start()
+
+    def phase(self, k):
+        for half in (0, 1):
+            bit = self.cube.order(half)[k - 1]
+            for m in self._masks(half, k - 1):
+                self._arrival(half, m | bit).wait_recv()
+                for stage in range(k, self.stages):
+                    self._hop(half, stage, m | bit).start()
+                self._core(half, m | bit).start()
+
+    def finish(self):
+        self._own_copy().wait()
+        for half in (0, 1):
+            for m in range(self.cube.chips):
+                self._core_arrival(half, m).wait_recv()
+                self._core(half, m).wait_send()
+            for stage in range(self.stages):
+                for m in self._masks(half, stage):
+                    self._hop(half, stage, m).wait_send()
+
+
+SPREAD_SEMS = 5
+
+
+def spread_sems(owners):
+    chips = owners // 2
+    return [pltpu.SemaphoreType.DMA] + [pltpu.SemaphoreType.DMA((2, chips))] * 4
+
+
+def spread_shapes(owners, shards):
+    return tuple(jax.ShapeDtypeStruct((owners,) + m.shape, m.dtype) for m in shards)
+
+
+def spread_kernel(owners, count, *refs):
+    cube = Cube(owners)
+    spreads = [
+        Spread(cube, refs[i], refs[count + i],
+               *refs[2 * count + SPREAD_SEMS * i:2 * count + SPREAD_SEMS * (i + 1)])
+        for i in range(count)]
+    bar = pltpu.get_barrier_semaphore()
+    cube.signal(bar)
+    pl.semaphore_wait(bar, len(cube.bits))
+    for s in spreads:
+        s.start()
+    for k in range(1, len(cube.chip_bits) + 1):
+        for s in spreads:
+            s.phase(k)
+    for s in spreads:
+        s.finish()
+
+
+def spread_all(owners, *shards):
+    count = len(shards)
+    return pl.pallas_call(
+        functools.partial(spread_kernel, owners, count),
+        out_shape=spread_shapes(owners, shards),
+        in_specs=[VM] * count,
+        out_specs=[ANY] * count,
+        scratch_shapes=spread_sems(owners) * count,
+        compiler_params=params(6),
+        cost_estimate=pl.CostEstimate(
+            flops=1 << 20, transcendentals=0, bytes_accessed=150 << 20),
+        name="spread_all",
+    )(*shards)
+
+
+def ffn_forward_kernel(n, pieces, count, *refs):
+    x_ref, w_ref = refs[:2]
+    next_own = refs[2:2 + count]
+    xall_ref, gate_ref, up_ref, y_ref = refs[2 + count:6 + count]
+    next_full = refs[6 + count:6 + 2 * count]
+    (w_v, xbuf, gbuf, ubuf, hbuf, part, from_l, from_r,
+     w_sem, x_sem, out_sem, *sems) = refs[6 + 2 * count:]
     line = Line(n)
     z = line.z
     owners, _, rows, width = w_ref.shape
@@ -245,25 +438,31 @@
     tile = lane_tile(width, 256)
     piece = d_model // pieces
     gather = Gather(line, xbuf, *sems[:3])
-    scatter = Scatter(line, pieces, part, from_l, from_r, *sems[3:])
+    scatter = Scatter(line, pieces, part, from_l, from_r, *sems[3:7])
+    spreads = []
+    stages = 0
+    if count:
+        cube = Cube(owners)
+        stages = len(cube.chip_bits)
+        for i in range(count):
+            at = 7 + SPREAD_SEMS * i
+            spreads.append(Spread(cube, next_own[i], next_full[i], *sems[at:at + SPREAD_SEMS]))
 
     def w_copy(k, f):
         return pltpu.make_async_copy(
             w_ref.at[f, k], w_v.at[k, pl.ds(f * rows, rows)], w_sem.at[k, f]
         )
 
-    def out_copies(b):
-        slot = lax.rem(b, 2)
-        return (
-            pltpu.make_async_copy(gbuf.at[slot], gate_ref.at[b], out_sem.at[0, slot]),
-            pltpu.make_async_copy(ubuf.at[slot], up_ref.at[b], out_sem.at[1, slot]),
-        )
-
     def x_out(b):
         return pltpu.make_async_copy(xbuf.at[b], xall_ref.at[b], x_sem.at[b])
 
-    line.barrier()
+    if count:
+        joint_barrier(line, cube)
+    else:
+        line.barrier()
     gather.start(x_ref)
+    for s in spreads:
+        s.start()
     for k in range(3):
         for f in range(owners):
             w_copy(k, f).start()
@@ -315,12 +514,26 @@
 
             scatter.computed(b, p)
 
+        if spreads:
+            @pl.when(i == n // 2)
+            def _():
+                for s in spreads:
+                    s.phase(1)
+
     def add_own(p, value):
         cols = slice(p * piece, (p + 1) * piece)
         y_ref[:, cols] = y_ref[:, cols] + value
 
+    passed = 2
     for t in scatter.steps():
         scatter.step(t, add_own)
+        if t >= 4 and t % 2 == 0 and passed <= stages:
+            for s in spreads:
+                s.phase(passed)
+            passed += 1
+    for k in range(passed, stages + 1):
+        for s in spreads:
+            s.phase(k)
     for i in range(max(0, n - 2), n):
         slot = i % 2
         pltpu.make_async_copy(gbuf.at[slot], gate_ref.at[0], out_sem.at[0, slot]).wait()
@@ -329,23 +542,26 @@
         x_out(b).wait()
     gather.finish()
     scatter.finish()
-
-
-def ffn_forward(x, w, n):
+    for s in spreads:
+        s.finish()
+
+
+def ffn_forward(x, w, n, following=()):
     rows, d_model = x.shape
     owners, _, shard, width = w.shape
     pieces = 3
     piece = d_model // pieces
+    count = len(following)
     return pl.pallas_call(
-        functools.partial(ffn_forward_kernel, n, pieces),
+        functools.partial(ffn_forward_kernel, n, pieces, count),
         out_shape=(
             jax.ShapeDtypeStruct((n, rows, d_model), BF),
             jax.ShapeDtypeStruct((n, rows, width), BF),
             jax.ShapeDtypeStruct((n, rows, width), BF),
             jax.ShapeDtypeStruct((rows, d_model), F32),
-        ),
-        in_specs=[VM, ANY],
-        out_specs=[ANY, ANY, ANY, VM],
+        ) + spread_shapes(owners, following),
+        in_specs=[VM, ANY] + [VM] * count,
+        out_specs=[ANY, ANY, ANY, VM] + [ANY] * count,
         scratch_shapes=[
             pltpu.VMEM((3, d_model, width), BF),
             pltpu.VMEM((n, rows, d_model), BF),
@@ -358,13 +574,13 @@
             pltpu.SemaphoreType.DMA((3, owners)),
             pltpu.SemaphoreType.DMA((n,)),
             pltpu.SemaphoreType.DMA((2, 2)),
-        ] + gather_sems(n) + scatter_sems(n, pieces),
-        compiler_params=params(1),
+        ] + gather_sems(n) + scatter_sems(n, pieces) + spread_sems(owners) * count,
+        compiler_params=params(7 if count else 1),
         cost_estimate=pl.CostEstimate(
             flops=6 * n * rows * d_model * width, transcendentals=n * rows * width,
             bytes_accessed=60 << 20),
         name="ffn_forward",
-    )(x, w)
+    )(x, w, *following)
 
 
 def ffn_backward_kernel(n, pieces, groups, g_ref, w_ref, xall_ref, gate_ref, up_ref, dw_ref, dx_ref,
@@ -681,69 +897,6 @@
     )(q, kvall, lse, dm, pos_q, pos_k)
 
 
-def bits_of(owners):
-    return [1 << i for i in range(owners.bit_length() - 1)]
-
-
-class Cube:
-    def __init__(self, owners):
-        self.owners = owners
-        self.me = lax.axis_index("fsdp")
-        self.bits = bits_of(owners)
-        self.chip_bits = [b // 2 for b in self.bits[1:]]
-        self.chips = owners // 2
-
-    def flip(self, mask):
-        index = self.me
-        for b in self.bits:
-            if mask & b:
-                index = index + b - 2 * b * lax.rem(self.me // b, 2)
-        return index
-
-    def signal(self, bar):
-        for b in self.bits:
-            pl.semaphore_signal(bar, inc=1, device_id={"fsdp": self.flip(b)}, device_id_type=MESH)
-
-    def order(self, half):
-        return self.chip_bits[::-1] if half == 0 else self.chip_bits
-
-    def plan(self):
-        steps = {}
-        for half in (0, 1):
-            order, slot = self.order(half), 0
-            for stage, bit in enumerate(order):
-                rest = [0]
-                for other in order[stage + 1:]:
-                    rest = rest + [m | other for m in rest]
-                steps[half, stage] = (bit, rest, slot)
-                slot += len(rest)
-        return steps
-
-
-def joint_barrier(line, cube):
-    bar = pltpu.get_barrier_semaphore()
-    cube.signal(bar)
-    peers = len(cube.bits)
-
-    @pl.when(line.has_right)
-    def _():
-        pl.semaphore_signal(bar, inc=1, device_id={"context": line.right}, device_id_type=MESH)
-
-    @pl.when(line.has_left)
-    def _():
-        pl.semaphore_signal(bar, inc=1, device_id={"context": line.left}, device_id_type=MESH)
-
-    both = line.has_right & line.has_left
-
-    @pl.when(both)
-    def _():
-        pl.semaphore_wait(bar, peers + 2)
-
-    @pl.when(jnp.logical_not(both))
-    def _():
-        pl.semaphore_wait(bar, peers + 1)
-
-
 class Fold:
     def __init__(self, cube, src, mine, first, later, load_sem, send1, recv1, send2, recv2):
         self.cube, self.src = cube, src
@@ -838,8 +991,8 @@
 FOLD_REFS = 8
 
 
-def reduce_kernel(n, owners, small_ref, out_ref, qkv_ref, dw_ref,
-                  small_o, out_o, qkv_o, dw_o, *refs):
+def reduce_kernel(n, owners, small_ref, out_ref, qkv_ref, dw_ref, early_out, early_qkv,
+                  small_o, out_o, qkv_o, dw_o, early_out_o, early_qkv_o, *refs):
     line = Line(n)
     cube = Cube(owners)
     refs = list(refs)
@@ -861,55 +1014,83 @@
     small_all, = take(1)
     gather_small = Gather(line, small_all, *take(3))
     shared = []
-    for _ in range(2):
+    for _ in range(4):
         part, from_l, from_r, total, own = take(5)
         shared.append((Scatter(line, 1, part, from_l, from_r, *take(4)), part,
                        Gather(line, total, *take(3)), total, own))
     write_sem, = take(1)
+    targets = (out_o, qkv_o, early_out_o, early_qkv_o)
+
+    def share(index, value):
+        scatter, part, _, _, own = shared[index]
+        rows = part.shape[2]
+        for b in range(n):
+            @pl.when(b == line.z)
+            def _():
+                own[...] = value(slice(b * rows, (b + 1) * rows)).astype(F32)
+
+            @pl.when(b != line.z)
+            def _():
+                part[b, 0] = value(slice(b * rows, (b + 1) * rows))
+
+            scatter.computed(b, 0)
+
+    def scatter_step(indices, t):
+        for index in indices:
+            scatter, _, _, _, own = shared[index]
+
+            def add_own(p, value):
+                own[...] = own[...] + value
+
+            scatter.step(t, add_own)
+
+    def gather_start(indices):
+        for index in indices:
+            _, _, gather, total, own = shared[index]
+            total[line.z] = own[...].astype(BF)
+            gather.start(total.at[line.z])
+
+    def gather_step(indices, i):
+        for index in indices:
+            shared[index][2].arrive(line.order(i))
+
+    def collect(indices):
+        for index in indices:
+            targets[index][...] = shared[index][3][...].reshape(targets[index].shape)
+
+    def line_jobs(indices):
+        jobs = [functools.partial(scatter_step, indices, t)
+                for t in range(1, 2 * (n - 1) + 1)]
+        jobs.append(functools.partial(gather_start, indices))
+        jobs += [functools.partial(gather_step, indices, i) for i in range(1, n)]
+        jobs.append(functools.partial(collect, indices))
+        return jobs
+
+    def small_job():
+        for i in range(1, n):
+            gather_small.arrive(line.order(i))
+        small_o[...] = jnp.sum(small_all[...], axis=0)
 
     joint_barrier(line, cube)
     for f in folds:
         f.start()
+    share(2, lambda rows: early_out[rows])
+    share(3, lambda rows: early_qkv[rows])
     last = folds[0].stages
+    jobs = line_jobs((2, 3))
 
     def after(index):
         fold = folds[index]
         if index == 0:
             small_all[line.z] = fold.mine[0]
             gather_small.start(small_all.at[line.z])
+            jobs.append(small_job)
         elif index <= 2:
-            scatter, part, _, _, own = shared[index - 1]
-            rows = part.shape[2]
-            for b in range(n):
-                @pl.when(b == line.z)
-                def _():
-                    own[...] = fold.mine[0, b * rows:(b + 1) * rows].astype(F32)
-
-                @pl.when(b != line.z)
-                def _():
-                    part[b, 0] = fold.mine[0, b * rows:(b + 1) * rows]
-
-                scatter.computed(b, 0)
+            share(index - 1, lambda rows: fold.mine[0, rows])
+            if index == 2:
+                jobs.extend(line_jobs((0, 1)))
         else:
             pltpu.make_async_copy(fold.mine.at[0], dw_o.at[index - 3], write_sem.at[index - 3]).start()
-
-    def along_line(index):
-        scatter, part, gather, total, own = shared[index]
-
-        def add_own(p, value):
-            own[...] = own[...] + value
-
-        for t in scatter.steps():
-            scatter.step(t, add_own)
-        total[line.z] = own[...].astype(BF)
-        gather.start(total.at[line.z])
-
-    def collect(index):
-        _, _, gather, total, _ = shared[index]
-        for i in range(1, n):
-            gather.arrive(line.order(i))
-        target = (out_o, qkv_o)[index]
-        target[...] = total[...].reshape(target.shape)
 
     count = len(folds)
     for t in range(count + last):
@@ -918,15 +1099,11 @@
                 folds[t - k].phase(k)
                 if k == last:
                     after(t - k)
-        if t == last + 2:
-            for i in range(1, n):
-                gather_small.arrive(line.order(i))
-            small_o[...] = jnp.sum(small_all[...], axis=0)
-            along_line(0)
-        if t == last + 3:
-            along_line(1)
-    collect(0)
-    collect(1)
+                for _ in range(2):
+                    if jobs and t >= 1:
+                        jobs.pop(0)()
+    for job in jobs:
+        job()
     for k in range(3):
         pltpu.make_async_copy(folds[3 + k].mine.at[0], dw_o.at[k], write_sem.at[k]).wait()
     for f in folds:
@@ -937,7 +1114,7 @@
         gather.finish()
 
 
-def reduce_all(small, out_g, qkv_g, dw, n):
+def reduce_all(small, out_g, qkv_g, dw, early_out, early_qkv, n):
     owners, shard, d_model = out_g.shape
     width = dw.shape[3]
     qkv_width = qkv_g.shape[2]
@@ -947,7 +1124,7 @@
     for _ in range(3):
         scratch += fold_scratch(owners, shard, width, BF)
     scratch += [pltpu.VMEM((n, small.shape[1], 128), F32)] + gather_sems(n)
-    for w in (d_model, qkv_width):
+    for w in (d_model, qkv_width, d_model, qkv_width):
         scratch += [pltpu.VMEM((n, 1, shard // n, w), BF)] * 3
         scratch += [pltpu.VMEM((n, shard // n, w), BF), pltpu.VMEM((shard // n, w), F32)]
         scratch += scatter_sems(n, 1) + gather_sems(n)
@@ -959,15 +1136,17 @@
             jax.ShapeDtypeStruct((shard, d_model), BF),
             jax.ShapeDtypeStruct((shard, qkv_width), BF),
             jax.ShapeDtypeStruct((3, shard, width), BF),
+            jax.ShapeDtypeStruct((shard, d_model), BF),
+            jax.ShapeDtypeStruct((shard, qkv_width), BF),
         ),
-        in_specs=[ANY] * 4,
-        out_specs=[VM, VM, VM, ANY],
+        in_specs=[ANY] * 4 + [VM] * 2,
+        out_specs=[VM, VM, VM, ANY, VM, VM],
         scratch_shapes=scratch,
         compiler_params=params(5),
         cost_estimate=pl.CostEstimate(
             flops=1 << 20, transcendentals=0, bytes_accessed=300 << 20),
         name="reduce_all",
-    )(small, out_g, qkv_g, dw)
+    )(small, out_g, qkv_g, dw, early_out, early_qkv)
 
 
 def normalize(stream, gain):
@@ -1016,12 +1195,29 @@
     angles = my_position.astype(F32)[:, None] * frequencies()
     cosine, sine = jnp.cos(angles)[:, None, :], jnp.sin(angles)[:, None, :]
 
-    small = jnp.concatenate(
-        [norm_attn.reshape(-1), norm_mlp.reshape(-1), b_qkv.reshape(-1)])[None, None]
-    small = lax.all_gather(small, "fsdp", axis=0, tiled=True)
-    small = small[:, 0].astype(F32)
     shard = norm_attn.shape[1]
     bias_shard = b_qkv.shape[1]
+
+    def ffn_shard(l):
+        return jnp.stack([
+            jnp.pad(m, ((0, 0), (0, pad))) for m in (w_gate[l], w_up[l], w_down[l].T)])
+
+    def packed(parts, lead):
+        flat = jnp.concatenate(parts, axis=-1)
+        used = flat.shape[-1]
+        lines = -(-used // (16 * 128)) * 16
+        flat = jnp.pad(flat, ((0, 0),) * (flat.ndim - 1) + ((0, lines * 128 - used),))
+        return flat.reshape(lead + (lines, 128))
+
+    small = packed(
+        [m.reshape(-1).astype(F32) for m in (norm_attn, norm_mlp, b_qkv)], ())
+    first_ffn = ffn_shard(0)
+    first_ffn, small = lax.optimization_barrier((first_ffn, small))
+    ffn_weights = [lax.all_gather(first_ffn, "fsdp", axis=0, tiled=False)]
+    small, qkv_w, out_w = spread_all(owners, small, w_qkv[0], w_out[0])
+    qkv_weights = [qkv_w.reshape(d_model, -1)]
+    out_weights = [out_w.reshape(Q_WIDTH, d_model)]
+    small = small.reshape(owners, -1)
     gains_attn, gains_mlp, biases = [], [], []
     for l in range(LAYERS):
         gains_attn.append(small[:, l * shard:(l + 1) * shard].reshape(-1))
@@ -1029,16 +1225,12 @@
         start = 2 * LAYERS * shard + l * bias_shard
         biases.append(small[:, start:start + bias_shard].reshape(-1))
 
-    def ffn_shard(l):
-        return jnp.stack([
-            jnp.pad(m, ((0, 0), (0, pad))) for m in (w_gate[l], w_up[l], w_down[l].T)])
-
     stream = hidden_in[0].astype(F32)
     kept = []
     for l in range(LAYERS):
-        qkv_w = lax.all_gather(w_qkv[l], "fsdp", axis=0, tiled=True)
-        out_w = lax.all_gather(w_out[l], "fsdp", axis=0, tiled=True)
-        ffn_w = lax.all_gather(ffn_shard(l), "fsdp", axis=0, tiled=False)
+        qkv_w, out_w, ffn_w = qkv_weights[l], out_weights[l], ffn_weights[l]
+        if l + 1 < LAYERS:
+            ffn_weights.append(lax.all_gather(ffn_shard(l + 1), "fsdp", axis=0, tiled=False))
         normed = normalize(stream, gains_attn[l]).astype(BF)
         projected = jnp.dot(normed, qkv_w, preferred_element_type=F32) + biases[l]
         qk = rotate(
@@ -1049,7 +1241,13 @@
         mixed, lse, kvall = attention_forward(q, kv, pos_q, pos_k, n)
         middle = stream + jnp.dot(mixed, out_w, preferred_element_type=F32)
         normed_two = normalize(middle, gains_mlp[l]).astype(BF)
-        xall, gate, up, y = ffn_forward(normed_two, ffn_w, n)
+        if l + 1 < LAYERS:
+            xall, gate, up, y, next_qkv, next_out = ffn_forward(
+                normed_two, ffn_w, n, (w_qkv[l + 1], w_out[l + 1]))
+            qkv_weights.append(next_qkv.reshape(d_model, -1))
+            out_weights.append(next_out.reshape(Q_WIDTH, d_model))
+        else:
+            xall, gate, up, y = ffn_forward(normed_two, ffn_w, n)
         kept.append((stream, normed, q, kvall, lse, mixed, middle, xall, gate, up,
                      qkv_w, out_w, ffn_w))
         stream = middle + y
@@ -1073,8 +1271,7 @@
         dq, dkv = attention_backward(q, kvall, lse, d_mixed, pos_q, pos_k, n)
         if l < LAYERS - 1:
             dq, out_sum, qkv_sum = lax.optimization_barrier((dq, out_sum, qkv_sum))
-            big_grads[l + 1] = (
-                lax.psum(out_sum, "context"), lax.psum(qkv_sum, "context"), dw_sum)
+            big_grads[l + 1] = (out_sum, qkv_sum, dw_sum)
         d_qk = rotate(
             jnp.concatenate([dq, dkv[:, :KV_WIDTH]], axis=1).reshape(
                 rows, QUERY_HEADS + KV_HEADS, HEAD),
@@ -1093,19 +1290,16 @@
                 lax.psum_scatter(qkv_grad, "fsdp", scatter_dimension=0, tiled=True),
                 lax.psum_scatter(dw, "fsdp", scatter_dimension=0, tiled=False))
         else:
-            pieces = [
+            small = packed([
                 m.reshape(owners, -1)
-                for k in range(3) for m in (small_grads[i][k] for i in range(LAYERS))]
-            small = jnp.concatenate(pieces, axis=1)
-            used = small.shape[1]
-            small_rows = -(-used // (16 * 128)) * 16
-            small = jnp.pad(small, ((0, 0), (0, small_rows * 128 - used)))
-            small, out_sum, qkv_sum, dw_sum = reduce_all(
-                small.reshape(owners, small_rows, 128),
-                out_grad.reshape(owners, shard, d_model),
-                qkv_grad.reshape(owners, shard, qkv_grad.shape[1]), dw, n)
+                for k in range(3) for m in (small_grads[i][k] for i in range(LAYERS))], (owners,))
+            out_early, qkv_early, dw_sum = big_grads[l + 1]
+            small, out_sum, qkv_sum, dw_last, out_early, qkv_early = reduce_all(
+                small, out_grad.reshape(owners, shard, d_model),
+                qkv_grad.reshape(owners, shard, qkv_grad.shape[1]), dw, out_early, qkv_early, n)
+            big_grads[l + 1] = (out_early, qkv_early, dw_sum)
             small = small.reshape(-1)
-            big_grads[l] = (out_sum, qkv_sum, dw_sum)
+            big_grads[l] = (out_sum, qkv_sum, dw_last)
 
     grad_norm_attn = small[:LAYERS * shard].reshape(LAYERS, shard)
     grad_norm_mlp = small[LAYERS * shard:2 * LAYERS * shard].reshape(LAYERS, shard)

time: 1150 us -> 1030 us (0.90)
  waiting for transfers between devices: 210 us -> 17.2 us
  Pallas kernels: 753 us -> 830 us
    all_gather x6 -> x2, waiting for transfers between devices: 159 us -> 0.01 us  [the longest x1 0.01 us: shards(): ffn_weights = [lax.all_gather(first_ffn, 'fsdp', axis=0, tiled=False)]]
    pallas_call x2 -> x3, Pallas kernels: 215 us -> 288 us  [the longest x2 200 us: ffn_forward(): pl.pallas_call(functools.partial(ffn_forward_kernel, n, pieces, count), o...]
    psum x1 -> x0, waiting for transfers between devices: 48.4 us -> none  [shards(): lax.psum(qkv_sum, 'context')]
    reduce_scatter x1, waiting for transfers between devices: 1.96 us -> 17.1 us  [shards(): lax.psum_scatter(qkv_grad, 'fsdp', scatter_dimension=0, tiled=True)]
  transfers between devices with their start and end apart: 10 -> 5, of which waited for: 5 -> 1; matrix products, arithmetic and copies ran while one was open for 10% -> 10% of each run, Pallas kernels for 32% -> 44%
where the time goes in v3:
time: 1030 us; the launch traced here: 1020 us
  Pallas kernels  830 us (81%)
  matrix products  58.8 us (6%)
  other arithmetic  53.7 us (5%)
  local copies, waits for them, and re-layouts  47.1 us (5%)
  waiting for transfers between devices  17.2 us (2%)
  between operations  15.8 us (2%)
    pallas_call x2, Pallas kernels, ffn_backward(): pl.pallas_call(functools.partial(ffn_backward_kernel, n, pieces, groups),...  234 us
    pallas_call x2, Pallas kernels, ffn_forward(): pl.pallas_call(functools.partial(ffn_forward_kernel, n, pieces, count), o...  200 us
    pallas_call x1, Pallas kernels, reduce_all(): pl.pallas_call(functools.partial(reduce_kernel, n, owners), out_shape=(ja...  169 us
    pallas_call x1, Pallas kernels, spread_all(): pl.pallas_call(functools.partial(spread_kernel, owners, count), out_shape...  88.1 us
    pallas_call x2, Pallas kernels, attention_backward(): pl.pallas_call(functools.partial(attention_backward_kernel, n), out_shape...  71.6 us
    pallas_call x2, Pallas kernels, attention_forward(): pl.pallas_call(functools.partial(attention_forward_kernel, n), out_shape=...  67.6 us
  transfers between devices with their start and end apart: 5, of which 1 were waited for; matrix products, arithmetic and copies ran while one was open for 10% of the time, Pallas kernels for 44%

profile of v3, /device:TPU:0, one launch (start us, length us, event | category | flops | bytes accessed | tf_op | source)
XLA Modules:
  0.0 1023.1 jit_solution(16390979868534851933)
XLA Ops:
  9.4 1.5 slice_bitcast_fusion.4
  14.8 1.8 pad_maximum_fusion
  16.9 1.8 pad_maximum_fusion.1
  22.3 88.1 %spread_all.1 = (f32[8,16,128]{2,1,0:T(8,128)}, bf16[8,192,2048]{2,1,0:T(8,128)(2,1)}, bf16[8,192,1536]{2,1,0:T(8,128)(2,1)}) custom-call(f32[16,128]{1,0:T(8,128)} %fusion.53.refs_0_, bf16[192,2048]{1,0:T(8,128)(2,1)} %get-tuple-element.127.refs_1_, bf16[192,1536]{1,0:T(8,128)(2,1)} %get-tuple-element.129.refs_2_), custom_call_target="tpu_custom_call" | custom-call | flops 1048576 | bytes 157286400 | tf_op jit(solution)/shard_map/spread_all/pallas_call | solution.py:414
  113.4 4.9 convolution_add_fusion.3
  118.5 1.7 copy.44
  121.9 1.8 subtract_convert_fusion.3
  130.9 36.0 %attention_forward.2 = (bf16[256,1536]{1,0:T(8,128)(2,1)}, f32[16,256]{1,0:T(8,128)}, bf16[4,256,512]{2,1,0:T(8,128)(2,1)}) custom-call(bf16[256,1536]{1,0:T(8,128)(2,1)} %copy.55.q_ref, bf16[256,512]{1,0:T(8,128)(2,1)} %pad_maximum_fusion.14.kv_ref, s32[1,256]{1,0:T(1,128)} %bitcast.186, s32[1024,1]{1,0:T(8,128)} %compare_select_fusion.pk_ref), custom_call_target="tpu_custom_call" | custom-call | flops 1610612736 | bytes 16777216 | tf_op jit(solution)/shard_map/attention_forward/pallas_call | solution.py:795
  167.0 4.3 multiply_reduce_fusion.8
  174.0 106.8 %ffn_forward.2 = (bf16[4,256,1536]{2,1,0:T(8,128)(2,1)}, bf16[4,256,2304]{2,1,0:T(8,128)(2,1)}, bf16[4,256,2304]{2,1,0:T(8,128)(2,1)}, f32[256,1536]{1,0:T(8,128...) custom-call(bf16[256,1536]{1,0:T(8,128)(2,1)} %multiply_convert_fusion.2.refs_0_, ...), custom_call_target="tpu_custom_call" | custom-call | flops 21743271936 | bytes 62914560 | tf_op jit(solution)/shard_map/ffn_forward/pallas_call | solution.py:555
  280.9 2.1 multiply_reduce_fusion.7
  283.7 4.7 convolution_add_fusion.2
  288.6 1.7 copy.48
  290.3 1.7 subtract_convert_fusion.2
  294.1 31.6 %attention_forward.3 = (bf16[256,1536]{1,0:T(8,128)(2,1)}, f32[16,256]{1,0:T(8,128)}, bf16[4,256,512]{2,1,0:T(8,128)(2,1)}) custom-call(bf16[256,1536]{1,0:T(8,128)(2,1)} %copy.57.q_ref, bf16[256,512]{1,0:T(8,128)(2,1)} %pad_maximum_fusion.15.kv_ref, s32[1,256]{1,0:T(1,128)} %bitcast.187, s32[1024,1]{1,0:T(8,128)} %compare_select_fusion.pk_ref), custom_call_target="tpu_custom_call" | custom-call | flops 1610612736 | bytes 16777216 | tf_op jit(solution)/shard_map/attention_forward/pallas_call | solution.py:795
  325.8 4.5 multiply_reduce_fusion.6
  332.6 92.8 %ffn_forward.3 = (bf16[4,256,1536]{2,1,0:T(8,128)(2,1)}, bf16[4,256,2304]{2,1,0:T(8,128)(2,1)}, bf16[4,256,2304]{2,1,0:T(8,128)(2,1)}, f32[256,1536]{1,0:T(8,128)}) custom-call(bf16[256,1536]{1,0:T(8,128)(2,1)} %multiply_convert_fusion.refs_0_, bf16[8,3,192,2304]{3,2,1,0:T(8,128)(2,1)} %bitcast.194), custom_call_target="tpu_custom_call" | custom-call | flops 21743271936 | bytes 62914560 | tf_op jit(solution)/shard_map/ffn_forward/pallas_call | solution.py:555
  425.5 117.2 %ffn_backward.2 = (bf16[8,3,192,2304]{3,2,1,0:T(8,128)(2,1)}, f32[256,1536]{1,0:T(8,128)}) custom-call(bf16[256,1536]{1,0:T(8,128)(2,1)} %fusion.19.g_ref, bf16[8,3,192,2304]{3,2,1,0:T(8,128)(2,1)} %bitcast.195, bf16[4,256,1536]{2,1,0:T(8,128)(2,1)} %get-tuple-element.61.xall_ref, bf16[4,256,2304]{2,1,0:T(8,128)(2,1)} %get-tuple-element.62.gate_ref, ...), custom_call_target="tpu_custom_call" | custom-call | flops 43486543872 | bytes 104857600 | tf_op jit(solution)/shard_map/ffn_backward/pallas_call | solution.py:730
  546.2 2.8 fusion.18
  549.0 3.6 convolution_convert_fusion.3
  552.7 5.9 convolution_convert_fusion.5.dm_ref
  558.5 36.3 %attention_backward.2 = (f32[256,1536]{1,0:T(8,128)}, f32[256,512]{1,0:T(8,128)}) custom-call(bf16[256,1536]{1,0:T(8,128)(2,1)} %copy.57.q_ref, bf16[4,256,512]{2,1,0:T(8,128)(2,1)} %get-tuple-element.65.kvall_ref, f32[16,256]{1,0:T(8,128)} %get-tuple-element.66.lse_ref, bf16[256,1536]{1,0:T(8,128)(2,1)} %convolution_convert_fusion.5.dm_ref, ...), custom_call_target="tpu_custom_call" | custom-call | flops 4026531840 | bytes 16777216 | tf_op jit(solution)/shard_map/attention_backward/pallas_call | solution.py:879
  596.9 1.5 pad_maximum_fusion.2
  598.5 1.7 copy.51
  600.2 1.7 subtract_convert_fusion.1
  603.7 4.6 convolution_convert_fusion.1
  609.7 6.3 multiply_reduce_fusion.2
  618.8 3.5 fusion.62
  622.2 117.1 %ffn_backward.3 = (bf16[8,3,192,2304]{3,2,1,0:T(8,128)(2,1)}, f32[256,1536]{1,0:T(8,128)}) custom-call(bf16[256,1536]{1,0:T(8,128)(2,1)} %get-tuple-element.98.g_ref, bf16[8,3,192,2304]{3,2,1,0:T(8,128)(2,1)} %bitcast.193, bf16[4,256,1536]{2,1,0:T(8,128)(2,1)} %get-tuple-element.69.xall_ref, bf16[4,256,2304]{2,1,0:T(8,128)(2,1)} %get-tuple-element.70.gate_ref, ...), custom_call_target="tpu_custom_call" | custom-call | flops 43486543872 | bytes 104857600 | tf_op jit(solution)/shard_map/ffn_backward/pallas_call | solution.py:730
  739.4 3.0 multiply_reduce_fusion.1
  742.4 1.9 multiply_add_fusion
  744.4 5.2 convolution_convert_fusion.4.dm_ref
  749.6 35.3 %attention_backward.3 = (f32[256,1536]{1,0:T(8,128)}, f32[256,512]{1,0:T(8,128)}) custom-call(bf16[256,1536]{1,0:T(8,128)(2,1)} %copy.55.q_ref, bf16[4,256,512]{2,1,0:T(8,128)(2,1)} %get-tuple-element.75.kvall_ref, f32[16,256]{1,0:T(8,128)} %get-tuple-element.76.lse_ref, bf16[256,1536]{1,0:T(8,128)(2,1)} %convolution_convert_fusion.4.dm_ref, ...), custom_call_target="tpu_custom_call" | custom-call | flops 4026531840 | bytes 16777216 | tf_op jit(solution)/shard_map/attention_backward/pallas_call | solution.py:879
  787.0 17.1 %reduce-scatter.8.cloned.1.call-done.early_qkv = bf16[192,2048]{1,0:T(8,128)(2,1)} async-done(((bf16[1536,2048]{1,0:T(8,128)(2,1)}), bf16[192,2048]{1,0:T(8,128)(2,1)}) %reduce-scatter.8.cloned.1.call-update) | async-done | bytes 786448 | tf_op jit(solution)/shard_map/reduce_scatter | solution.py:1290
  805.6 1.7 copy.53
  807.3 1.7 subtract_convert_fusion
  810.2 6.7 fusion.13
  818.0 3.6 convolution_convert_fusion.2
  821.6 4.6 convolution_convert_fusion
  827.1 169.0 %reduce_all.1 = (f32[16,128]{1,0:T(8,128)}, bf16[192,1536]{1,0:T(8,128)(2,1)}, bf16[192,2048]{1,0:T(8,128)(2,1)}, bf16[3,192,2304]{2,1,0:T(8,128)(2,1)}, bf16[19...) custom-call(f32[8,16,128]{2,1,0:T(8,128)} %bitcast.178, bf16[8,192,1536]{2,1,0:T(8,128)(2,1)} %bitcast.158, ...), custom_call_target="tpu_custom_call" | custom-call | flops 1048576 | bytes 314572800 | tf_op jit(solution)/shard_map/reduce_all/pallas_call | solution.py:1132
  997.6 1.9 slice_bitcast_fusion
  1001.4 2.0 slice_bitcast_fusion.1
  1003.6 1.9 maximum_convert_fusion.3
  1005.4 1.6 maximum_convert_fusion.4
  1007.0 2.0 maximum_convert_fusion.2
  1009.0 2.0 maximum_convert_fusion.1
  1011.1 2.0 maximum_convert_fusion
  1014.5 1.7 fusion.10
  (239 shorter events, 52.3 us)
Async XLA Ops:
  7.2 166.9 %all-gather.5.cloned.1.call-start = ((), (), s32[]{:S(2)}) async-start(), calls=%async_computation.6 | async-start | bytes 23887872 | tf_op jit(solution)/shard_map/all_gather | solution.py:1216
  16.6 316.0 %all-gather.7.cloned.1.call-start = ((), (), s32[]{:S(2)}) async-start(), calls=%async_computation.7 | async-start | bytes 23887872 | tf_op jit(solution)/shard_map/all_gather | solution.py:1233
  18.7 2.3 copy-start.27
  18.7 720.6 %reduce-scatter.4.cloned.1.call-start = ((), (), s32[]{:S(2)}) async-start(), calls=%async_computation.3 | async-start | bytes 23887872 | tf_op jit(solution)/shard_map/reduce_scatter | solution.py:1291
  111.4 6.9 copy-start.44
  113.4 4.9 copy-start.56
  121.9 1.8 copy-start.23
  121.9 1.8 copy-start.36
  166.9 4.9 copy-start.17
  166.9 4.9 copy-start.61
  280.9 2.8 copy-start.40
  280.9 2.8 copy-start.63
  283.0 5.3 copy-start.2
  283.7 4.7 copy-start.59
  325.8 5.8 copy-start.42
  542.7 1.9 copy-start.15
  542.7 1.9 copy-start.43
  542.7 1.9 copy-start.55
  542.8 244.2 %reduce-scatter.6.cloned.1.call-start = ((), (), s32[]{:S(2)}) async-start(), calls=%async_computation.4 | async-start | bytes 5308416 | tf_op jit(solution)/shard_map/reduce_scatter | solution.py:1289
  546.2 2.8 copy-start.20
  549.0 3.6 copy-start.4
  552.6 251.4 %reduce-scatter.8.cloned.1.call-start = ((), (), s32[]{:S(2)}) async-start(), calls=%async_computation.5 | async-start | bytes 7077888 | tf_op jit(solution)/shard_map/reduce_scatter | solution.py:1290
  601.9 1.8 copy-start.3
  601.9 1.8 copy-start.41
  609.7 9.1 copy-start.5
  609.7 9.1 copy-start.65
  739.3 3.1 copy-start.1
  739.3 3.1 copy-start.14
  739.3 3.1 copy-start.39
  739.3 3.1 copy-start.53
  739.4 3.1 copy-start.64
  744.4 5.2 copy-start.8
  810.2 7.0 copy-start.9
  821.6 4.6 copy-start.48
  821.6 4.8 copy-start.49
  821.6 4.8 copy-start.50
  821.6 4.8 copy-start.51
  997.6 1.9 copy-start.68
  1001.4 2.0 copy-start.30
  1001.4 2.2 copy-start.31
  1003.6 1.9 copy-start.32
  1003.6 1.9 copy-start.33
  1011.1 2.1 copy-start.10
  1011.1 2.7 copy-start.12
  1011.1 3.4 copy-start.28
  1011.1 3.4 copy-start.46
  1011.1 3.4 copy-start.58
  1011.1 3.4 copy-start.67
  (27 other events, 37.8 us)
Sparse Core Ops, SparseCore 0:
  16.7 144.3 all-gather.4
  163.6 145.4 all-gather.6
  542.9 138.9 reduce-scatter.3
  685.2 53.7 reduce-scatter.5
  742.3 61.7 reduce-scatter.7

commit v4 on v3

--- a/solution.py
+++ b/solution.py
@@ -583,7 +583,8 @@
     )(x, w, *following)
 
 
-def ffn_backward_kernel(n, pieces, groups, g_ref, w_ref, xall_ref, gate_ref, up_ref, dw_ref, dx_ref,
+def ffn_backward_kernel(n, pieces, groups, g_ref, w_ref, xall_ref, gate_ref, up_ref,
+                        dw_ref, dwd_ref, dx_ref,
                         w_v, gbuf, xv, gate_v, up_v, hid_v, part, from_l, from_r, stage,
                         w_sem, in_sem, out_sem, *sems):
     line = Line(n)
@@ -678,10 +679,12 @@
     per = group // shard
 
     def dw_copies(k, q, slot):
+        def target(owner):
+            return dw_ref.at[owner, k] if k < 2 else dwd_ref.at[owner]
+
         return [
             pltpu.make_async_copy(
-                stage.at[slot, pl.ds(s * shard, shard)], dw_ref.at[q * per + s, k],
-                out_sem.at[slot, s])
+                stage.at[slot, pl.ds(s * shard, shard)], target(q * per + s), out_sem.at[slot, s])
             for s in range(per)
         ]
 
@@ -730,11 +733,12 @@
     return pl.pallas_call(
         functools.partial(ffn_backward_kernel, n, pieces, groups),
         out_shape=(
-            jax.ShapeDtypeStruct((owners, 3, shard, width), BF),
+            jax.ShapeDtypeStruct((owners, 2, shard, width), BF),
+            jax.ShapeDtypeStruct((owners, shard, width), BF),
             jax.ShapeDtypeStruct((rows, d_model), F32),
         ),
         in_specs=[VM, ANY, ANY, ANY, ANY],
-        out_specs=[ANY, VM],
+        out_specs=[ANY, ANY, VM],
         scratch_shapes=[
             pltpu.VMEM((3, d_model, width), BF),
             pltpu.VMEM((n, rows, d_model), BF),
@@ -756,6 +760,100 @@
             bytes_accessed=100 << 20),
         name="ffn_backward",
     )(g, w, xall, gate, up)
+
+
+class Fold:
+    def __init__(self, cube, src, mine, first, later, load_sem, send1, recv1, send2, recv2):
+        self.cube, self.src = cube, src
+        self.mine, self.first, self.later = mine, first, later
+        self.load_sem, self.send1, self.recv1 = load_sem, send1, recv1
+        self.send2, self.recv2 = send2, recv2
+        self.rows = mine.shape[1]
+        self.half = self.rows // 2
+        self.steps = cube.plan()
+        self.stages = len(cube.chip_bits)
+
+    def _load(self, d):
+        return pltpu.make_async_copy(
+            self.src(self.cube.flip(2 * d)), self.mine.at[d], self.load_sem.at[d])
+
+    def _core(self, d):
+        return pltpu.make_async_remote_copy(
+            src_ref=self.src(self.cube.flip(2 * d | 1)), dst_ref=self.first.at[d],
+            send_sem=self.send1.at[d], recv_sem=self.recv1.at[d],
+            device_id={"fsdp": self.cube.flip(1)}, device_id_type=MESH)
+
+    def _hop(self, half, stage, index):
+        bit, rest, slot = self.steps[half, stage]
+        rows = pl.ds(half * self.half, self.half)
+        return pltpu.make_async_remote_copy(
+            src_ref=self.mine.at[bit | rest[index], rows],
+            dst_ref=self.later.at[half, slot + index],
+            send_sem=self.send2.at[half, slot + index],
+            recv_sem=self.recv2.at[half, slot + index],
+            device_id={"fsdp": self.cube.flip(2 * bit)}, device_id_type=MESH)
+
+    def _hops(self, stage):
+        return [self._hop(half, stage, i)
+                for half in (0, 1) for i in range(len(self.steps[half, stage][1]))]
+
+    def _add(self, d, base, size, other):
+        dtype = self.mine.dtype
+        strip = 48 if size % 48 == 0 else size
+
+        @pl.loop(0, size // strip)
+        def _(i):
+            into = pl.ds(pl.multiple_of(base + i * strip, 8), strip)
+            rows = pl.ds(pl.multiple_of(i * strip, 8), strip)
+            self.mine[d, into] = (
+                self.mine[d, into].astype(F32) + other(rows).astype(F32)).astype(dtype)
+
+    def start(self):
+        for d in range(self.cube.chips):
+            self._core(d).start()
+        for d in range(self.cube.chips):
+            self._load(d).start()
+
+    def phase(self, k):
+        if k == 0:
+            for d in range(self.cube.chips):
+                self._load(d).wait()
+                self._core(d).wait_recv()
+                self._add(d, 0, self.rows, lambda rows, d=d: self.first[d, rows])
+        else:
+            for half in (0, 1):
+                _, rest, slot = self.steps[half, k - 1]
+                for i, e in enumerate(rest):
+                    self._hop(half, k - 1, i).wait_recv()
+                    self._add(e, half * self.half, self.half,
+                              lambda rows, h=half, j=slot + i: self.later[h, j, rows])
+        if k < self.stages:
+            for c in self._hops(k):
+                c.start()
+
+    def finish(self):
+        for d in range(self.cube.chips):
+            self._core(d).wait_send()
+        for stage in range(self.stages):
+            for c in self._hops(stage):
+                c.wait_send()
+
+
+def fold_scratch(owners, rows, width, dtype):
+    chips = owners // 2
+    return [
+        pltpu.VMEM((chips, rows, width), dtype),
+        pltpu.VMEM((chips, rows, width), dtype),
+        pltpu.VMEM((2, chips - 1, rows // 2, width), dtype),
+        pltpu.SemaphoreType.DMA((chips,)),
+        pltpu.SemaphoreType.DMA((chips,)),
+        pltpu.SemaphoreType.DMA((chips,)),
+        pltpu.SemaphoreType.DMA((2, chips - 1)),
+        pltpu.SemaphoreType.DMA((2, chips - 1)),
+    ]
+
+
+FOLD_REFS = 8
 
 
 def attention_forward_kernel(n, q_ref, kv_ref, pq_ref, pk_ref, mixed_ref, lse_ref, kvall_ref,
@@ -813,15 +911,20 @@
     )(q, kv, pos_q, pos_k)
 
 
-def attention_backward_kernel(n, q_ref, kvall_ref, lse_ref, dm_ref, pq_ref, pk_ref,
-                              dq_ref, dkv_ref, kt, dk_acc, dv_acc, part, from_l, from_r, *sems):
+def attention_backward_kernel(n, owners, q_ref, kvall_ref, lse_ref, dm_ref, pq_ref, pk_ref,
+                              grad_ref, dq_ref, dkv_ref, sum_ref,
+                              kt, dk_acc, dv_acc, part, from_l, from_r, *refs):
+    fold_refs, sems = refs[:FOLD_REFS], refs[FOLD_REFS:]
     line = Line(n)
+    cube = Cube(owners)
+    fold = Fold(cube, lambda q: grad_ref.at[q], *fold_refs)
     z = line.z
     rows = q_ref.shape[0]
     total = n * rows
     pieces = KV_HEADS
     scatter = Scatter(line, pieces, part, from_l, from_r, *sems)
-    line.barrier()
+    joint_barrier(line, cube)
+    fold.start()
     allowed = pk_ref[...] <= pq_ref[...]
     for g in range(KV_HEADS):
         k = kvall_ref[:, :, g * HEAD:(g + 1) * HEAD].reshape(total, HEAD)
@@ -848,6 +951,10 @@
                 dk_acc[...] += dk
                 dv_acc[...] += dv
             dq_ref[:, cols] = dot_nn(kt[g], ds).T
+            if h == 1:
+                fold.phase(0)
+            if h == 8:
+                fold.phase(1)
         for b in range(n):
             sl = slice(b * rows, (b + 1) * rows)
 
@@ -871,128 +978,44 @@
 
     for t in scatter.steps():
         scatter.step(t, add_own)
+    for k in range(2, fold.stages + 1):
+        fold.phase(k)
+    sum_ref[...] = fold.mine[0]
     scatter.finish()
-
-
-def attention_backward(q, kvall, lse, dm, pos_q, pos_k, n):
+    fold.finish()
+
+
+def attention_backward(q, kvall, lse, dm, pos_q, pos_k, grad, n):
     rows = q.shape[0]
+    owners, shard, d_model = grad.shape
     return pl.pallas_call(
-        functools.partial(attention_backward_kernel, n),
+        functools.partial(attention_backward_kernel, n, owners),
         out_shape=(
             jax.ShapeDtypeStruct((rows, Q_WIDTH), F32),
             jax.ShapeDtypeStruct((rows, 2 * KV_WIDTH), F32),
+            jax.ShapeDtypeStruct((shard, d_model), BF),
         ),
-        in_specs=[VM] * 6,
-        out_specs=[VM] * 2,
+        in_specs=[VM] * 6 + [ANY],
+        out_specs=[VM] * 3,
         scratch_shapes=[
             pltpu.VMEM((KV_HEADS, HEAD, n * rows), BF),
             pltpu.VMEM((n * rows, HEAD), F32),
             pltpu.VMEM((n * rows, HEAD), F32),
-        ] + [pltpu.VMEM((n, KV_HEADS, rows, 2 * HEAD), BF)] * 3 + scatter_sems(n, KV_HEADS),
+        ] + [pltpu.VMEM((n, KV_HEADS, rows, 2 * HEAD), BF)] * 3
+        + fold_scratch(owners, shard, d_model, BF) + scatter_sems(n, KV_HEADS),
         compiler_params=params(4),
         cost_estimate=pl.CostEstimate(
             flops=10 * n * rows * rows * Q_WIDTH, transcendentals=n * rows * rows * QUERY_HEADS,
             bytes_accessed=16 << 20),
         name="attention_backward",
-    )(q, kvall, lse, dm, pos_q, pos_k)
-
-
-class Fold:
-    def __init__(self, cube, src, mine, first, later, load_sem, send1, recv1, send2, recv2):
-        self.cube, self.src = cube, src
-        self.mine, self.first, self.later = mine, first, later
-        self.load_sem, self.send1, self.recv1 = load_sem, send1, recv1
-        self.send2, self.recv2 = send2, recv2
-        self.rows = mine.shape[1]
-        self.half = self.rows // 2
-        self.steps = cube.plan()
-        self.stages = len(cube.chip_bits)
-
-    def _load(self, d):
-        return pltpu.make_async_copy(
-            self.src(self.cube.flip(2 * d)), self.mine.at[d], self.load_sem.at[d])
-
-    def _core(self, d):
-        return pltpu.make_async_remote_copy(
-            src_ref=self.src(self.cube.flip(2 * d | 1)), dst_ref=self.first.at[d],
-            send_sem=self.send1.at[d], recv_sem=self.recv1.at[d],
-            device_id={"fsdp": self.cube.flip(1)}, device_id_type=MESH)
-
-    def _hop(self, half, stage, index):
-        bit, rest, slot = self.steps[half, stage]
-        rows = pl.ds(half * self.half, self.half)
-        return pltpu.make_async_remote_copy(
-            src_ref=self.mine.at[bit | rest[index], rows],
-            dst_ref=self.later.at[half, slot + index],
-            send_sem=self.send2.at[half, slot + index],
-            recv_sem=self.recv2.at[half, slot + index],
-            device_id={"fsdp": self.cube.flip(2 * bit)}, device_id_type=MESH)
-
-    def _hops(self, stage):
-        return [self._hop(half, stage, i)
-                for half in (0, 1) for i in range(len(self.steps[half, stage][1]))]
-
-    def _add(self, d, base, size, other):
-        dtype = self.mine.dtype
-        strip = 48 if size % 48 == 0 else size
-
-        @pl.loop(0, size // strip)
-        def _(i):
-            into = pl.ds(pl.multiple_of(base + i * strip, 8), strip)
-            rows = pl.ds(pl.multiple_of(i * strip, 8), strip)
-            self.mine[d, into] = (
-                self.mine[d, into].astype(F32) + other(rows).astype(F32)).astype(dtype)
-
-    def start(self):
-        for d in range(self.cube.chips):
-            self._core(d).start()
-        for d in range(self.cube.chips):
-            self._load(d).start()
-
-    def phase(self, k):
-        if k == 0:
-            for d in range(self.cube.chips):
-                self._load(d).wait()
-                self._core(d).wait_recv()
-                self._add(d, 0, self.rows, lambda rows, d=d: self.first[d, rows])
-        else:
-            for half in (0, 1):
-                _, rest, slot = self.steps[half, k - 1]
-                for i, e in enumerate(rest):
-                    self._hop(half, k - 1, i).wait_recv()
-                    self._add(e, half * self.half, self.half,
-                              lambda rows, h=half, j=slot + i: self.later[h, j, rows])
-        if k < self.stages:
-            for c in self._hops(k):
-                c.start()
-
-    def finish(self):
-        for d in range(self.cube.chips):
-            self._core(d).wait_send()
-        for stage in range(self.stages):
-            for c in self._hops(stage):
-                c.wait_send()
-
-
-def fold_scratch(owners, rows, width, dtype):
-    chips = owners // 2
-    return [
-        pltpu.VMEM((chips, rows, width), dtype),
-        pltpu.VMEM((chips, rows, width), dtype),
-        pltpu.VMEM((2, chips - 1, rows // 2, width), dtype),
-        pltpu.SemaphoreType.DMA((chips,)),
-        pltpu.SemaphoreType.DMA((chips,)),
-        pltpu.SemaphoreType.DMA((chips,)),
-        pltpu.SemaphoreType.DMA((2, chips - 1)),
-        pltpu.SemaphoreType.DMA((2, chips - 1)),
-    ]
-
-
-FOLD_REFS = 8
-
-
-def reduce_kernel(n, owners, small_ref, out_ref, qkv_ref, dw_ref, early_out, early_qkv,
-                  small_o, out_o, qkv_o, dw_o, early_out_o, early_qkv_o, *refs):
+    )(q, kvall, lse, dm, pos_q, pos_k, grad)
+
+
+def reduce_kernel(n, owners, count, small_ref, qkv_ref, dw_ref, *refs):
+    early = refs[:count]
+    small_o, qkv_o, dw_o = refs[count:count + 3]
+    targets = (qkv_o,) + refs[count + 3:2 * count + 3]
+    refs = refs[2 * count + 3:]
     line = Line(n)
     cube = Cube(owners)
     refs = list(refs)
@@ -1004,22 +1027,18 @@
 
     sources = [
         lambda q: small_ref.at[q],
-        lambda q: out_ref.at[q],
         lambda q: qkv_ref.at[q],
-        lambda q: dw_ref.at[q, 0],
-        lambda q: dw_ref.at[q, 1],
-        lambda q: dw_ref.at[q, 2],
+        lambda q: dw_ref.at[q],
     ]
     folds = [Fold(cube, src, *take(FOLD_REFS)) for src in sources]
     small_all, = take(1)
     gather_small = Gather(line, small_all, *take(3))
     shared = []
-    for _ in range(4):
+    for _ in targets:
         part, from_l, from_r, total, own = take(5)
         shared.append((Scatter(line, 1, part, from_l, from_r, *take(4)), part,
                        Gather(line, total, *take(3)), total, own))
     write_sem, = take(1)
-    targets = (out_o, qkv_o, early_out_o, early_qkv_o)
 
     def share(index, value):
         scatter, part, _, _, own = shared[index]
@@ -1074,10 +1093,10 @@
     joint_barrier(line, cube)
     for f in folds:
         f.start()
-    share(2, lambda rows: early_out[rows])
-    share(3, lambda rows: early_qkv[rows])
+    for i, ref in enumerate(early):
+        share(1 + i, lambda rows, ref=ref: ref[rows])
     last = folds[0].stages
-    jobs = line_jobs((2, 3))
+    jobs = line_jobs(range(1, 1 + count))
 
     def after(index):
         fold = folds[index]
@@ -1085,27 +1104,24 @@
             small_all[line.z] = fold.mine[0]
             gather_small.start(small_all.at[line.z])
             jobs.append(small_job)
-        elif index <= 2:
-            share(index - 1, lambda rows: fold.mine[0, rows])
-            if index == 2:
-                jobs.extend(line_jobs((0, 1)))
+        elif index == 1:
+            share(0, lambda rows: fold.mine[0, rows])
+            jobs.extend(line_jobs((0,)))
         else:
-            pltpu.make_async_copy(fold.mine.at[0], dw_o.at[index - 3], write_sem.at[index - 3]).start()
-
-    count = len(folds)
-    for t in range(count + last):
+            pltpu.make_async_copy(fold.mine.at[0], dw_o, write_sem).start()
+
+    for t in range(len(folds) + last):
         for k in range(last + 1):
-            if 0 <= t - k < count:
+            if 0 <= t - k < len(folds):
                 folds[t - k].phase(k)
                 if k == last:
                     after(t - k)
-                for _ in range(2):
+                for _ in range(3):
                     if jobs and t >= 1:
                         jobs.pop(0)()
     for job in jobs:
         job()
-    for k in range(3):
-        pltpu.make_async_copy(folds[3 + k].mine.at[0], dw_o.at[k], write_sem.at[k]).wait()
+    pltpu.make_async_copy(folds[2].mine.at[0], dw_o, write_sem).wait()
     for f in folds:
         f.finish()
     gather_small.finish()
@@ -1114,39 +1130,33 @@
         gather.finish()
 
 
-def reduce_all(small, out_g, qkv_g, dw, early_out, early_qkv, n):
-    owners, shard, d_model = out_g.shape
-    width = dw.shape[3]
-    qkv_width = qkv_g.shape[2]
+def reduce_all(small, qkv_g, dw, early, n):
+    owners, shard, qkv_width = qkv_g.shape
+    width = dw.shape[2]
     scratch = fold_scratch(owners, small.shape[1], 128, F32)
-    scratch += fold_scratch(owners, shard, d_model, BF)
     scratch += fold_scratch(owners, shard, qkv_width, BF)
-    for _ in range(3):
-        scratch += fold_scratch(owners, shard, width, BF)
+    scratch += fold_scratch(owners, shard, width, BF)
     scratch += [pltpu.VMEM((n, small.shape[1], 128), F32)] + gather_sems(n)
-    for w in (d_model, qkv_width, d_model, qkv_width):
+    for w in [qkv_width] + [m.shape[1] for m in early]:
         scratch += [pltpu.VMEM((n, 1, shard // n, w), BF)] * 3
         scratch += [pltpu.VMEM((n, shard // n, w), BF), pltpu.VMEM((shard // n, w), F32)]
         scratch += scatter_sems(n, 1) + gather_sems(n)
-    scratch += [pltpu.SemaphoreType.DMA((3,))]
+    scratch += [pltpu.SemaphoreType.DMA]
     return pl.pallas_call(
-        functools.partial(reduce_kernel, n, owners),
+        functools.partial(reduce_kernel, n, owners, len(early)),
         out_shape=(
             jax.ShapeDtypeStruct(small.shape[1:], F32),
-            jax.ShapeDtypeStruct((shard, d_model), BF),
             jax.ShapeDtypeStruct((shard, qkv_width), BF),
-            jax.ShapeDtypeStruct((3, shard, width), BF),
-            jax.ShapeDtypeStruct((shard, d_model), BF),
-            jax.ShapeDtypeStruct((shard, qkv_width), BF),
-        ),
-        in_specs=[ANY] * 4 + [VM] * 2,
-        out_specs=[VM, VM, VM, ANY, VM, VM],
+            jax.ShapeDtypeStruct((shard, width), BF),
+        ) + tuple(jax.ShapeDtypeStruct(m.shape, BF) for m in early),
+        in_specs=[ANY] * 3 + [VM] * len(early),
+        out_specs=[VM, VM, ANY] + [VM] * len(early),
         scratch_shapes=scratch,
         compiler_params=params(5),
         cost_estimate=pl.CostEstimate(
             flops=1 << 20, transcendentals=0, bytes_accessed=300 << 20),
         name="reduce_all",
-    )(small, out_g, qkv_g, dw, early_out, early_qkv)
+    )(small, qkv_g, dw, *early)
 
 
 def normalize(stream, gain):
@@ -1255,23 +1265,26 @@
 
     gradient = cotangent[0].astype(F32) * my_valid[:, None].astype(F32)
     small_grads = [None] * LAYERS
-    big_grads = [None] * LAYERS
+    out_sums, qkv_sums, ffn_sums, down_sums = ([None] * LAYERS for _ in range(4))
     for l in reversed(range(LAYERS)):
         (stream, normed, q, kvall, lse, mixed, middle, xall, gate, up,
          qkv_w, out_w, ffn_w) = kept[l]
-        dw, dx = ffn_backward(gradient.astype(BF), ffn_w, xall, gate, up, n)
+        dw, dw_down, dx = ffn_backward(gradient.astype(BF), ffn_w, xall, gate, up, n)
         if l < LAYERS - 1:
-            out_sum, qkv_sum, dw_sum = big_grads[l + 1]
-            dx, dw_sum = lax.optimization_barrier((dx, dw_sum))
+            dx, ffn_sums[l + 1], down_sums[l + 1] = lax.optimization_barrier(
+                (dx, ffn_sums[l + 1], down_sums[l + 1]))
+        ffn_sums[l] = lax.psum_scatter(dw, "fsdp", scatter_dimension=0, tiled=False)
+        if l > 0:
+            down_sums[l] = lax.psum_scatter(dw_down, "fsdp", scatter_dimension=0, tiled=False)
         back, gain_two = normalize_back(dx, middle, gains_mlp[l])
         d_middle = gradient + back
         d_low = d_middle.astype(BF)
         d_mixed = jnp.einsum("td,cd->tc", d_low, out_w, preferred_element_type=F32).astype(BF)
         out_grad = jnp.einsum("tc,td->cd", mixed, d_low, preferred_element_type=F32).astype(BF)
-        dq, dkv = attention_backward(q, kvall, lse, d_mixed, pos_q, pos_k, n)
+        dq, dkv, out_sums[l] = attention_backward(
+            q, kvall, lse, d_mixed, pos_q, pos_k, out_grad.reshape(owners, shard, d_model), n)
         if l < LAYERS - 1:
-            dq, out_sum, qkv_sum = lax.optimization_barrier((dq, out_sum, qkv_sum))
-            big_grads[l + 1] = (out_sum, qkv_sum, dw_sum)
+            dq, qkv_sums[l + 1] = lax.optimization_barrier((dq, qkv_sums[l + 1]))
         d_qk = rotate(
             jnp.concatenate([dq, dkv[:, :KV_WIDTH]], axis=1).reshape(
                 rows, QUERY_HEADS + KV_HEADS, HEAD),
@@ -1285,41 +1298,35 @@
         gradient = d_middle + back
         small_grads[l] = (gain_one, gain_two, bias_grad)
         if l > 0:
-            big_grads[l] = (
-                lax.psum_scatter(out_grad, "fsdp", scatter_dimension=0, tiled=True),
-                lax.psum_scatter(qkv_grad, "fsdp", scatter_dimension=0, tiled=True),
-                lax.psum_scatter(dw, "fsdp", scatter_dimension=0, tiled=False))
-        else:
-            small = packed([
-                m.reshape(owners, -1)
-                for k in range(3) for m in (small_grads[i][k] for i in range(LAYERS))], (owners,))
-            out_early, qkv_early, dw_sum = big_grads[l + 1]
-            small, out_sum, qkv_sum, dw_last, out_early, qkv_early = reduce_all(
-                small, out_grad.reshape(owners, shard, d_model),
-                qkv_grad.reshape(owners, shard, qkv_grad.shape[1]), dw, out_early, qkv_early, n)
-            big_grads[l + 1] = (out_early, qkv_early, dw_sum)
-            small = small.reshape(-1)
-            big_grads[l] = (out_sum, qkv_sum, dw_last)
+            qkv_sums[l] = lax.psum_scatter(qkv_grad, "fsdp", scatter_dimension=0, tiled=True)
+    small = packed([
+        m.reshape(owners, -1)
+        for k in range(3) for m in (small_grads[i][k] for i in range(LAYERS))], (owners,))
+    small, qkv_sums[0], down_sums[0], *early = reduce_all(
+        small, qkv_grad.reshape(owners, shard, qkv_grad.shape[1]), dw_down,
+        out_sums + qkv_sums[1:], n)
+    out_sums, qkv_sums = early[:LAYERS], qkv_sums[:1] + early[LAYERS:]
+    small = small.reshape(-1)
 
     grad_norm_attn = small[:LAYERS * shard].reshape(LAYERS, shard)
     grad_norm_mlp = small[LAYERS * shard:2 * LAYERS * shard].reshape(LAYERS, shard)
     start = 2 * LAYERS * shard
     grad_b_qkv = small[start:start + LAYERS * bias_shard].reshape(LAYERS, bias_shard)
 
-    def stacked(pick):
-        return jnp.stack([pick(big_grads[l]).astype(F32) for l in range(LAYERS)])
+    def stacked(sums, pick=lambda m: m):
+        return jnp.stack([pick(m).astype(F32) for m in sums])
 
     return (
         layer_out,
         gradient[None],
         grad_norm_attn,
-        stacked(lambda m: m[1]),
+        stacked(qkv_sums),
         grad_b_qkv,
-        stacked(lambda m: m[0]),
+        stacked(out_sums),
         grad_norm_mlp,
-        stacked(lambda m: m[2][0, :, :hidden_units]),
-        stacked(lambda m: m[2][1, :, :hidden_units]),
-        stacked(lambda m: m[2][2, :, :hidden_units].T),
+        stacked(ffn_sums, lambda m: m[0, :, :hidden_units]),
+        stacked(ffn_sums, lambda m: m[1, :, :hidden_units]),
+        stacked(down_sums, lambda m: m[:, :hidden_units].T),
     )
 
 

time: 1030 us -> 1030 us (level)
  Pallas kernels: 830 us -> 857 us
  waiting for transfers between devices: 17.2 us -> 0.59 us
    pallas_call x3, Pallas kernels: 241 us -> 262 us  [the longest x1 136 us: reduce_all(): pl.pallas_call(functools.partial(reduce_kernel, n, owners, len(early)), o...]
    reduce_scatter x1, waiting for transfers between devices: 17.1 us -> 0.01 us  [shards(): lax.psum_scatter(qkv_grad, 'fsdp', scatter_dimension=0, tiled=True)]
  transfers between devices with their start and end apart: 5 -> 6, of which waited for: 1 -> 0; matrix products, arithmetic and copies ran while one was open for 10% -> 11% of each run, Pallas kernels for 44% -> 63%
where the time goes in v4:
time: 1030 us
  Pallas kernels  857 us (83%)
  matrix products  54.2 us (5%)
  local copies, waits for them, and re-layouts  49.3 us (5%)
  other arithmetic  48 us (5%)
  between operations  16 us (2%)
    pallas_call x2, Pallas kernels, ffn_backward(): pl.pallas_call(functools.partial(ffn_backward_kernel, n, pieces, groups),...  240 us
    pallas_call x2, Pallas kernels, ffn_forward(): pl.pallas_call(functools.partial(ffn_forward_kernel, n, pieces, count), o...  199 us
    pallas_call x1, Pallas kernels, reduce_all(): pl.pallas_call(functools.partial(reduce_kernel, n, owners, len(early)), o...  136 us
    pallas_call x2, Pallas kernels, attention_backward(): pl.pallas_call(functools.partial(attention_backward_kernel, n, owners), o...  126 us
    pallas_call x1, Pallas kernels, spread_all(): pl.pallas_call(functools.partial(spread_kernel, owners, count), out_shape...  88.1 us
    pallas_call x2, Pallas kernels, attention_forward(): pl.pallas_call(functools.partial(attention_forward_kernel, n), out_shape=...  68 us
  transfers between devices with their start and end apart: 6, of which 0 were waited for; matrix products, arithmetic and copies ran while one was open for 11% of the time, Pallas kernels for 63%

profile of v4, /device:TPU:0, one launch (start us, length us, event | category | flops | bytes accessed | tf_op | source)
XLA Modules:
  0.0 1025.7 jit_solution(1841428720165049912)
XLA Ops:
  9.4 1.5 slice_bitcast_fusion.4
  11.1 1.4 copy-done.22
  14.8 1.8 pad_maximum_fusion
  16.9 1.8 pad_maximum_fusion.1
  22.3 88.1 %spread_all.1 = (f32[8,16,128]{2,1,0:T(8,128)}, bf16[8,192,2048]{2,1,0:T(8,128)(2,1)}, bf16[8,192,1536]{2,1,0:T(8,128)(2,1)}) custom-call(f32[16,128]{1,0:T(8,128)} %fusion.53.refs_0_, bf16[192,2048]{1,0:T(8,128)(2,1)} %get-tuple-element.133.refs_1_, bf16[192,1536]{1,0:T(8,128)(2,1)} %get-tuple-element.135.refs_2_), custom_call_target="tpu_custom_call" | custom-call | flops 1048576 | bytes 157286400 | tf_op jit(solution)/shard_map/spread_all/pallas_call | solution.py:414
  111.4 1.4 fusion.5
  113.4 4.9 convolution_add_fusion.3
  118.5 1.7 copy.44
  121.9 1.8 subtract_convert_fusion.3
  130.9 36.2 %attention_forward.2 = (bf16[256,1536]{1,0:T(8,128)(2,1)}, f32[16,256]{1,0:T(8,128)}, bf16[4,256,512]{2,1,0:T(8,128)(2,1)}) custom-call(bf16[256,1536]{1,0:T(8,128)(2,1)} %copy.55.q_ref, bf16[256,512]{1,0:T(8,128)(2,1)} %pad_maximum_fusion.14.kv_ref, s32[1,256]{1,0:T(1,128)} %bitcast.188, s32[1024,1]{1,0:T(8,128)} %compare_select_fusion.pk_ref), custom_call_target="tpu_custom_call" | custom-call | flops 1610612736 | bytes 16777216 | tf_op jit(solution)/shard_map/attention_forward/pallas_call | solution.py:893
  167.1 4.3 multiply_reduce_fusion.8
  174.2 107.1 %ffn_forward.2 = (bf16[4,256,1536]{2,1,0:T(8,128)(2,1)}, bf16[4,256,2304]{2,1,0:T(8,128)(2,1)}, bf16[4,256,2304]{2,1,0:T(8,128)(2,1)}, f32[256,1536]{1,0:T(8,128...) custom-call(bf16[256,1536]{1,0:T(8,128)(2,1)} %multiply_convert_fusion.2.refs_0_, ...), custom_call_target="tpu_custom_call" | custom-call | flops 21743271936 | bytes 62914560 | tf_op jit(solution)/shard_map/ffn_forward/pallas_call | solution.py:555
  281.3 2.1 multiply_reduce_fusion.7
  284.1 4.8 convolution_add_fusion.2
  289.1 1.7 copy.48
  290.8 1.7 subtract_convert_fusion.2
  294.6 31.8 %attention_forward.3 = (bf16[256,1536]{1,0:T(8,128)(2,1)}, f32[16,256]{1,0:T(8,128)}, bf16[4,256,512]{2,1,0:T(8,128)(2,1)}) custom-call(bf16[256,1536]{1,0:T(8,128)(2,1)} %copy.57.q_ref, bf16[256,512]{1,0:T(8,128)(2,1)} %pad_maximum_fusion.15.kv_ref, s32[1,256]{1,0:T(1,128)} %bitcast.189, s32[1024,1]{1,0:T(8,128)} %compare_select_fusion.pk_ref), custom_call_target="tpu_custom_call" | custom-call | flops 1610612736 | bytes 16777216 | tf_op jit(solution)/shard_map/attention_forward/pallas_call | solution.py:893
  326.4 4.5 multiply_reduce_fusion.6
  333.2 92.4 %ffn_forward.3 = (bf16[4,256,1536]{2,1,0:T(8,128)(2,1)}, bf16[4,256,2304]{2,1,0:T(8,128)(2,1)}, bf16[4,256,2304]{2,1,0:T(8,128)(2,1)}, f32[256,1536]{1,0:T(8,128)}) custom-call(bf16[256,1536]{1,0:T(8,128)(2,1)} %multiply_convert_fusion.refs_0_, bf16[8,3,192,2304]{3,2,1,0:T(8,128)(2,1)} %bitcast.196), custom_call_target="tpu_custom_call" | custom-call | flops 21743271936 | bytes 62914560 | tf_op jit(solution)/shard_map/ffn_forward/pallas_call | solution.py:555
  425.6 116.9 %ffn_backward.2 = (bf16[8,2,192,2304]{3,2,1,0:T(8,128)(2,1)}, bf16[8,192,2304]{2,1,0:T(8,128)(2,1)}, f32[256,1536]{1,0:T(8,128)}) custom-call(bf16[256,1536]{1,0:T(8,128)(2,1)} %fusion.19.g_ref, bf16[8,3,192,2304]{3,2,1,0:T(8,128)(2,1)} %bitcast.197, bf16[4,256,1536]{2,1,0:T(8,128)(2,1)} %get-tuple-element.65.xall_ref, ...), custom_call_target="tpu_custom_call" | custom-call | flops 43486543872 | bytes 104857600 | tf_op jit(solution)/shard_map/ffn_backward/pallas_call | solution.py:733
  547.5 4.0 convolution_convert_fusion.3
  552.5 2.3 convolution_convert_fusion.5.dm_ref
  554.8 67.1 %attention_backward.2 = (f32[256,1536]{1,0:T(8,128)}, f32[256,512]{1,0:T(8,128)}, bf16[192,1536]{1,0:T(8,128)(2,1)}) custom-call(bf16[256,1536]{1,0:T(8,128)(2,1)} %copy.57.q_ref, bf16[4,256,512]{2,1,0:T(8,128)(2,1)} %get-tuple-element.69.kvall_ref, f32[16,256]{1,0:T(8,128)} %get-tuple-element.70.lse_ref, ...), custom_call_target="tpu_custom_call" | custom-call | flops 4026531840 | bytes 16777216 | tf_op jit(solution)/shard_map/attention_backward/pallas_call | solution.py:991
  624.0 1.6 pad_maximum_fusion.2
  625.6 1.7 copy.51
  627.3 1.7 subtract_convert_fusion.1
  630.8 4.6 convolution_convert_fusion.1
  635.5 7.8 multiply_reduce_fusion.2
  643.4 1.9 fusion.62
  645.3 123.0 %ffn_backward.3 = (bf16[8,2,192,2304]{3,2,1,0:T(8,128)(2,1)}, bf16[8,192,2304]{2,1,0:T(8,128)(2,1)}, f32[256,1536]{1,0:T(8,128)}) custom-call(bf16[256,1536]{1,0:T(8,128)(2,1)} %get-tuple-element.106.g_ref, bf16[8,3,192,2304]{3,2,1,0:T(8,128)(2,1)} %bitcast.195, bf16[4,256,1536]{2,1,0:T(8,128)(2,1)} %get-tuple-element.73.xall_ref, ...), custom_call_target="tpu_custom_call" | custom-call | flops 43486543872 | bytes 104857600 | tf_op jit(solution)/shard_map/ffn_backward/pallas_call | solution.py:733
  771.3 2.6 multiply_reduce_fusion.1
  775.1 3.6 convolution_convert_fusion.2
  778.7 2.3 convolution_convert_fusion.4.dm_ref
  781.0 59.0 %attention_backward.3 = (f32[256,1536]{1,0:T(8,128)}, f32[256,512]{1,0:T(8,128)}, bf16[192,1536]{1,0:T(8,128)(2,1)}) custom-call(bf16[256,1536]{1,0:T(8,128)(2,1)} %copy.55.q_ref, bf16[4,256,512]{2,1,0:T(8,128)(2,1)} %get-tuple-element.80.kvall_ref, f32[16,256]{1,0:T(8,128)} %get-tuple-element.81.lse_ref, ...), custom_call_target="tpu_custom_call" | custom-call | flops 4026531840 | bytes 16777216 | tf_op jit(solution)/shard_map/attention_backward/pallas_call | solution.py:991
  842.8 1.8 pad_maximum_fusion.3
  844.6 1.7 copy.53
  846.2 1.7 subtract_convert_fusion
  849.3 6.5 fusion.13
  857.0 4.6 convolution_convert_fusion
  861.6 135.9 %reduce_all.1 = (f32[16,128]{1,0:T(8,128)}, bf16[192,2048]{1,0:T(8,128)(2,1)}, bf16[192,2304]{1,0:T(8,128)(2,1)}, bf16[192,1536]{1,0:T(8,128)(2,1)}, bf16[192,15...) custom-call(f32[8,16,128]{2,1,0:T(8,128)} %bitcast.180, bf16[8,192,2048]{2,1,0:T(8,128)(2,1)} %bitcast.156, ...), custom_call_target="tpu_custom_call" | custom-call | flops 1048576 | bytes 314572800 | tf_op jit(solution)/shard_map/reduce_all/pallas_call | solution.py:1145
  998.9 1.5 fusion.65
  1000.5 1.6 fusion.64
  1006.3 2.0 maximum_convert_fusion.1
  1008.4 2.0 maximum_convert_fusion
  1010.4 1.9 maximum_convert_fusion.3
  1012.3 2.0 maximum_convert_fusion.2
  1014.4 1.6 maximum_convert_fusion.4
  1016.9 1.7 fusion.10
  (264 shorter events, 52.1 us)
Async XLA Ops:
  7.2 167.0 %all-gather.5.cloned.1.call-start = ((), (), s32[]{:S(2)}) async-start(), calls=%async_computation.8 | async-start | bytes 23887872 | tf_op jit(solution)/shard_map/all_gather | solution.py:1226
  16.6 316.6 %all-gather.7.cloned.1.call-start = ((), (), s32[]{:S(2)}) async-start(), calls=%async_computation.9 | async-start | bytes 23887872 | tf_op jit(solution)/shard_map/all_gather | solution.py:1243
  18.7 2.3 copy-start.28
  18.7 752.6 %reduce-scatter.7.cloned.1.call-start = ((), (), s32[]{:S(2)}) async-start(), calls=%async_computation.5 | async-start | bytes 7962624 | tf_op jit(solution)/shard_map/reduce_scatter | solution.py:1278
  111.4 6.9 copy-start.49
  113.4 4.9 copy-start.60
  167.1 4.9 copy-start.18
  167.1 4.9 copy-start.65
  281.3 2.8 copy-start.45
  281.3 2.8 copy-start.67
  283.4 5.4 copy-start.2
  284.1 4.8 copy-start.63
  326.4 5.7 copy-start.47
  542.5 228.8 %reduce-scatter.5.cloned.1.call-start = ((), (), s32[]{:S(2)}) async-start(), calls=%async_computation.4 | async-start | bytes 15925248 | tf_op jit(solution)/shard_map/reduce_scatter | solution.py:1276
  542.6 1.9 copy-start.16
  543.1 299.5 %reduce-scatter.9.cloned.1.call-start = ((), (), s32[]{:S(2)}) async-start(), calls=%async_computation.6 | async-start | bytes 7077888 | tf_op jit(solution)/shard_map/reduce_scatter | solution.py:1301
  546.1 5.3 slice-start.2
  547.5 4.0 copy-start.4
  547.5 5.0 slice-start.3
  624.0 11.5 %copy-start.31 = (bf16[256,256]{0,1:T(8,128)(2,1)}, bf16[256,256]{0,1:T(8,128)(2,1)S(1)}, u32[]{:S(2)}) copy-start(bf16[256,256]{0,1:T(8,128)(2,1)S(1)} %copy.52) | copy-start | bytes 393220
  635.4 7.9 copy-start.5
  635.4 7.9 copy-start.70
  635.4 365.1 %reduce-scatter.11.cloned.1.call-start = ((), (), s32[]{:S(2)}) async-start(), calls=%async_computation.7 | async-start | bytes 15925248 | tf_op jit(solution)/shard_map/reduce_scatter | solution.py:1276
  768.3 2.0 copy-start.13
  768.3 2.0 copy-start.32
  768.3 3.0 copy-start.1
  768.3 3.0 copy-start.44
  768.4 2.9 copy-start.57
  771.3 2.6 copy-start.14
  771.3 2.6 copy-start.15
  771.3 2.6 copy-start.69
  774.0 4.7 slice-start
  775.1 3.6 copy-start.8
  775.1 3.6 slice-start.1
  849.3 6.9 copy-start.53
  849.3 6.9 copy-start.54
  849.3 6.9 copy-start.55
  1008.4 2.0 copy-start.35
  1008.4 2.0 copy-start.36
  1010.4 1.9 copy-start.17
  1012.3 2.0 copy-start.37
  1012.3 2.0 copy-start.38
  1012.3 3.6 copy-start.29
  1014.3 2.3 copy-start.9
  1014.3 2.6 copy-start.11
  1014.3 2.6 copy-start.51
  1014.3 2.6 copy-start.62
  1014.3 2.6 copy-start.72
  (37 other events, 54.4 us)
Sparse Core Ops, SparseCore 0:
  16.7 144.3 all-gather.4
  163.6 145.4 all-gather.6
  542.6 80.8 reduce-scatter.6
  626.9 101.7 reduce-scatter.4
  732.0 61.7 reduce-scatter.8
  797.2 112.7 reduce-scatter.10

commit v5 on v4

--- a/solution.py
+++ b/solution.py
@@ -422,6 +422,100 @@
             flops=1 << 20, transcendentals=0, bytes_accessed=150 << 20),
         name="spread_all",
     )(*shards)
+
+
+class Fold:
+    def __init__(self, cube, src, mine, first, later, load_sem, send1, recv1, send2, recv2):
+        self.cube, self.src = cube, src
+        self.mine, self.first, self.later = mine, first, later
+        self.load_sem, self.send1, self.recv1 = load_sem, send1, recv1
+        self.send2, self.recv2 = send2, recv2
+        self.rows = mine.shape[1]
+        self.half = self.rows // 2
+        self.steps = cube.plan()
+        self.stages = len(cube.chip_bits)
+
+    def _load(self, d):
+        return pltpu.make_async_copy(
+            self.src(self.cube.flip(2 * d)), self.mine.at[d], self.load_sem.at[d])
+
+    def _core(self, d):
+        return pltpu.make_async_remote_copy(
+            src_ref=self.src(self.cube.flip(2 * d | 1)), dst_ref=self.first.at[d],
+            send_sem=self.send1.at[d], recv_sem=self.recv1.at[d],
+            device_id={"fsdp": self.cube.flip(1)}, device_id_type=MESH)
+
+    def _hop(self, half, stage, index):
+        bit, rest, slot = self.steps[half, stage]
+        rows = pl.ds(half * self.half, self.half)
+        return pltpu.make_async_remote_copy(
+            src_ref=self.mine.at[bit | rest[index], rows],
+            dst_ref=self.later.at[half, slot + index],
+            send_sem=self.send2.at[half, slot + index],
+            recv_sem=self.recv2.at[half, slot + index],
+            device_id={"fsdp": self.cube.flip(2 * bit)}, device_id_type=MESH)
+
+    def _hops(self, stage):
+        return [self._hop(half, stage, i)
+                for half in (0, 1) for i in range(len(self.steps[half, stage][1]))]
+
+    def _add(self, d, base, size, other):
+        dtype = self.mine.dtype
+        strip = 48 if size % 48 == 0 else size
+
+        @pl.loop(0, size // strip)
+        def _(i):
+            into = pl.ds(pl.multiple_of(base + i * strip, 8), strip)
+            rows = pl.ds(pl.multiple_of(i * strip, 8), strip)
+            self.mine[d, into] = (
+                self.mine[d, into].astype(F32) + other(rows).astype(F32)).astype(dtype)
+
+    def start(self):
+        for d in range(self.cube.chips):
+            self._core(d).start()
+        for d in range(self.cube.chips):
+            self._load(d).start()
+
+    def phase(self, k):
+        if k == 0:
+            for d in range(self.cube.chips):
+                self._load(d).wait()
+                self._core(d).wait_recv()
+                self._add(d, 0, self.rows, lambda rows, d=d: self.first[d, rows])
+        else:
+            for half in (0, 1):
+                _, rest, slot = self.steps[half, k - 1]
+                for i, e in enumerate(rest):
+                    self._hop(half, k - 1, i).wait_recv()
+                    self._add(e, half * self.half, self.half,
+                              lambda rows, h=half, j=slot + i: self.later[h, j, rows])
+        if k < self.stages:
+            for c in self._hops(k):
+                c.start()
+
+    def finish(self):
+        for d in range(self.cube.chips):
+            self._core(d).wait_send()
+        for stage in range(self.stages):
+            for c in self._hops(stage):
+                c.wait_send()
+
+
+def fold_scratch(owners, rows, width, dtype):
+    chips = owners // 2
+    return [
+        pltpu.VMEM((chips, rows, width), dtype),
+        pltpu.VMEM((chips, rows, width), dtype),
+        pltpu.VMEM((2, chips - 1, rows // 2, width), dtype),
+        pltpu.SemaphoreType.DMA((chips,)),
+        pltpu.SemaphoreType.DMA((chips,)),
+        pltpu.SemaphoreType.DMA((chips,)),
+        pltpu.SemaphoreType.DMA((2, chips - 1)),
+        pltpu.SemaphoreType.DMA((2, chips - 1)),
+    ]
+
+
+FOLD_REFS = 8
 
 
 def ffn_forward_kernel(n, pieces, count, *refs):
@@ -583,10 +677,13 @@
     )(x, w, *following)
 
 
-def ffn_backward_kernel(n, pieces, groups, g_ref, w_ref, xall_ref, gate_ref, up_ref,
-                        dw_ref, dwd_ref, dx_ref,
-                        w_v, gbuf, xv, gate_v, up_v, hid_v, part, from_l, from_r, stage,
-                        w_sem, in_sem, out_sem, *sems):
+def ffn_backward_kernel(n, pieces, groups, count, *refs):
+    g_ref, w_ref, xall_ref, gate_ref, up_ref = refs[:5]
+    later_grads = refs[5:5 + count]
+    dw_ref, dwd_ref, dx_ref = refs[5 + count:8 + count]
+    later_sums = refs[8 + count:8 + 2 * count]
+    (w_v, gbuf, xv, gate_v, up_v, hid_v, part, from_l, from_r, stage,
+     w_sem, in_sem, out_sem, *sems) = refs[8 + 2 * count:]
     line = Line(n)
     z = line.z
     owners, _, shard, width = w_ref.shape
@@ -594,7 +691,20 @@
     tile = lane_tile(width, 256)
     piece = d_model // pieces
     gather = Gather(line, gbuf, *sems[:3])
-    scatter = Scatter(line, pieces, part, from_l, from_r, *sems[3:])
+    scatter = Scatter(line, pieces, part, from_l, from_r, *sems[3:7])
+    folds = []
+    stages = 0
+    if count:
+        cube = Cube(owners)
+        stages = len(cube.chip_bits)
+        for i in range(count):
+            at = 7 + FOLD_REFS * i
+            folds.append(Fold(cube, lambda q, ref=later_grads[i]: ref.at[q],
+                              *sems[at:at + FOLD_REFS]))
+
+    def fold_phase(k):
+        for fold in folds:
+            fold.phase(k)
 
     def w_copy(k, f):
         return pltpu.make_async_copy(
@@ -610,7 +720,10 @@
     def x_load(b):
         return pltpu.make_async_copy(xall_ref.at[b], xv.at[b], in_sem.at[2, b])
 
-    line.barrier()
+    if count:
+        joint_barrier(line, cube)
+    else:
+        line.barrier()
     gather.start(g_ref)
     for f in range(owners):
         w_copy(2, f).start()
@@ -626,6 +739,8 @@
                 c.start()
     for b in range(n):
         x_load(b).start()
+    for fold in folds:
+        fold.start()
     gbuf[z] = g_ref[...]
     for k in (2, 0, 1):
         for f in range(owners):
@@ -668,6 +783,15 @@
 
             scatter.computed(b, p)
 
+        if folds:
+            @pl.when(i == 1)
+            def _():
+                fold_phase(0)
+
+            @pl.when(i == n - 1)
+            def _():
+                fold_phase(1)
+
     def add_own(p, value):
         cols = slice(p * piece, (p + 1) * piece)
         dx_ref[:, cols] = dx_ref[:, cols] + value
@@ -711,34 +835,48 @@
     units = 3 * groups
     steps = list(scatter.steps())
     done = 0
+    passed = 2
     for index, t in enumerate(steps):
         scatter.step(t, add_own)
         until = units * (index + 1) // len(steps)
         while done < until:
             weight_unit(done)
             done += 1
+        if t >= 4 and t % 2 == 0 and passed <= stages:
+            fold_phase(passed)
+            passed += 1
+    for k in range(passed, stages + 1):
+        fold_phase(k)
+    for fold, ref in zip(folds, later_sums):
+        ref[...] = fold.mine[0]
     for unit in range(units - 2, units):
         for c in dw_copies(unit // groups, unit % groups, unit % 2):
             c.wait()
     gather.finish()
     scatter.finish()
-
-
-def ffn_backward(g, w, xall, gate, up, n):
+    for fold in folds:
+        fold.finish()
+
+
+def ffn_backward(g, w, xall, gate, up, n, later=()):
     rows, d_model = g.shape
     owners, _, shard, width = w.shape
     pieces, groups = 3, 4
     piece = d_model // pieces
     per = d_model // groups // shard
+    count = len(later)
+    fold_refs = []
+    for m in later:
+        fold_refs += fold_scratch(owners, m.shape[1], m.shape[2], BF)
     return pl.pallas_call(
-        functools.partial(ffn_backward_kernel, n, pieces, groups),
+        functools.partial(ffn_backward_kernel, n, pieces, groups, count),
         out_shape=(
             jax.ShapeDtypeStruct((owners, 2, shard, width), BF),
             jax.ShapeDtypeStruct((owners, shard, width), BF),
             jax.ShapeDtypeStruct((rows, d_model), F32),
-        ),
-        in_specs=[VM, ANY, ANY, ANY, ANY],
-        out_specs=[ANY, ANY, VM],
+        ) + tuple(jax.ShapeDtypeStruct(m.shape[1:], BF) for m in later),
+        in_specs=[VM, ANY, ANY, ANY, ANY] + [ANY] * count,
+        out_specs=[ANY, ANY, VM] + [VM] * count,
         scratch_shapes=[
             pltpu.VMEM((3, d_model, width), BF),
             pltpu.VMEM((n, rows, d_model), BF),
@@ -753,118 +891,27 @@
             pltpu.SemaphoreType.DMA((3, owners)),
             pltpu.SemaphoreType.DMA((3, n)),
             pltpu.SemaphoreType.DMA((2, per)),
-        ] + gather_sems(n) + scatter_sems(n, pieces),
-        compiler_params=params(2),
+        ] + gather_sems(n) + scatter_sems(n, pieces) + fold_refs,
+        compiler_params=params(8 if count else 2),
         cost_estimate=pl.CostEstimate(
             flops=12 * n * rows * d_model * width, transcendentals=n * rows * width,
             bytes_accessed=100 << 20),
         name="ffn_backward",
-    )(g, w, xall, gate, up)
-
-
-class Fold:
-    def __init__(self, cube, src, mine, first, later, load_sem, send1, recv1, send2, recv2):
-        self.cube, self.src = cube, src
-        self.mine, self.first, self.later = mine, first, later
-        self.load_sem, self.send1, self.recv1 = load_sem, send1, recv1
-        self.send2, self.recv2 = send2, recv2
-        self.rows = mine.shape[1]
-        self.half = self.rows // 2
-        self.steps = cube.plan()
-        self.stages = len(cube.chip_bits)
-
-    def _load(self, d):
-        return pltpu.make_async_copy(
-            self.src(self.cube.flip(2 * d)), self.mine.at[d], self.load_sem.at[d])
-
-    def _core(self, d):
-        return pltpu.make_async_remote_copy(
-            src_ref=self.src(self.cube.flip(2 * d | 1)), dst_ref=self.first.at[d],
-            send_sem=self.send1.at[d], recv_sem=self.recv1.at[d],
-            device_id={"fsdp": self.cube.flip(1)}, device_id_type=MESH)
-
-    def _hop(self, half, stage, index):
-        bit, rest, slot = self.steps[half, stage]
-        rows = pl.ds(half * self.half, self.half)
-        return pltpu.make_async_remote_copy(
-            src_ref=self.mine.at[bit | rest[index], rows],
-            dst_ref=self.later.at[half, slot + index],
-            send_sem=self.send2.at[half, slot + index],
-            recv_sem=self.recv2.at[half, slot + index],
-            device_id={"fsdp": self.cube.flip(2 * bit)}, device_id_type=MESH)
-
-    def _hops(self, stage):
-        return [self._hop(half, stage, i)
-                for half in (0, 1) for i in range(len(self.steps[half, stage][1]))]
-
-    def _add(self, d, base, size, other):
-        dtype = self.mine.dtype
-        strip = 48 if size % 48 == 0 else size
-
-        @pl.loop(0, size // strip)
-        def _(i):
-            into = pl.ds(pl.multiple_of(base + i * strip, 8), strip)
-            rows = pl.ds(pl.multiple_of(i * strip, 8), strip)
-            self.mine[d, into] = (
-                self.mine[d, into].astype(F32) + other(rows).astype(F32)).astype(dtype)
-
-    def start(self):
-        for d in range(self.cube.chips):
-            self._core(d).start()
-        for d in range(self.cube.chips):
-            self._load(d).start()
-
-    def phase(self, k):
-        if k == 0:
-            for d in range(self.cube.chips):
-                self._load(d).wait()
-                self._core(d).wait_recv()
-                self._add(d, 0, self.rows, lambda rows, d=d: self.first[d, rows])
-        else:
-            for half in (0, 1):
-                _, rest, slot = self.steps[half, k - 1]
-                for i, e in enumerate(rest):
-                    self._hop(half, k - 1, i).wait_recv()
-                    self._add(e, half * self.half, self.half,
-                              lambda rows, h=half, j=slot + i: self.later[h, j, rows])
-        if k < self.stages:
-            for c in self._hops(k):
-                c.start()
-
-    def finish(self):
-        for d in range(self.cube.chips):
-            self._core(d).wait_send()
-        for stage in range(self.stages):
-            for c in self._hops(stage):
-                c.wait_send()
-
-
-def fold_scratch(owners, rows, width, dtype):
-    chips = owners // 2
-    return [
-        pltpu.VMEM((chips, rows, width), dtype),
-        pltpu.VMEM((chips, rows, width), dtype),
-        pltpu.VMEM((2, chips - 1, rows // 2, width), dtype),
-        pltpu.SemaphoreType.DMA((chips,)),
-        pltpu.SemaphoreType.DMA((chips,)),
-        pltpu.SemaphoreType.DMA((chips,)),
-        pltpu.SemaphoreType.DMA((2, chips - 1)),
-        pltpu.SemaphoreType.DMA((2, chips - 1)),
-    ]
-
-
-FOLD_REFS = 8
-
-
-def attention_forward_kernel(n, q_ref, kv_ref, pq_ref, pk_ref, mixed_ref, lse_ref, kvall_ref,
-                             kvbuf, vt, *sems):
+    )(g, w, xall, gate, up, *later)
+
+
+def attention_forward_kernel(n, owners, q_ref, kv_ref, pq_ref, pk_ref, w_ref,
+                             mixed_ref, lse_ref, kvall_ref, full_ref, kvbuf, vt, *sems):
     line = Line(n)
+    cube = Cube(owners)
+    spread = Spread(cube, w_ref, full_ref, *sems[3:])
     z = line.z
     rows = q_ref.shape[0]
     total = n * rows
-    gather = Gather(line, kvbuf, *sems)
-    line.barrier()
+    gather = Gather(line, kvbuf, *sems[:3])
+    joint_barrier(line, cube)
     gather.start(kv_ref)
+    spread.start()
     kvbuf[z] = kv_ref[...]
     for i in range(1, n):
         gather.arrive(line.order(i))
@@ -885,46 +932,46 @@
             o = dot_nn(vt[g], e.astype(BF)) / den
             mixed_ref[:, h * HEAD:(h + 1) * HEAD] = o.T.astype(BF)
             lse_ref[h:h + 1, :] = top + jnp.log(den)
+            if h == 5:
+                spread.phase(1)
+    for k in range(2, spread.stages + 1):
+        spread.phase(k)
+    spread.finish()
     gather.finish()
 
 
-def attention_forward(q, kv, pos_q, pos_k, n):
+def attention_forward(q, kv, pos_q, pos_k, w_out, n, owners):
     rows = q.shape[0]
     return pl.pallas_call(
-        functools.partial(attention_forward_kernel, n),
+        functools.partial(attention_forward_kernel, n, owners),
         out_shape=(
             jax.ShapeDtypeStruct((rows, Q_WIDTH), BF),
             jax.ShapeDtypeStruct((16, rows), F32),
             jax.ShapeDtypeStruct((n, rows, 2 * KV_WIDTH), BF),
-        ),
-        in_specs=[VM] * 4,
-        out_specs=[VM] * 3,
+        ) + spread_shapes(owners, (w_out,)),
+        in_specs=[VM] * 5,
+        out_specs=[VM] * 3 + [ANY],
         scratch_shapes=[
             pltpu.VMEM((n, rows, 2 * KV_WIDTH), BF),
             pltpu.VMEM((KV_HEADS, HEAD, n * rows), BF),
-        ] + gather_sems(n),
+        ] + gather_sems(n) + spread_sems(owners),
         compiler_params=params(3),
         cost_estimate=pl.CostEstimate(
             flops=4 * n * rows * rows * Q_WIDTH, transcendentals=n * rows * rows * QUERY_HEADS,
             bytes_accessed=16 << 20),
         name="attention_forward",
-    )(q, kv, pos_q, pos_k)
-
-
-def attention_backward_kernel(n, owners, q_ref, kvall_ref, lse_ref, dm_ref, pq_ref, pk_ref,
-                              grad_ref, dq_ref, dkv_ref, sum_ref,
-                              kt, dk_acc, dv_acc, part, from_l, from_r, *refs):
-    fold_refs, sems = refs[:FOLD_REFS], refs[FOLD_REFS:]
+    )(q, kv, pos_q, pos_k, w_out)
+
+
+def attention_backward_kernel(n, q_ref, kvall_ref, lse_ref, dm_ref, pq_ref, pk_ref,
+                              dq_ref, dkv_ref, kt, dk_acc, dv_acc, part, from_l, from_r, *sems):
     line = Line(n)
-    cube = Cube(owners)
-    fold = Fold(cube, lambda q: grad_ref.at[q], *fold_refs)
     z = line.z
     rows = q_ref.shape[0]
     total = n * rows
     pieces = KV_HEADS
     scatter = Scatter(line, pieces, part, from_l, from_r, *sems)
-    joint_barrier(line, cube)
-    fold.start()
+    line.barrier()
     allowed = pk_ref[...] <= pq_ref[...]
     for g in range(KV_HEADS):
         k = kvall_ref[:, :, g * HEAD:(g + 1) * HEAD].reshape(total, HEAD)
@@ -951,10 +998,6 @@
                 dk_acc[...] += dk
                 dv_acc[...] += dv
             dq_ref[:, cols] = dot_nn(kt[g], ds).T
-            if h == 1:
-                fold.phase(0)
-            if h == 8:
-                fold.phase(1)
         for b in range(n):
             sl = slice(b * rows, (b + 1) * rows)
 
@@ -978,44 +1021,37 @@
 
     for t in scatter.steps():
         scatter.step(t, add_own)
-    for k in range(2, fold.stages + 1):
-        fold.phase(k)
-    sum_ref[...] = fold.mine[0]
     scatter.finish()
-    fold.finish()
-
-
-def attention_backward(q, kvall, lse, dm, pos_q, pos_k, grad, n):
+
+
+def attention_backward(q, kvall, lse, dm, pos_q, pos_k, n):
     rows = q.shape[0]
-    owners, shard, d_model = grad.shape
     return pl.pallas_call(
-        functools.partial(attention_backward_kernel, n, owners),
+        functools.partial(attention_backward_kernel, n),
         out_shape=(
             jax.ShapeDtypeStruct((rows, Q_WIDTH), F32),
             jax.ShapeDtypeStruct((rows, 2 * KV_WIDTH), F32),
-            jax.ShapeDtypeStruct((shard, d_model), BF),
         ),
-        in_specs=[VM] * 6 + [ANY],
-        out_specs=[VM] * 3,
+        in_specs=[VM] * 6,
+        out_specs=[VM] * 2,
         scratch_shapes=[
             pltpu.VMEM((KV_HEADS, HEAD, n * rows), BF),
             pltpu.VMEM((n * rows, HEAD), F32),
             pltpu.VMEM((n * rows, HEAD), F32),
-        ] + [pltpu.VMEM((n, KV_HEADS, rows, 2 * HEAD), BF)] * 3
-        + fold_scratch(owners, shard, d_model, BF) + scatter_sems(n, KV_HEADS),
+        ] + [pltpu.VMEM((n, KV_HEADS, rows, 2 * HEAD), BF)] * 3 + scatter_sems(n, KV_HEADS),
         compiler_params=params(4),
         cost_estimate=pl.CostEstimate(
             flops=10 * n * rows * rows * Q_WIDTH, transcendentals=n * rows * rows * QUERY_HEADS,
             bytes_accessed=16 << 20),
         name="attention_backward",
-    )(q, kvall, lse, dm, pos_q, pos_k, grad)
-
-
-def reduce_kernel(n, owners, count, small_ref, qkv_ref, dw_ref, *refs):
+    )(q, kvall, lse, dm, pos_q, pos_k)
+
+
+def reduce_kernel(n, owners, count, small_ref, out_ref, qkv_ref, dw_ref, *refs):
     early = refs[:count]
-    small_o, qkv_o, dw_o = refs[count:count + 3]
-    targets = (qkv_o,) + refs[count + 3:2 * count + 3]
-    refs = refs[2 * count + 3:]
+    small_o, out_o, qkv_o, dw_o = refs[count:count + 4]
+    targets = (out_o, qkv_o) + refs[count + 4:2 * count + 4]
+    refs = refs[2 * count + 4:]
     line = Line(n)
     cube = Cube(owners)
     refs = list(refs)
@@ -1027,6 +1063,7 @@
 
     sources = [
         lambda q: small_ref.at[q],
+        lambda q: out_ref.at[q],
         lambda q: qkv_ref.at[q],
         lambda q: dw_ref.at[q],
     ]
@@ -1094,9 +1131,9 @@
     for f in folds:
         f.start()
     for i, ref in enumerate(early):
-        share(1 + i, lambda rows, ref=ref: ref[rows])
+        share(2 + i, lambda rows, ref=ref: ref[rows])
     last = folds[0].stages
-    jobs = line_jobs(range(1, 1 + count))
+    jobs = line_jobs(range(2, 2 + count))
 
     def after(index):
         fold = folds[index]
@@ -1104,9 +1141,9 @@
             small_all[line.z] = fold.mine[0]
             gather_small.start(small_all.at[line.z])
             jobs.append(small_job)
-        elif index == 1:
-            share(0, lambda rows: fold.mine[0, rows])
-            jobs.extend(line_jobs((0,)))
+        elif index <= 2:
+            share(index - 1, lambda rows: fold.mine[0, rows])
+            jobs.extend(line_jobs((index - 1,)))
         else:
             pltpu.make_async_copy(fold.mine.at[0], dw_o, write_sem).start()
 
@@ -1116,12 +1153,12 @@
                 folds[t - k].phase(k)
                 if k == last:
                     after(t - k)
-                for _ in range(3):
+                for _ in range(2):
                     if jobs and t >= 1:
                         jobs.pop(0)()
     for job in jobs:
         job()
-    pltpu.make_async_copy(folds[2].mine.at[0], dw_o, write_sem).wait()
+    pltpu.make_async_copy(folds[3].mine.at[0], dw_o, write_sem).wait()
     for f in folds:
         f.finish()
     gather_small.finish()
@@ -1130,14 +1167,16 @@
         gather.finish()
 
 
-def reduce_all(small, qkv_g, dw, early, n):
+def reduce_all(small, out_g, qkv_g, dw, early, n):
     owners, shard, qkv_width = qkv_g.shape
+    d_model = out_g.shape[2]
     width = dw.shape[2]
     scratch = fold_scratch(owners, small.shape[1], 128, F32)
+    scratch += fold_scratch(owners, shard, d_model, BF)
     scratch += fold_scratch(owners, shard, qkv_width, BF)
     scratch += fold_scratch(owners, shard, width, BF)
     scratch += [pltpu.VMEM((n, small.shape[1], 128), F32)] + gather_sems(n)
-    for w in [qkv_width] + [m.shape[1] for m in early]:
+    for w in [d_model, qkv_width] + [m.shape[1] for m in early]:
         scratch += [pltpu.VMEM((n, 1, shard // n, w), BF)] * 3
         scratch += [pltpu.VMEM((n, shard // n, w), BF), pltpu.VMEM((shard // n, w), F32)]
         scratch += scatter_sems(n, 1) + gather_sems(n)
@@ -1146,17 +1185,18 @@
         functools.partial(reduce_kernel, n, owners, len(early)),
         out_shape=(
             jax.ShapeDtypeStruct(small.shape[1:], F32),
+            jax.ShapeDtypeStruct((shard, d_model), BF),
             jax.ShapeDtypeStruct((shard, qkv_width), BF),
             jax.ShapeDtypeStruct((shard, width), BF),
         ) + tuple(jax.ShapeDtypeStruct(m.shape, BF) for m in early),
-        in_specs=[ANY] * 3 + [VM] * len(early),
-        out_specs=[VM, VM, ANY] + [VM] * len(early),
+        in_specs=[ANY] * 4 + [VM] * len(early),
+        out_specs=[VM, VM, VM, ANY] + [VM] * len(early),
         scratch_shapes=scratch,
         compiler_params=params(5),
         cost_estimate=pl.CostEstimate(
             flops=1 << 20, transcendentals=0, bytes_accessed=300 << 20),
         name="reduce_all",
-    )(small, qkv_g, dw, *early)
+    )(small, out_g, qkv_g, dw, *early)
 
 
 def normalize(stream, gain):
@@ -1224,9 +1264,8 @@
     first_ffn = ffn_shard(0)
     first_ffn, small = lax.optimization_barrier((first_ffn, small))
     ffn_weights = [lax.all_gather(first_ffn, "fsdp", axis=0, tiled=False)]
-    small, qkv_w, out_w = spread_all(owners, small, w_qkv[0], w_out[0])
+    small, qkv_w = spread_all(owners, small, w_qkv[0])
     qkv_weights = [qkv_w.reshape(d_model, -1)]
-    out_weights = [out_w.reshape(Q_WIDTH, d_model)]
     small = small.reshape(owners, -1)
     gains_attn, gains_mlp, biases = [], [], []
     for l in range(LAYERS):
@@ -1238,7 +1277,7 @@
     stream = hidden_in[0].astype(F32)
     kept = []
     for l in range(LAYERS):
-        qkv_w, out_w, ffn_w = qkv_weights[l], out_weights[l], ffn_weights[l]
+        qkv_w, ffn_w = qkv_weights[l], ffn_weights[l]
         if l + 1 < LAYERS:
             ffn_weights.append(lax.all_gather(ffn_shard(l + 1), "fsdp", axis=0, tiled=False))
         normed = normalize(stream, gains_attn[l]).astype(BF)
@@ -1248,14 +1287,13 @@
             cosine, sine).astype(BF).reshape(rows, Q_WIDTH + KV_WIDTH)
         q = qk[:, :Q_WIDTH]
         kv = jnp.concatenate([qk[:, Q_WIDTH:], projected[:, Q_WIDTH + KV_WIDTH:].astype(BF)], axis=1)
-        mixed, lse, kvall = attention_forward(q, kv, pos_q, pos_k, n)
+        mixed, lse, kvall, out_w = attention_forward(q, kv, pos_q, pos_k, w_out[l], n, owners)
+        out_w = out_w.reshape(Q_WIDTH, d_model)
         middle = stream + jnp.dot(mixed, out_w, preferred_element_type=F32)
         normed_two = normalize(middle, gains_mlp[l]).astype(BF)
         if l + 1 < LAYERS:
-            xall, gate, up, y, next_qkv, next_out = ffn_forward(
-                normed_two, ffn_w, n, (w_qkv[l + 1], w_out[l + 1]))
+            xall, gate, up, y, next_qkv = ffn_forward(normed_two, ffn_w, n, (w_qkv[l + 1],))
             qkv_weights.append(next_qkv.reshape(d_model, -1))
-            out_weights.append(next_out.reshape(Q_WIDTH, d_model))
         else:
             xall, gate, up, y = ffn_forward(normed_two, ffn_w, n)
         kept.append((stream, normed, q, kvall, lse, mixed, middle, xall, gate, up,
@@ -1269,8 +1307,11 @@
     for l in reversed(range(LAYERS)):
         (stream, normed, q, kvall, lse, mixed, middle, xall, gate, up,
          qkv_w, out_w, ffn_w) = kept[l]
-        dw, dw_down, dx = ffn_backward(gradient.astype(BF), ffn_w, xall, gate, up, n)
+        later = (out_grad.reshape(owners, shard, d_model),) if l < LAYERS - 1 else ()
+        dw, dw_down, dx, *later_sums = ffn_backward(
+            gradient.astype(BF), ffn_w, xall, gate, up, n, later)
         if l < LAYERS - 1:
+            out_sums[l + 1], = later_sums
             dx, ffn_sums[l + 1], down_sums[l + 1] = lax.optimization_barrier(
                 (dx, ffn_sums[l + 1], down_sums[l + 1]))
         ffn_sums[l] = lax.psum_scatter(dw, "fsdp", scatter_dimension=0, tiled=False)
@@ -1281,8 +1322,7 @@
         d_low = d_middle.astype(BF)
         d_mixed = jnp.einsum("td,cd->tc", d_low, out_w, preferred_element_type=F32).astype(BF)
         out_grad = jnp.einsum("tc,td->cd", mixed, d_low, preferred_element_type=F32).astype(BF)
-        dq, dkv, out_sums[l] = attention_backward(
-            q, kvall, lse, d_mixed, pos_q, pos_k, out_grad.reshape(owners, shard, d_model), n)
+        dq, dkv = attention_backward(q, kvall, lse, d_mixed, pos_q, pos_k, n)
         if l < LAYERS - 1:
             dq, qkv_sums[l + 1] = lax.optimization_barrier((dq, qkv_sums[l + 1]))
         d_qk = rotate(
@@ -1302,10 +1342,11 @@
     small = packed([
         m.reshape(owners, -1)
         for k in range(3) for m in (small_grads[i][k] for i in range(LAYERS))], (owners,))
-    small, qkv_sums[0], down_sums[0], *early = reduce_all(
-        small, qkv_grad.reshape(owners, shard, qkv_grad.shape[1]), dw_down,
-        out_sums + qkv_sums[1:], n)
-    out_sums, qkv_sums = early[:LAYERS], qkv_sums[:1] + early[LAYERS:]
+    small, out_sums[0], qkv_sums[0], down_sums[0], *early = reduce_all(
+        small, out_grad.reshape(owners, shard, d_model),
+        qkv_grad.reshape(owners, shard, qkv_grad.shape[1]), dw_down,
+        out_sums[1:] + qkv_sums[1:], n)
+    out_sums[1:], qkv_sums[1:] = early[:LAYERS - 1], early[LAYERS - 1:]
     small = small.reshape(-1)
 
     grad_norm_attn = small[:LAYERS * shard].reshape(LAYERS, shard)

time: 1030 us -> 1060 us (1.029)
  Pallas kernels: 857 us -> 872 us
    pallas_call x1, Pallas kernels: 136 us -> 184 us  [reduce_all(): pl.pallas_call(functools.partial(reduce_kernel, n, owners, len(early)), o...]
    pallas_call x1, Pallas kernels: 88.1 us -> 57.2 us  [spread_all(): pl.pallas_call(functools.partial(spread_kernel, owners, count), out_shape...]
    pallas_call x6, Pallas kernels: 434 us -> 416 us  [the longest x2 248 us: ffn_backward(): pl.pallas_call(functools.partial(ffn_backward_kernel, n, pieces, groups,...]
    pallas_call x2, Pallas kernels: 199 us -> 215 us  [ffn_forward(): pl.pallas_call(functools.partial(ffn_forward_kernel, n, pieces, count), o...]
  transfers between devices with their start and end apart: 6 -> 6, of which waited for: 0 -> 1; matrix products, arithmetic and copies ran while one was open for 11% -> 11% of each run, Pallas kernels for 63% -> 61%
where the time goes in v5:
time: 1060 us; the launch traced here: 1050 us
  Pallas kernels  872 us (82%)
  matrix products  57.2 us (5%)
  local copies, waits for them, and re-layouts  48.8 us (5%)
  other arithmetic  48.7 us (5%)
  between operations  15.9 us (2%)
    pallas_call x2, Pallas kernels, ffn_backward(): pl.pallas_call(functools.partial(ffn_backward_kernel, n, pieces, groups,...  248 us
    pallas_call x2, Pallas kernels, ffn_forward(): pl.pallas_call(functools.partial(ffn_forward_kernel, n, pieces, count), o...  215 us
    pallas_call x1, Pallas kernels, reduce_all(): pl.pallas_call(functools.partial(reduce_kernel, n, owners, len(early)), o...  184 us
    pallas_call x2, Pallas kernels, attention_forward(): pl.pallas_call(functools.partial(attention_forward_kernel, n, owners), ou...  89.1 us
    pallas_call x2, Pallas kernels, attention_backward(): pl.pallas_call(functools.partial(attention_backward_kernel, n), out_shape...  79.1 us
    pallas_call x1, Pallas kernels, spread_all(): pl.pallas_call(functools.partial(spread_kernel, owners, count), out_shape...  57.2 us
  transfers between devices with their start and end apart: 6, of which 1 were waited for; matrix products, arithmetic and copies ran while one was open for 11% of the time, Pallas kernels for 61%

profile of v5, /device:TPU:0, one launch (start us, length us, event | category | flops | bytes accessed | tf_op | source)
XLA Modules:
  0.0 1054.1 jit_solution(660615892443294818)
XLA Ops:
  9.4 1.5 slice_bitcast_fusion.4
  11.1 1.4 copy-done.22
  14.8 1.8 pad_maximum_fusion
  16.9 1.8 pad_maximum_fusion.1
  21.3 57.2 %spread_all.1 = (f32[8,16,128]{2,1,0:T(8,128)}, bf16[8,192,2048]{2,1,0:T(8,128)(2,1)}) custom-call(f32[16,128]{1,0:T(8,128)} %fusion.53.refs_0_, bf16[192,2048]{1,0:T(8,128)(2,1)} %get-tuple-element.131.refs_1_), custom_call_target="tpu_custom_call" | custom-call | flops 1048576 | bytes 157286400 | tf_op jit(solution)/shard_map/spread_all/pallas_call | solution.py:414
  81.5 4.9 convolution_add_fusion.3
  86.6 1.7 copy.44
  90.0 2.3 subtract_convert_fusion.3
  100.6 50.1 %attention_forward.2 = (bf16[256,1536]{1,0:T(8,128)(2,1)}, f32[16,256]{1,0:T(8,128)}, bf16[4,256,512]{2,1,0:T(8,128)(2,1)}, bf16[8,192,1536]{2,1,0:T(8,128)(2,1)}) custom-call(bf16[256,1536]{1,0:T(8,128)(2,1)} %copy.55.q_ref, bf16[256,512]{1,0:T(8,128)(2,1)} %pad_maximum_fusion.14.kv_ref, s32[1,256]{1,0:T(1,128)} %bitcast.188, ...), custom_call_target="tpu_custom_call" | custom-call | flops 1610612736 | bytes 16777216 | tf_op jit(solution)/shard_map/attention_forward/pallas_call | solution.py:945
  150.7 4.7 multiply_reduce_fusion.8
  158.1 9.8 all-gather.5.cloned.1.call-done
  167.9 108.6 %ffn_forward.2 = (bf16[4,256,1536]{2,1,0:T(8,128)(2,1)}, bf16[4,256,2304]{2,1,0:T(8,128)(2,1)}, bf16[4,256,2304]{2,1,0:T(8,128)(2,1)}, f32[256,1536]{1,0:T(8,128)}, bf16[8,192,2048]{2,1,0:T(8,128)(2,1)}) custom-call(bf16[256,1536]{1,0:T(8,128)(2,1)} %multiply_convert_fusion.2.refs_0_, bf16[8,3,192,2304]{3,2,1,0:T(8,128)(2,1)} %bitcast.194, ...), custom_call_target="tpu_custom_call" | custom-call | flops 21743271936 | bytes 62914560 | tf_op jit(solution)/shard_map/ffn_forward/pallas_call | solution.py:649
  276.6 2.5 multiply_reduce_fusion.7
  279.7 4.7 convolution_add_fusion.2
  284.5 1.7 copy.48
  286.2 1.7 subtract_convert_fusion.2
  290.1 39.1 %attention_forward.3 = (bf16[256,1536]{1,0:T(8,128)(2,1)}, f32[16,256]{1,0:T(8,128)}, bf16[4,256,512]{2,1,0:T(8,128)(2,1)}, bf16[8,192,1536]{2,1,0:T(8,128)(2,1)}) custom-call(bf16[256,1536]{1,0:T(8,128)(2,1)} %copy.57.q_ref, bf16[256,512]{1,0:T(8,128)(2,1)} %pad_maximum_fusion.15.kv_ref, s32[1,256]{1,0:T(1,128)} %bitcast.189, ...), custom_call_target="tpu_custom_call" | custom-call | flops 1610612736 | bytes 16777216 | tf_op jit(solution)/shard_map/attention_forward/pallas_call | solution.py:945
  329.2 4.5 multiply_reduce_fusion.6
  336.0 106.6 %ffn_forward.3 = (bf16[4,256,1536]{2,1,0:T(8,128)(2,1)}, bf16[4,256,2304]{2,1,0:T(8,128)(2,1)}, bf16[4,256,2304]{2,1,0:T(8,128)(2,1)}, f32[256,1536]{1,0:T(8,128)}) custom-call(bf16[256,1536]{1,0:T(8,128)(2,1)} %multiply_convert_fusion.refs_0_, bf16[8,3,192,2304]{3,2,1,0:T(8,128)(2,1)} %bitcast.196), custom_call_target="tpu_custom_call" | custom-call | flops 21743271936 | bytes 62914560 | tf_op jit(solution)/shard_map/ffn_forward/pallas_call | solution.py:649
  442.7 119.1 %ffn_backward.2 = (bf16[8,2,192,2304]{3,2,1,0:T(8,128)(2,1)}, bf16[8,192,2304]{2,1,0:T(8,128)(2,1)}, f32[256,1536]{1,0:T(8,128)}) custom-call(bf16[256,1536]{1,0:T(8,128)(2,1)} %fusion.19.refs_0_, bf16[8,3,192,2304]{3,2,1,0:T(8,128)(2,1)} %bitcast.197, bf16[4,256,1536]{2,1,0:T(8,128)(2,1)} %get-tuple-element.64.refs_2_, ...), custom_call_target="tpu_custom_call" | custom-call | flops 43486543872 | bytes 104857600 | tf_op jit(solution)/shard_map/ffn_backward/pallas_call | solution.py:871
  567.7 2.3 convolution_convert_fusion.5.dm_ref
  570.0 38.6 %attention_backward.2 = (f32[256,1536]{1,0:T(8,128)}, f32[256,512]{1,0:T(8,128)}) custom-call(bf16[256,1536]{1,0:T(8,128)(2,1)} %copy.57.q_ref, bf16[4,256,512]{2,1,0:T(8,128)(2,1)} %get-tuple-element.68.kvall_ref, f32[16,256]{1,0:T(8,128)} %get-tuple-element.69.lse_ref, bf16[256,1536]{1,0:T(8,128)(2,1)} %convolution_convert_fusion.5.dm_ref, ...), custom_call_target="tpu_custom_call" | custom-call | flops 4026531840 | bytes 16777216 | tf_op jit(solution)/shard_map/attention_backward/pallas_call | solution.py:1029
  610.7 1.6 pad_maximum_fusion.2
  612.3 1.7 copy.51
  614.0 1.7 subtract_convert_fusion.1
  617.5 4.6 convolution_convert_fusion.1
  622.6 5.9 multiply_reduce_fusion.2
  628.6 3.6 convolution_convert_fusion.3
  632.2 1.9 fusion.62
  634.1 128.6 %ffn_backward.3 = (bf16[8,2,192,2304]{3,2,1,0:T(8,128)(2,1)}, bf16[8,192,2304]{2,1,0:T(8,128)(2,1)}, f32[256,1536]{1,0:T(8,128)}, bf16[192,1536]{1,0:T(8,128)(2,1)}) custom-call(bf16[256,1536]{1,0:T(8,128)(2,1)} %get-tuple-element.104.refs_0_, bf16[8,3,192,2304]{3,2,1,0:T(8,128)(2,1)} %bitcast.195, bf16[4,256,1536]{2,1,0:T(8,128)(2,1)} %get-tuple-element.72.refs_2_, ...), custom_call_target="tpu_custom_call" | custom-call | flops 43486543872 | bytes 104857600 | tf_op jit(solution)/shard_map/ffn_backward/pallas_call | solution.py:871
  765.7 2.7 multiply_reduce_fusion.1
  769.0 5.2 convolution_convert_fusion.4.dm_ref
  774.2 40.4 %attention_backward.3 = (f32[256,1536]{1,0:T(8,128)}, f32[256,512]{1,0:T(8,128)}) custom-call(bf16[256,1536]{1,0:T(8,128)(2,1)} %copy.55.q_ref, bf16[4,256,512]{2,1,0:T(8,128)(2,1)} %get-tuple-element.79.kvall_ref, f32[16,256]{1,0:T(8,128)} %get-tuple-element.80.lse_ref, bf16[256,1536]{1,0:T(8,128)(2,1)} %convolution_convert_fusion.4.dm_ref, ...), custom_call_target="tpu_custom_call" | custom-call | flops 4026531840 | bytes 16777216 | tf_op jit(solution)/shard_map/attention_backward/pallas_call | solution.py:1029
  817.5 1.5 pad_maximum_fusion.3
  819.1 1.7 copy.53
  820.8 1.7 subtract_convert_fusion
  823.9 6.7 fusion.13
  831.9 5.5 convolution_convert_fusion.2
  837.4 4.6 convolution_convert_fusion
  842.0 183.9 %reduce_all.1 = (f32[16,128]{1,0:T(8,128)}, bf16[192,1536]{1,0:T(8,128)(2,1)}, bf16[192,2048]{1,0:T(8,128)(2,1)}, bf16[192,2304]{1,0:T(8,128)(2,1)}, bf16[192,15...) custom-call(f32[8,16,128]{2,1,0:T(8,128)} %bitcast.180, bf16[8,192,1536]{2,1,0:T(8,128)(2,1)} %bitcast.157, ...), custom_call_target="tpu_custom_call" | custom-call | flops 1048576 | bytes 314572800 | tf_op jit(solution)/shard_map/reduce_all/pallas_call | solution.py:1184
  1027.4 1.5 fusion.65
  1029.0 1.6 fusion.64
  1034.8 2.0 maximum_convert_fusion.1
  1036.8 2.0 maximum_convert_fusion
  1038.8 1.9 maximum_convert_fusion.3
  1040.7 2.0 maximum_convert_fusion.2
  1042.8 1.6 maximum_convert_fusion.4
  1045.4 1.7 fusion.10
  (259 shorter events, 53.5 us)
Async XLA Ops:
  7.2 160.7 %all-gather.5.cloned.1.call-start = ((), (), s32[]{:S(2)}) async-start(), calls=%async_computation.8 | async-start | bytes 23887872 | tf_op jit(solution)/shard_map/all_gather | solution.py:1266
  16.6 319.4 %all-gather.7.cloned.1.call-start = ((), (), s32[]{:S(2)}) async-start(), calls=%async_computation.9 | async-start | bytes 23887872 | tf_op jit(solution)/shard_map/all_gather | solution.py:1282
  18.7 747.0 %reduce-scatter.7.cloned.1.call-start = ((), (), s32[]{:S(2)}) async-start(), calls=%async_computation.5 | async-start | bytes 7962624 | tf_op jit(solution)/shard_map/reduce_scatter | solution.py:1319
  79.6 6.8 copy-start.49
  81.5 4.9 copy-start.60
  90.0 2.3 copy-start.24
  90.0 2.3 copy-start.41
  95.9 3.6 copy-start.33
  150.6 5.3 copy-start.19
  150.7 5.3 copy-start.65
  276.5 3.1 copy-start.45
  276.5 3.1 copy-start.67
  279.0 5.3 copy-start.2
  279.6 4.7 copy-start.63
  329.1 5.8 copy-start.47
  561.8 203.9 %reduce-scatter.5.cloned.1.call-start = ((), (), s32[]{:S(2)}) async-start(), calls=%async_computation.4 | async-start | bytes 15925248 | tf_op jit(solution)/shard_map/reduce_scatter | solution.py:1317
  562.4 255.2 %reduce-scatter.9.cloned.1.call-start = ((), (), s32[]{:S(2)}) async-start(), calls=%async_computation.6 | async-start | bytes 7077888 | tf_op jit(solution)/shard_map/reduce_scatter | solution.py:1341
  563.8 3.8 slice-start
  565.5 2.2 slice-start.1
  566.8 3.1 copy-start.4
  610.7 11.9 %copy-start.31 = (bf16[256,256]{0,1:T(8,128)(2,1)}, bf16[256,256]{0,1:T(8,128)(2,1)S(1)}, u32[]{:S(2)}) copy-start(bf16[256,256]{0,1:T(8,128)(2,1)S(1)} %copy.52) | copy-start | bytes 393220
  622.1 6.4 copy-start.5
  622.1 406.8 %reduce-scatter.11.cloned.1.call-start = ((), (), s32[]{:S(2)}) async-start(), calls=%async_computation.7 | async-start | bytes 15925248 | tf_op jit(solution)/shard_map/reduce_scatter | solution.py:1317
  622.6 6.0 copy-start.21
  628.6 3.6 copy-start.70
  762.7 2.0 copy-start.14
  762.7 2.0 copy-start.32
  762.7 3.0 copy-start.1
  762.7 3.0 copy-start.44
  762.7 2.9 copy-start.57
  765.7 2.8 copy-start.15
  765.7 2.8 copy-start.16
  765.7 2.8 copy-start.69
  769.0 5.2 copy-start.8
  823.9 7.2 copy-start.53
  823.9 7.2 copy-start.54
  823.9 7.2 copy-start.55
  823.9 7.9 copy-start.9
  1036.8 2.0 copy-start.35
  1036.8 2.0 copy-start.36
  1040.7 2.0 copy-start.37
  1040.7 2.0 copy-start.38
  1040.7 3.6 copy-start.29
  1042.8 2.3 copy-start.10
  1042.8 2.6 copy-start.12
  1042.8 2.6 copy-start.51
  1042.8 2.6 copy-start.62
  1042.8 2.6 copy-start.72
  (35 other events, 52.8 us)
Sparse Core Ops, SparseCore 0:
  16.7 151.1 all-gather.4
  170.3 122.7 all-gather.6
  561.9 63.4 reduce-scatter.6
  628.8 120.4 reduce-scatter.4
  752.6 61.6 reduce-scatter.8
  817.7 158.8 reduce-scatter.10

commit v6 on v3

--- a/solution.py
+++ b/solution.py
@@ -549,7 +549,7 @@
 def ffn_forward(x, w, n, following=()):
     rows, d_model = x.shape
     owners, _, shard, width = w.shape
-    pieces = 3
+    pieces = 6
     piece = d_model // pieces
     count = len(following)
     return pl.pallas_call(
@@ -724,7 +724,7 @@
 def ffn_backward(g, w, xall, gate, up, n):
     rows, d_model = g.shape
     owners, _, shard, width = w.shape
-    pieces, groups = 3, 4
+    pieces, groups = 6, 4
     piece = d_model // pieces
     per = d_model // groups // shard
     return pl.pallas_call(
@@ -758,16 +758,44 @@
     )(g, w, xall, gate, up)
 
 
-def attention_forward_kernel(n, q_ref, kv_ref, pq_ref, pk_ref, mixed_ref, lse_ref, kvall_ref,
-                             kvbuf, vt, *sems):
+def half_turn(x):
+    return pltpu.roll(x, HEAD // 2, 1)
+
+
+def attention_forward_kernel(n, owners, count, proj_ref, cos_ref, sin_ref, pq_ref, pk_ref, *refs):
+    own = refs[:count]
+    mixed_ref, lse_ref, kvall_ref, q_ref = refs[count:count + 4]
+    full = refs[count + 4:2 * count + 4]
+    kvbuf, vt, *sems = refs[2 * count + 4:]
     line = Line(n)
     z = line.z
     rows = q_ref.shape[0]
     total = n * rows
-    gather = Gather(line, kvbuf, *sems)
-    line.barrier()
-    gather.start(kv_ref)
-    kvbuf[z] = kv_ref[...]
+    gather = Gather(line, kvbuf, *sems[:3])
+
+    def rotated(h):
+        x = proj_ref[:, h * HEAD:(h + 1) * HEAD]
+        return (x * cos_ref[...] + half_turn(x) * sin_ref[...]).astype(BF)
+
+    for g in range(KV_HEADS):
+        kvbuf[z, :, g * HEAD:(g + 1) * HEAD] = rotated(QUERY_HEADS + g)
+    kvbuf[z, :, KV_WIDTH:] = proj_ref[:, Q_WIDTH + KV_WIDTH:].astype(BF)
+    spreads = []
+    stages = 0
+    if count:
+        cube = Cube(owners)
+        stages = len(cube.chip_bits)
+        for i in range(count):
+            at = 3 + SPREAD_SEMS * i
+            spreads.append(Spread(cube, own[i], full[i], *sems[at:at + SPREAD_SEMS]))
+        joint_barrier(line, cube)
+    else:
+        line.barrier()
+    gather.start(kvbuf.at[z])
+    for s in spreads:
+        s.start()
+    for h in range(QUERY_HEADS):
+        q_ref[:, h * HEAD:(h + 1) * HEAD] = rotated(h)
     for i in range(1, n):
         gather.arrive(line.order(i))
     kvall_ref[...] = kvbuf[...]
@@ -787,34 +815,45 @@
             o = dot_nn(vt[g], e.astype(BF)) / den
             mixed_ref[:, h * HEAD:(h + 1) * HEAD] = o.T.astype(BF)
             lse_ref[h:h + 1, :] = top + jnp.log(den)
+            if h == 5 and stages:
+                for sp in spreads:
+                    sp.phase(1)
+    for k in range(2, stages + 1):
+        for sp in spreads:
+            sp.phase(k)
     gather.finish()
-
-
-def attention_forward(q, kv, pos_q, pos_k, n):
-    rows = q.shape[0]
+    for sp in spreads:
+        sp.finish()
+
+
+def attention_forward(projected, cosine, sine, pos_q, pos_k, n, owners, following=()):
+    rows = projected.shape[0]
+    count = len(following)
     return pl.pallas_call(
-        functools.partial(attention_forward_kernel, n),
+        functools.partial(attention_forward_kernel, n, owners, count),
         out_shape=(
             jax.ShapeDtypeStruct((rows, Q_WIDTH), BF),
             jax.ShapeDtypeStruct((16, rows), F32),
             jax.ShapeDtypeStruct((n, rows, 2 * KV_WIDTH), BF),
-        ),
-        in_specs=[VM] * 4,
-        out_specs=[VM] * 3,
+            jax.ShapeDtypeStruct((rows, Q_WIDTH), BF),
+        ) + spread_shapes(owners, following),
+        in_specs=[VM] * (5 + count),
+        out_specs=[VM] * 4 + [ANY] * count,
         scratch_shapes=[
             pltpu.VMEM((n, rows, 2 * KV_WIDTH), BF),
             pltpu.VMEM((KV_HEADS, HEAD, n * rows), BF),
-        ] + gather_sems(n),
-        compiler_params=params(3),
+        ] + gather_sems(n) + spread_sems(owners) * count,
+        compiler_params=params(9 if count else 3),
         cost_estimate=pl.CostEstimate(
             flops=4 * n * rows * rows * Q_WIDTH, transcendentals=n * rows * rows * QUERY_HEADS,
             bytes_accessed=16 << 20),
         name="attention_forward",
-    )(q, kv, pos_q, pos_k)
-
-
-def attention_backward_kernel(n, q_ref, kvall_ref, lse_ref, dm_ref, pq_ref, pk_ref,
-                              dq_ref, dkv_ref, kt, dk_acc, dv_acc, part, from_l, from_r, *sems):
+    )(projected, cosine, sine, pos_q, pos_k, *following)
+
+
+def attention_backward_kernel(n, q_ref, kvall_ref, lse_ref, dm_ref, cos_ref, sin_ref, pq_ref,
+                              pk_ref, dproj_ref, dkv_ref, kt, dk_acc, dv_acc, part,
+                              from_l, from_r, *sems):
     line = Line(n)
     z = line.z
     rows = q_ref.shape[0]
@@ -822,6 +861,10 @@
     pieces = KV_HEADS
     scatter = Scatter(line, pieces, part, from_l, from_r, *sems)
     line.barrier()
+
+    def rotated_back(x):
+        return (x * cos_ref[...] - half_turn(x) * sin_ref[...]).astype(BF)
+
     allowed = pk_ref[...] <= pq_ref[...]
     for g in range(KV_HEADS):
         k = kvall_ref[:, :, g * HEAD:(g + 1) * HEAD].reshape(total, HEAD)
@@ -847,7 +890,7 @@
             else:
                 dk_acc[...] += dk
                 dv_acc[...] += dv
-            dq_ref[:, cols] = dot_nn(kt[g], ds).T
+            dproj_ref[:, cols] = rotated_back(dot_nn(kt[g], ds).T)
         for b in range(n):
             sl = slice(b * rows, (b + 1) * rows)
 
@@ -871,20 +914,22 @@
 
     for t in scatter.steps():
         scatter.step(t, add_own)
+    for g in range(KV_HEADS):
+        cols = slice(Q_WIDTH + g * HEAD, Q_WIDTH + (g + 1) * HEAD)
+        dproj_ref[:, cols] = rotated_back(dkv_ref[:, g * HEAD:(g + 1) * HEAD])
+    dproj_ref[:, Q_WIDTH + KV_WIDTH:] = dkv_ref[:, KV_WIDTH:].astype(BF)
     scatter.finish()
 
 
-def attention_backward(q, kvall, lse, dm, pos_q, pos_k, n):
+def attention_backward(q, kvall, lse, dm, cosine, sine, pos_q, pos_k, n):
     rows = q.shape[0]
     return pl.pallas_call(
         functools.partial(attention_backward_kernel, n),
-        out_shape=(
-            jax.ShapeDtypeStruct((rows, Q_WIDTH), F32),
-            jax.ShapeDtypeStruct((rows, 2 * KV_WIDTH), F32),
-        ),
-        in_specs=[VM] * 6,
-        out_specs=[VM] * 2,
+        out_shape=jax.ShapeDtypeStruct((rows, Q_WIDTH + 2 * KV_WIDTH), BF),
+        in_specs=[VM] * 8,
+        out_specs=VM,
         scratch_shapes=[
+            pltpu.VMEM((rows, 2 * KV_WIDTH), F32),
             pltpu.VMEM((KV_HEADS, HEAD, n * rows), BF),
             pltpu.VMEM((n * rows, HEAD), F32),
             pltpu.VMEM((n * rows, HEAD), F32),
@@ -894,7 +939,7 @@
             flops=10 * n * rows * rows * Q_WIDTH, transcendentals=n * rows * rows * QUERY_HEADS,
             bytes_accessed=16 << 20),
         name="attention_backward",
-    )(q, kvall, lse, dm, pos_q, pos_k)
+    )(q, kvall, lse, dm, cosine, sine, pos_q, pos_k)
 
 
 class Fold:
@@ -1160,12 +1205,6 @@
     return back, jnp.sum(grad * stream * r, axis=0)
 
 
-def rotate(heads, cosine, sine):
-    half = HEAD // 2
-    a, b = heads[..., :half], heads[..., half:]
-    return jnp.concatenate([a * cosine - b * sine, b * cosine + a * sine], axis=-1)
-
-
 def frequencies():
     return jnp.power(ROPE_BASE, -(jnp.arange(HEAD // 2, dtype=F32) * 2.0 / HEAD))
 
@@ -1193,7 +1232,9 @@
     pos_q = my_position[None, :]
     pos_k = jnp.where(valid, position, 1 << 30)[:, None]
     angles = my_position.astype(F32)[:, None] * frequencies()
-    cosine, sine = jnp.cos(angles)[:, None, :], jnp.sin(angles)[:, None, :]
+    cosine, sine = jnp.cos(angles), jnp.sin(angles)
+    cosine = jnp.concatenate([cosine, cosine], axis=1)
+    sine = jnp.concatenate([-sine, sine], axis=1)
 
     shard = norm_attn.shape[1]
     bias_shard = b_qkv.shape[1]
@@ -1214,9 +1255,9 @@
     first_ffn = ffn_shard(0)
     first_ffn, small = lax.optimization_barrier((first_ffn, small))
     ffn_weights = [lax.all_gather(first_ffn, "fsdp", axis=0, tiled=False)]
-    small, qkv_w, out_w = spread_all(owners, small, w_qkv[0], w_out[0])
+    small, qkv_w = spread_all(owners, small, w_qkv[0])
     qkv_weights = [qkv_w.reshape(d_model, -1)]
-    out_weights = [out_w.reshape(Q_WIDTH, d_model)]
+    out_weights = []
     small = small.reshape(owners, -1)
     gains_attn, gains_mlp, biases = [], [], []
     for l in range(LAYERS):
@@ -1228,17 +1269,16 @@
     stream = hidden_in[0].astype(F32)
     kept = []
     for l in range(LAYERS):
-        qkv_w, out_w, ffn_w = qkv_weights[l], out_weights[l], ffn_weights[l]
+        qkv_w, ffn_w = qkv_weights[l], ffn_weights[l]
         if l + 1 < LAYERS:
             ffn_weights.append(lax.all_gather(ffn_shard(l + 1), "fsdp", axis=0, tiled=False))
         normed = normalize(stream, gains_attn[l]).astype(BF)
         projected = jnp.dot(normed, qkv_w, preferred_element_type=F32) + biases[l]
-        qk = rotate(
-            projected[:, :Q_WIDTH + KV_WIDTH].reshape(rows, QUERY_HEADS + KV_HEADS, HEAD),
-            cosine, sine).astype(BF).reshape(rows, Q_WIDTH + KV_WIDTH)
-        q = qk[:, :Q_WIDTH]
-        kv = jnp.concatenate([qk[:, Q_WIDTH:], projected[:, Q_WIDTH + KV_WIDTH:].astype(BF)], axis=1)
-        mixed, lse, kvall = attention_forward(q, kv, pos_q, pos_k, n)
+        following = (w_out[l],) if l == 0 else ()
+        mixed, lse, kvall, q, *out_w = attention_forward(
+            projected, cosine, sine, pos_q, pos_k, n, owners, following)
+        out_weights += [m.reshape(Q_WIDTH, d_model) for m in out_w]
+        out_w = out_weights[l]
         middle = stream + jnp.dot(mixed, out_w, preferred_element_type=F32)
         normed_two = normalize(middle, gains_mlp[l]).astype(BF)
         if l + 1 < LAYERS:
@@ -1268,15 +1308,11 @@
         d_low = d_middle.astype(BF)
         d_mixed = jnp.einsum("td,cd->tc", d_low, out_w, preferred_element_type=F32).astype(BF)
         out_grad = jnp.einsum("tc,td->cd", mixed, d_low, preferred_element_type=F32).astype(BF)
-        dq, dkv = attention_backward(q, kvall, lse, d_mixed, pos_q, pos_k, n)
+        d_projected = attention_backward(
+            q, kvall, lse, d_mixed, cosine, sine, pos_q, pos_k, n)
         if l < LAYERS - 1:
-            dq, out_sum, qkv_sum = lax.optimization_barrier((dq, out_sum, qkv_sum))
+            d_projected, out_sum = lax.optimization_barrier((d_projected, out_sum))
             big_grads[l + 1] = (out_sum, qkv_sum, dw_sum)
-        d_qk = rotate(
-            jnp.concatenate([dq, dkv[:, :KV_WIDTH]], axis=1).reshape(
-                rows, QUERY_HEADS + KV_HEADS, HEAD),
-            cosine, -sine).reshape(rows, Q_WIDTH + KV_WIDTH)
-        d_projected = jnp.concatenate([d_qk, dkv[:, KV_WIDTH:]], axis=1).astype(BF)
         bias_grad = jnp.sum(d_projected.astype(F32), axis=0)
         d_normed = jnp.einsum("tc,dc->td", d_projected, qkv_w, preferred_element_type=F32)
         qkv_grad = jnp.einsum(

time: 1030 us -> 1040 us (level)
  Pallas kernels: 830 us -> 860 us
  local copies, waits for them, and re-layouts: 47.1 us -> 33.1 us
  other arithmetic: 53.7 us -> 42.5 us
    pallas_call x1, Pallas kernels: 88.1 us -> 59 us  [spread_all(): pl.pallas_call(functools.partial(spread_kernel, owners, count), out_shape...]
    pallas_call x2, Pallas kernels: 234 us -> 262 us  [ffn_backward(): pl.pallas_call(functools.partial(ffn_backward_kernel, n, pieces, groups),...]
    pallas_call x2, Pallas kernels: 200 us -> 219 us  [ffn_forward(): pl.pallas_call(functools.partial(ffn_forward_kernel, n, pieces, count), o...]
    reduce_scatter x1, waiting for transfers between devices: 17.1 us -> 0.01 us  [shards(): lax.psum_scatter(qkv_grad, 'fsdp', scatter_dimension=0, tiled=True)]
    pallas_call x2, Pallas kernels: 67.6 us -> 82.3 us  [attention_forward(): pl.pallas_call(functools.partial(attention_forward_kernel, n, owners, cou...]
    all_gather x1, waiting for transfers between devices: 0.01 us -> 13.6 us  [shards(): ffn_weights = [lax.all_gather(first_ffn, 'fsdp', axis=0, tiled=False)]]
  transfers between devices with their start and end apart: 5 -> 5, of which waited for: 1 -> 1; matrix products, arithmetic and copies ran while one was open for 10% -> 10% of each run, Pallas kernels for 44% -> 45%
where the time goes in v6:
time: 1040 us; the launch traced here: 1030 us
  Pallas kernels  860 us (83%)
  matrix products  64.3 us (6%)
  other arithmetic  42.5 us (4%)
  local copies, waits for them, and re-layouts  33.1 us (3%)
  between operations  15.4 us (1%)
  waiting for transfers between devices  13.7 us (1%)
    pallas_call x2, Pallas kernels, ffn_backward(): pl.pallas_call(functools.partial(ffn_backward_kernel, n, pieces, groups),...  262 us
    pallas_call x2, Pallas kernels, ffn_forward(): pl.pallas_call(functools.partial(ffn_forward_kernel, n, pieces, count), o...  219 us
    pallas_call x1, Pallas kernels, reduce_all(): pl.pallas_call(functools.partial(reduce_kernel, n, owners), out_shape=(ja...  163 us
    pallas_call x2, Pallas kernels, attention_forward(): pl.pallas_call(functools.partial(attention_forward_kernel, n, owners, cou...  82.3 us
    pallas_call x2, Pallas kernels, attention_backward(): pl.pallas_call(functools.partial(attention_backward_kernel, n), out_shape...  75.6 us
    pallas_call x1, Pallas kernels, spread_all(): pl.pallas_call(functools.partial(spread_kernel, owners, count), out_shape...  59 us
  transfers between devices with their start and end apart: 5, of which 1 were waited for; matrix products, arithmetic and copies ran while one was open for 10% of the time, Pallas kernels for 45%

profile of v6, /device:TPU:0, one launch (start us, length us, event | category | flops | bytes accessed | tf_op | source)
XLA Modules:
  0.0 1029.6 jit_solution(165871044291505469)
XLA Ops:
  9.4 1.5 slice_bitcast_fusion.4
  11.1 1.4 copy-done.23
  12.6 1.4 copy-done.24
  14.8 1.8 pad_maximum_fusion
  16.9 1.8 pad_maximum_fusion.1
  21.8 1.2 slice_bitcast_fusion.8
  23.1 59.0 %spread_all.1 = (f32[8,16,128]{2,1,0:T(8,128)}, bf16[8,192,2048]{2,1,0:T(8,128)(2,1)}) custom-call(f32[16,128]{1,0:T(8,128)} %fusion.51.refs_0_, bf16[192,2048]{1,0:T(8,128)(2,1)} %get-tuple-element.113.refs_1_), custom_call_target="tpu_custom_call" | custom-call | flops 1048576 | bytes 157286400 | tf_op jit(solution)/shard_map/spread_all/pallas_call | solution.py:414
  87.2 1.3 fusion.57
  91.6 1.1 slice_bitcast_fusion.10
  92.7 5.9 convolution_add_fusion.3.proj_ref
  98.7 50.3 %attention_forward.2 = (bf16[256,1536]{1,0:T(8,128)(2,1)}, f32[16,256]{1,0:T(8,128)}, bf16[4,256,512]{2,1,0:T(8,128)(2,1)}, bf16[256,1536]{1,0:T(8,128)(2,1)}, bf16[8,192,1536]{2,1,0:T(8,128)(2,1)}) custom-call(f32[256,2048]{1,0:T(8,128)} %convolution_add_fusion.3.proj_ref, f32[256,128]{1,0:T(8,128)} %get-tuple-element.145.cos_ref, ...), custom_call_target="tpu_custom_call" | custom-call | flops 1610612736 | bytes 16777216 | tf_op jit(solution)/shard_map/attention_forward/pallas_call | solution.py:832
  149.0 4.3 multiply_reduce_fusion.8
  155.1 1.1 multiply_convert_fusion.2.refs_0_
  156.2 13.6 %all-gather.5.cloned.1.call-done = bf16[24,192,2304]{2,1,0:T(8,128)(2,1)} async-done(((bf16[3,192,2304]{2,1,0:T(8,128)(2,1)}), bf16[24,192,2304]{2,1,0:T(8,128)(2,1)}) %all-gather.5.cloned.1.call-update) | async-done | bytes 21233680 | tf_op jit(solution)/shard_map/all_gather | solution.py:1257
  169.7 114.0 %ffn_forward.2 = (bf16[4,256,1536]{2,1,0:T(8,128)(2,1)}, bf16[4,256,2304]{2,1,0:T(8,128)(2,1)}, bf16[4,256,2304]{2,1,0:T(8,128)(2,1)}, f32[256,1536]{1,0:T(8,128...) custom-call(bf16[256,1536]{1,0:T(8,128)(2,1)} %multiply_convert_fusion.2.refs_0_, ...), custom_call_target="tpu_custom_call" | custom-call | flops 21743271936 | bytes 62914560 | tf_op jit(solution)/shard_map/ffn_forward/pallas_call | solution.py:555
  283.8 2.1 multiply_reduce_fusion.7
  287.1 6.0 convolution_add_fusion.2.proj_ref
  293.1 31.9 %attention_forward.3 = (bf16[256,1536]{1,0:T(8,128)(2,1)}, f32[16,256]{1,0:T(8,128)}, bf16[4,256,512]{2,1,0:T(8,128)(2,1)}, bf16[256,1536]{1,0:T(8,128)(2,1)}) custom-call(f32[256,2048]{1,0:T(8,128)} %convolution_add_fusion.2.proj_ref, f32[256,128]{1,0:T(8,128)} %get-tuple-element.145.cos_ref, f32[256,128]{1,0:T(8,128)} %get-tuple-element.146.sin_ref, ...), custom_call_target="tpu_custom_call" | custom-call | flops 1610612736 | bytes 16777216 | tf_op jit(solution)/shard_map/attention_forward/pallas_call | solution.py:832
  325.1 4.5 multiply_reduce_fusion.6
  331.8 105.1 %ffn_forward.3 = (bf16[4,256,1536]{2,1,0:T(8,128)(2,1)}, bf16[4,256,2304]{2,1,0:T(8,128)(2,1)}, bf16[4,256,2304]{2,1,0:T(8,128)(2,1)}, f32[256,1536]{1,0:T(8,128)}) custom-call(bf16[256,1536]{1,0:T(8,128)(2,1)} %multiply_convert_fusion.refs_0_, bf16[8,3,192,2304]{3,2,1,0:T(8,128)(2,1)} %bitcast.176), custom_call_target="tpu_custom_call" | custom-call | flops 21743271936 | bytes 62914560 | tf_op jit(solution)/shard_map/ffn_forward/pallas_call | solution.py:555
  437.0 131.0 %ffn_backward.2 = (bf16[8,3,192,2304]{3,2,1,0:T(8,128)(2,1)}, f32[256,1536]{1,0:T(8,128)}) custom-call(bf16[256,1536]{1,0:T(8,128)(2,1)} %fusion.19.g_ref, bf16[8,3,192,2304]{3,2,1,0:T(8,128)(2,1)} %bitcast.177, bf16[4,256,1536]{2,1,0:T(8,128)(2,1)} %get-tuple-element.58.xall_ref, bf16[4,256,2304]{2,1,0:T(8,128)(2,1)} %get-tuple-element.59.gate_ref, ...), custom_call_target="tpu_custom_call" | custom-call | flops 43486543872 | bytes 104857600 | tf_op jit(solution)/shard_map/ffn_backward/pallas_call | solution.py:730
  568.1 1.3 copy-done.7
  572.0 3.2 fusion.18
  575.2 4.2 convolution_convert_fusion.3
  580.2 5.7 convolution_convert_fusion.5.dm_ref
  585.9 37.8 %attention_backward.2 = bf16[256,2048]{1,0:T(8,128)(2,1)} custom-call(bf16[256,1536]{1,0:T(8,128)(2,1)} %get-tuple-element.62.q_ref, bf16[4,256,512]{2,1,0:T(8,128)(2,1)} %get-tuple-element.63.kvall_ref, f32[16,256]{1,0:T(8,128)} %get-tuple-element.64.lse_ref, bf16[256,1536]{1,0:T(8,128)(2,1)} %convolution_convert_fusion.5.dm_ref, ...), custom_call_target="tpu_custom_call" | custom-call | flops 4026531840 | bytes 16777216 | tf_op jit(solution)/shard_map/attention_backward/pallas_call | solution.py:926
  623.7 6.3 convolution_convert_fusion
  630.1 1.4 copy-done.3
  631.5 6.7 multiply_reduce_fusion.2
  638.8 1.6 convert_reduce_fusion
  641.0 3.3 fusion.56
  644.3 130.7 %ffn_backward.3 = (bf16[8,3,192,2304]{3,2,1,0:T(8,128)(2,1)}, f32[256,1536]{1,0:T(8,128)}) custom-call(bf16[256,1536]{1,0:T(8,128)(2,1)} %get-tuple-element.92.g_ref, bf16[8,3,192,2304]{3,2,1,0:T(8,128)(2,1)} %bitcast.175, bf16[4,256,1536]{2,1,0:T(8,128)(2,1)} %get-tuple-element.65.xall_ref, bf16[4,256,2304]{2,1,0:T(8,128)(2,1)} %get-tuple-element.66.gate_ref, ...), custom_call_target="tpu_custom_call" | custom-call | flops 43486543872 | bytes 104857600 | tf_op jit(solution)/shard_map/ffn_backward/pallas_call | solution.py:730
  775.1 2.7 multiply_reduce_fusion.1
  778.5 1.9 multiply_add_fusion
  780.4 5.2 convolution_convert_fusion.4.dm_ref
  785.6 37.7 %attention_backward.3 = bf16[256,2048]{1,0:T(8,128)(2,1)} custom-call(bf16[256,1536]{1,0:T(8,128)(2,1)} %get-tuple-element.71.q_ref, bf16[4,256,512]{2,1,0:T(8,128)(2,1)} %get-tuple-element.72.kvall_ref, f32[16,256]{1,0:T(8,128)} %get-tuple-element.73.lse_ref, bf16[256,1536]{1,0:T(8,128)(2,1)} %convolution_convert_fusion.4.dm_ref, ...), custom_call_target="tpu_custom_call" | custom-call | flops 4026531840 | bytes 16777216 | tf_op jit(solution)/shard_map/attention_backward/pallas_call | solution.py:926
  823.5 7.2 fusion.13
  831.8 3.6 convolution_convert_fusion.2
  835.4 4.6 convolution_convert_fusion.1
  840.0 162.8 %reduce_all.1 = (f32[16,128]{1,0:T(8,128)}, bf16[192,1536]{1,0:T(8,128)(2,1)}, bf16[192,2048]{1,0:T(8,128)(2,1)}, bf16[3,192,2304]{2,1,0:T(8,128)(2,1)}, bf16[19...) custom-call(f32[8,16,128]{2,1,0:T(8,128)} %bitcast.160, bf16[8,192,1536]{2,1,0:T(8,128)(2,1)} %bitcast.154, ...), custom_call_target="tpu_custom_call" | custom-call | flops 1048576 | bytes 314572800 | tf_op jit(solution)/shard_map/reduce_all/pallas_call | solution.py:1177
  1004.2 1.9 slice_bitcast_fusion
  1008.1 2.0 slice_bitcast_fusion.1
  1010.2 1.9 maximum_convert_fusion.3
  1012.1 1.6 maximum_convert_fusion.4
  1013.7 2.0 maximum_convert_fusion.2
  1015.7 2.0 maximum_convert_fusion.1
  1017.7 2.0 maximum_convert_fusion
  1021.1 1.7 fusion.10
  (194 shorter events, 30.7 us)
Async XLA Ops:
  7.2 162.5 %all-gather.5.cloned.1.call-start = ((), (), s32[]{:S(2)}) async-start(), calls=%async_computation.6 | async-start | bytes 23887872 | tf_op jit(solution)/shard_map/all_gather | solution.py:1257
  16.6 315.2 %all-gather.7.cloned.1.call-start = ((), (), s32[]{:S(2)}) async-start(), calls=%async_computation.7 | async-start | bytes 23887872 | tf_op jit(solution)/shard_map/all_gather | solution.py:1274
  18.7 3.2 copy-start.25
  18.7 756.3 %reduce-scatter.4.cloned.1.call-start = ((), (), s32[]{:S(2)}) async-start(), calls=%async_computation.3 | async-start | bytes 23887872 | tf_op jit(solution)/shard_map/reduce_scatter | solution.py:1327
  82.1 7.8 copy-start.11
  82.1 8.7 copy-start.22
  83.0 8.6 copy-start.27
  85.1 7.6 copy-start.38
  90.7 2.0 copy-start.50
  149.0 5.0 copy-start.18
  149.0 5.0 copy-start.55
  283.7 3.4 copy-start.34
  283.7 3.4 copy-start.57
  325.0 5.7 copy-start.36
  568.0 2.3 copy-start.15
  568.0 2.3 copy-start.37
  568.0 2.3 copy-start.49
  568.1 255.4 %reduce-scatter.6.cloned.1.call-start = ((), (), s32[]{:S(2)}) async-start(), calls=%async_computation.4 | async-start | bytes 5308416 | tf_op jit(solution)/shard_map/reduce_scatter | solution.py:1325
  572.0 3.2 copy-start.21
  575.2 5.0 copy-start.4
  579.4 260.5 %reduce-scatter.8.cloned.1.call-start = ((), (), s32[]{:S(2)}) async-start(), calls=%async_computation.5 | async-start | bytes 7077888 | tf_op jit(solution)/shard_map/reduce_scatter | solution.py:1326
  631.5 9.5 copy-start.5
  631.5 9.5 copy-start.59
  775.0 3.4 copy-start.1
  775.1 3.4 copy-start.14
  775.1 3.4 copy-start.33
  775.1 3.4 copy-start.47
  775.1 3.4 copy-start.58
  780.4 5.2 copy-start.8
  823.4 7.3 copy-start.17
  823.4 7.5 copy-start.42
  823.4 7.5 copy-start.43
  823.4 7.5 copy-start.44
  823.4 7.5 copy-start.45
  823.4 8.2 copy-start.9
  831.8 3.6 copy-start.12
  831.8 3.6 copy-start.39
  831.8 3.6 copy-start.51
  1004.2 1.9 copy-start.62
  1008.1 2.0 copy-start.28
  1008.1 2.2 copy-start.29
  1010.2 1.9 copy-start.31
  1017.7 2.1 copy-start.10
  1017.7 2.7 copy-start.13
  1017.7 3.4 copy-start.26
  1017.7 3.4 copy-start.40
  1017.7 3.4 copy-start.52
  1017.7 3.4 copy-start.61
  (21 other events, 27.3 us)
Sparse Core Ops, SparseCore 0:
  16.7 152.9 all-gather.4
  172.2 137.0 all-gather.6
  568.2 133.4 reduce-scatter.3
  705.0 53.7 reduce-scatter.5
  762.1 61.7 reduce-scatter.7

commit v7 on v6

--- a/solution.py
+++ b/solution.py
@@ -524,14 +524,9 @@
         cols = slice(p * piece, (p + 1) * piece)
         y_ref[:, cols] = y_ref[:, cols] + value
 
-    passed = 2
     for t in scatter.steps():
         scatter.step(t, add_own)
-        if t >= 4 and t % 2 == 0 and passed <= stages:
-            for s in spreads:
-                s.phase(passed)
-            passed += 1
-    for k in range(passed, stages + 1):
+    for k in range(2, stages + 1):
         for s in spreads:
             s.phase(k)
     for i in range(max(0, n - 2), n):
@@ -549,7 +544,7 @@
 def ffn_forward(x, w, n, following=()):
     rows, d_model = x.shape
     owners, _, shard, width = w.shape
-    pieces = 6
+    pieces = 3
     piece = d_model // pieces
     count = len(following)
     return pl.pallas_call(
@@ -724,7 +719,7 @@
 def ffn_backward(g, w, xall, gate, up, n):
     rows, d_model = g.shape
     owners, _, shard, width = w.shape
-    pieces, groups = 6, 4
+    pieces, groups = 3, 4
     piece = d_model // pieces
     per = d_model // groups // shard
     return pl.pallas_call(

time: 1040 us -> 1010 us (0.971)
  Pallas kernels: 860 us -> 837 us
    pallas_call x2, Pallas kernels: 262 us -> 235 us  [ffn_backward(): pl.pallas_call(functools.partial(ffn_backward_kernel, n, pieces, groups),...]
  transfers between devices with their start and end apart: 5 -> 5, of which waited for: 1 -> 2; matrix products, arithmetic and copies ran while one was open for 10% -> 10% of each run, Pallas kernels for 45% -> 45%
where the time goes in v7:
time: 1010 us
  Pallas kernels  837 us (83%)
  matrix products  64.3 us (6%)
  other arithmetic  42 us (4%)
  local copies, waits for them, and re-layouts  33.5 us (3%)
  between operations  15.4 us (2%)
  waiting for transfers between devices  13.9 us (1%)
    pallas_call x2, Pallas kernels, ffn_backward(): pl.pallas_call(functools.partial(ffn_backward_kernel, n, pieces, groups),...  235 us
    pallas_call x2, Pallas kernels, ffn_forward(): pl.pallas_call(functools.partial(ffn_forward_kernel, n, pieces, count), o...  215 us
    pallas_call x1, Pallas kernels, reduce_all(): pl.pallas_call(functools.partial(reduce_kernel, n, owners), out_shape=(ja...  169 us
    pallas_call x2, Pallas kernels, attention_forward(): pl.pallas_call(functools.partial(attention_forward_kernel, n, owners, cou...  85.1 us
    pallas_call x2, Pallas kernels, attention_backward(): pl.pallas_call(functools.partial(attention_backward_kernel, n), out_shape...  74.5 us
    pallas_call x1, Pallas kernels, spread_all(): pl.pallas_call(functools.partial(spread_kernel, owners, count), out_shape...  59 us
  transfers between devices with their start and end apart: 5, of which 2 were waited for; matrix products, arithmetic and copies ran while one was open for 10% of the time, Pallas kernels for 45%

profile of v7, /device:TPU:0, one launch (start us, length us, event | category | flops | bytes accessed | tf_op | source)
XLA Modules:
  0.0 1006.3 jit_solution(16410419170811343389)
XLA Ops:
  9.4 1.5 slice_bitcast_fusion.4
  11.1 1.4 copy-done.23
  12.6 1.4 copy-done.24
  14.8 1.8 pad_maximum_fusion
  16.9 1.8 pad_maximum_fusion.1
  21.8 1.2 slice_bitcast_fusion.8
  23.1 59.0 %spread_all.1 = (f32[8,16,128]{2,1,0:T(8,128)}, bf16[8,192,2048]{2,1,0:T(8,128)(2,1)}) custom-call(f32[16,128]{1,0:T(8,128)} %fusion.51.refs_0_, bf16[192,2048]{1,0:T(8,128)(2,1)} %get-tuple-element.113.refs_1_), custom_call_target="tpu_custom_call" | custom-call | flops 1048576 | bytes 157286400 | tf_op jit(solution)/shard_map/spread_all/pallas_call | solution.py:414
  87.2 1.3 fusion.57
  91.6 1.1 slice_bitcast_fusion.10
  92.7 5.9 convolution_add_fusion.3.proj_ref
  98.7 50.3 %attention_forward.2 = (bf16[256,1536]{1,0:T(8,128)(2,1)}, f32[16,256]{1,0:T(8,128)}, bf16[4,256,512]{2,1,0:T(8,128)(2,1)}, bf16[256,1536]{1,0:T(8,128)(2,1)}, bf16[8,192,1536]{2,1,0:T(8,128)(2,1)}) custom-call(f32[256,2048]{1,0:T(8,128)} %convolution_add_fusion.3.proj_ref, f32[256,128]{1,0:T(8,128)} %get-tuple-element.145.cos_ref, ...), custom_call_target="tpu_custom_call" | custom-call | flops 1610612736 | bytes 16777216 | tf_op jit(solution)/shard_map/attention_forward/pallas_call | solution.py:827
  149.0 4.3 multiply_reduce_fusion.8
  156.2 13.6 %all-gather.5.cloned.1.call-done = bf16[24,192,2304]{2,1,0:T(8,128)(2,1)} async-done(((bf16[3,192,2304]{2,1,0:T(8,128)(2,1)}), bf16[24,192,2304]{2,1,0:T(8,128)(2,1)}) %all-gather.5.cloned.1.call-update) | async-done | bytes 21233680 | tf_op jit(solution)/shard_map/all_gather | solution.py:1252
  169.7 115.6 %ffn_forward.2 = (bf16[4,256,1536]{2,1,0:T(8,128)(2,1)}, bf16[4,256,2304]{2,1,0:T(8,128)(2,1)}, bf16[4,256,2304]{2,1,0:T(8,128)(2,1)}, f32[256,1536]{1,0:T(8,128...) custom-call(bf16[256,1536]{1,0:T(8,128)(2,1)} %multiply_convert_fusion.2.refs_0_, ...), custom_call_target="tpu_custom_call" | custom-call | flops 21743271936 | bytes 62914560 | tf_op jit(solution)/shard_map/ffn_forward/pallas_call | solution.py:550
  285.3 2.3 multiply_reduce_fusion.7
  288.8 6.0 convolution_add_fusion.2.proj_ref
  294.8 34.8 %attention_forward.3 = (bf16[256,1536]{1,0:T(8,128)(2,1)}, f32[16,256]{1,0:T(8,128)}, bf16[4,256,512]{2,1,0:T(8,128)(2,1)}, bf16[256,1536]{1,0:T(8,128)(2,1)}) custom-call(f32[256,2048]{1,0:T(8,128)} %convolution_add_fusion.2.proj_ref, f32[256,128]{1,0:T(8,128)} %get-tuple-element.145.cos_ref, f32[256,128]{1,0:T(8,128)} %get-tuple-element.146.sin_ref, ...), custom_call_target="tpu_custom_call" | custom-call | flops 1610612736 | bytes 16777216 | tf_op jit(solution)/shard_map/attention_forward/pallas_call | solution.py:827
  329.6 4.5 multiply_reduce_fusion.6
  336.4 99.0 %ffn_forward.3 = (bf16[4,256,1536]{2,1,0:T(8,128)(2,1)}, bf16[4,256,2304]{2,1,0:T(8,128)(2,1)}, bf16[4,256,2304]{2,1,0:T(8,128)(2,1)}, f32[256,1536]{1,0:T(8,128)}) custom-call(bf16[256,1536]{1,0:T(8,128)(2,1)} %multiply_convert_fusion.refs_0_, bf16[8,3,192,2304]{3,2,1,0:T(8,128)(2,1)} %bitcast.176), custom_call_target="tpu_custom_call" | custom-call | flops 21743271936 | bytes 62914560 | tf_op jit(solution)/shard_map/ffn_forward/pallas_call | solution.py:550
  435.4 117.8 %ffn_backward.2 = (bf16[8,3,192,2304]{3,2,1,0:T(8,128)(2,1)}, f32[256,1536]{1,0:T(8,128)}) custom-call(bf16[256,1536]{1,0:T(8,128)(2,1)} %fusion.19.g_ref, bf16[8,3,192,2304]{3,2,1,0:T(8,128)(2,1)} %bitcast.177, bf16[4,256,1536]{2,1,0:T(8,128)(2,1)} %get-tuple-element.58.xall_ref, bf16[4,256,2304]{2,1,0:T(8,128)(2,1)} %get-tuple-element.59.gate_ref, ...), custom_call_target="tpu_custom_call" | custom-call | flops 43486543872 | bytes 104857600 | tf_op jit(solution)/shard_map/ffn_backward/pallas_call | solution.py:725
  553.4 1.3 copy-done.7
  555.7 1.3 copy-done.16
  557.4 2.8 fusion.18
  560.2 4.2 convolution_convert_fusion.3
  565.1 5.8 convolution_convert_fusion.5.dm_ref
  570.9 37.4 %attention_backward.2 = bf16[256,2048]{1,0:T(8,128)(2,1)} custom-call(bf16[256,1536]{1,0:T(8,128)(2,1)} %get-tuple-element.62.q_ref, bf16[4,256,512]{2,1,0:T(8,128)(2,1)} %get-tuple-element.63.kvall_ref, f32[16,256]{1,0:T(8,128)} %get-tuple-element.64.lse_ref, bf16[256,1536]{1,0:T(8,128)(2,1)} %convolution_convert_fusion.5.dm_ref, ...), custom_call_target="tpu_custom_call" | custom-call | flops 4026531840 | bytes 16777216 | tf_op jit(solution)/shard_map/attention_backward/pallas_call | solution.py:921
  608.3 6.4 convolution_convert_fusion
  614.7 1.6 copy-done.3
  616.4 6.5 multiply_reduce_fusion.2
  623.6 1.4 convert_reduce_fusion
  625.6 3.6 fusion.56
  629.1 117.0 %ffn_backward.3 = (bf16[8,3,192,2304]{3,2,1,0:T(8,128)(2,1)}, f32[256,1536]{1,0:T(8,128)}) custom-call(bf16[256,1536]{1,0:T(8,128)(2,1)} %get-tuple-element.92.g_ref, bf16[8,3,192,2304]{3,2,1,0:T(8,128)(2,1)} %bitcast.175, bf16[4,256,1536]{2,1,0:T(8,128)(2,1)} %get-tuple-element.65.xall_ref, bf16[4,256,2304]{2,1,0:T(8,128)(2,1)} %get-tuple-element.66.gate_ref, ...), custom_call_target="tpu_custom_call" | custom-call | flops 43486543872 | bytes 104857600 | tf_op jit(solution)/shard_map/ffn_backward/pallas_call | solution.py:725
  746.2 2.4 multiply_reduce_fusion.1
  749.3 1.9 multiply_add_fusion
  751.2 5.3 convolution_convert_fusion.4.dm_ref
  756.5 37.1 %attention_backward.3 = bf16[256,2048]{1,0:T(8,128)(2,1)} custom-call(bf16[256,1536]{1,0:T(8,128)(2,1)} %get-tuple-element.71.q_ref, bf16[4,256,512]{2,1,0:T(8,128)(2,1)} %get-tuple-element.72.kvall_ref, f32[16,256]{1,0:T(8,128)} %get-tuple-element.73.lse_ref, bf16[256,1536]{1,0:T(8,128)(2,1)} %convolution_convert_fusion.4.dm_ref, ...), custom_call_target="tpu_custom_call" | custom-call | flops 4026531840 | bytes 16777216 | tf_op jit(solution)/shard_map/attention_backward/pallas_call | solution.py:921
  793.8 7.2 fusion.13
  802.1 3.6 convolution_convert_fusion.2
  805.7 4.6 convolution_convert_fusion.1
  810.5 169.0 %reduce_all.1 = (f32[16,128]{1,0:T(8,128)}, bf16[192,1536]{1,0:T(8,128)(2,1)}, bf16[192,2048]{1,0:T(8,128)(2,1)}, bf16[3,192,2304]{2,1,0:T(8,128)(2,1)}, bf16[19...) custom-call(f32[8,16,128]{2,1,0:T(8,128)} %bitcast.160, bf16[8,192,1536]{2,1,0:T(8,128)(2,1)} %bitcast.154, ...), custom_call_target="tpu_custom_call" | custom-call | flops 1048576 | bytes 314572800 | tf_op jit(solution)/shard_map/reduce_all/pallas_call | solution.py:1172
  981.0 1.9 slice_bitcast_fusion
  984.9 2.0 slice_bitcast_fusion.1
  987.0 1.9 maximum_convert_fusion.3
  988.9 1.6 maximum_convert_fusion.4
  990.5 2.0 maximum_convert_fusion.2
  992.5 2.0 maximum_convert_fusion.1
  994.5 2.0 maximum_convert_fusion
  997.9 1.7 fusion.10
  (194 shorter events, 30.9 us)
Async XLA Ops:
  7.2 162.5 %all-gather.5.cloned.1.call-start = ((), (), s32[]{:S(2)}) async-start(), calls=%async_computation.6 | async-start | bytes 23887872 | tf_op jit(solution)/shard_map/all_gather | solution.py:1252
  16.6 319.8 %all-gather.7.cloned.1.call-start = ((), (), s32[]{:S(2)}) async-start(), calls=%async_computation.7 | async-start | bytes 23887872 | tf_op jit(solution)/shard_map/all_gather | solution.py:1269
  18.7 3.2 copy-start.25
  18.7 727.4 %reduce-scatter.4.cloned.1.call-start = ((), (), s32[]{:S(2)}) async-start(), calls=%async_computation.3 | async-start | bytes 23887872 | tf_op jit(solution)/shard_map/reduce_scatter | solution.py:1322
  82.1 7.8 copy-start.11
  82.1 8.7 copy-start.22
  83.0 8.6 copy-start.27
  85.1 7.6 copy-start.38
  90.7 2.0 copy-start.50
  149.0 5.0 copy-start.18
  149.0 5.0 copy-start.55
  285.3 3.5 copy-start.34
  285.3 3.5 copy-start.57
  329.6 5.7 copy-start.36
  553.3 240.4 %reduce-scatter.6.cloned.1.call-start = ((), (), s32[]{:S(2)}) async-start(), calls=%async_computation.4 | async-start | bytes 5308416 | tf_op jit(solution)/shard_map/reduce_scatter | solution.py:1320
  555.1 2.3 copy-start.19
  555.1 2.3 copy-start.56
  555.1 2.2 copy-start.60
  557.4 2.8 copy-start.21
  560.2 4.9 copy-start.4
  564.4 246.1 %reduce-scatter.8.cloned.1.call-start = ((), (), s32[]{:S(2)}) async-start(), calls=%async_computation.5 | async-start | bytes 7077888 | tf_op jit(solution)/shard_map/reduce_scatter | solution.py:1321
  616.4 9.2 copy-start.5
  616.4 9.2 copy-start.59
  746.1 3.2 copy-start.1
  746.1 3.2 copy-start.14
  746.2 3.1 copy-start.33
  746.2 3.1 copy-start.47
  746.2 3.1 copy-start.58
  751.2 5.3 copy-start.8
  793.7 7.3 copy-start.17
  793.7 7.5 copy-start.42
  793.7 7.5 copy-start.43
  793.7 7.5 copy-start.44
  793.7 7.5 copy-start.45
  793.7 8.2 copy-start.9
  802.1 3.6 copy-start.12
  802.1 3.6 copy-start.39
  802.1 3.6 copy-start.51
  981.0 1.9 copy-start.62
  984.9 2.0 copy-start.28
  984.9 2.2 copy-start.29
  987.0 1.9 copy-start.31
  994.5 2.1 copy-start.10
  994.5 2.7 copy-start.13
  994.5 3.4 copy-start.26
  994.5 3.4 copy-start.40
  994.5 3.4 copy-start.52
  994.5 3.4 copy-start.61
  (21 other events, 29.2 us)
Sparse Core Ops, SparseCore 0:
  16.7 152.9 all-gather.4
  172.2 137.0 all-gather.6
  553.4 134.8 reduce-scatter.3
  691.6 53.7 reduce-scatter.5
  748.7 61.8 reduce-scatter.7

commit v8 on v7

--- a/solution.py
+++ b/solution.py
@@ -141,17 +141,24 @@
 
 
 class Scatter:
-    def __init__(self, line, pieces, part, from_left, from_right, send_r, send_l, recv_l, recv_r):
-        self.line, self.pieces, self.part = line, pieces, part
+    def __init__(self, line, pieces, part, from_left, from_right, send_r, send_l, recv_l, recv_r,
+                 trim=0):
+        self.line, self.pieces, self.part, self.trim = line, pieces, part, trim
         self.from_left, self.from_right = from_left, from_right
         self.send_r, self.send_l, self.recv_l, self.recv_r = send_r, send_l, recv_l, recv_r
 
+    def left_slot(self, b):
+        return max(b - self.trim, 0) if isinstance(b, int) else b - self.trim
+
+    def right_slot(self, b):
+        return min(b, self.line.n - 1 - self.trim) if isinstance(b, int) else b
+
     def _right(self, b, p):
-        return remote(self.part.at[b, p], self.from_left.at[b, p], self.send_r.at[b, p],
+        return remote(self.part.at[b, p], self.from_left.at[self.left_slot(b), p], self.send_r.at[b, p],
                       self.recv_l.at[b, p], self.line.right)
 
     def _left(self, b, p):
-        return remote(self.part.at[b, p], self.from_right.at[b, p], self.send_l.at[b, p],
+        return remote(self.part.at[b, p], self.from_right.at[self.right_slot(b), p], self.send_l.at[b, p],
                       self.recv_r.at[b, p], self.line.left)
 
     def computed(self, b, p):
@@ -180,12 +187,12 @@
 
                 @pl.when(b_left == z)
                 def _():
-                    add_own(p, self.from_left[b_left, p].astype(F32))
+                    add_own(p, self.from_left[self.left_slot(b_left), p].astype(F32))
 
                 @pl.when(b_left != z)
                 def _():
                     self.part[b_left, p] = (
-                        self.part[b_left, p].astype(F32) + self.from_left[b_left, p].astype(F32)
+                        self.part[b_left, p].astype(F32) + self.from_left[self.left_slot(b_left), p].astype(F32)
                     ).astype(BF)
                     self._right(b_left, p).start()
 
@@ -198,12 +205,12 @@
 
                 @pl.when(b_right == z)
                 def _():
-                    add_own(p, self.from_right[b_right, p].astype(F32))
+                    add_own(p, self.from_right[self.right_slot(b_right), p].astype(F32))
 
                 @pl.when(b_right != z)
                 def _():
                     self.part[b_right, p] = (
-                        self.part[b_right, p].astype(F32) + self.from_right[b_right, p].astype(F32)
+                        self.part[b_right, p].astype(F32) + self.from_right[self.right_slot(b_right), p].astype(F32)
                     ).astype(BF)
                     self._left(b_right, p).start()
 
@@ -751,6 +758,196 @@
             bytes_accessed=100 << 20),
         name="ffn_backward",
     )(g, w, xall, gate, up)
+
+
+def ffn_both_kernel(n, pieces, groups, x_ref, g_ref, w_ref, dw_ref, dx_ref, y_ref,
+                    w_v, gbuf, xv, gate_v, up_v, hid_v, y_part, y_left, y_right,
+                    x_part, x_left, x_right, stage, w_sem, own_sem, out_sem, *sems):
+    line = Line(n)
+    z = line.z
+    owners, _, shard, width = w_ref.shape
+    rows, d_model = y_ref.shape
+    tile = lane_tile(width, 256)
+    piece = d_model // pieces
+    gather_x = Gather(line, xv, *sems[:3])
+    gather_g = Gather(line, gbuf, *sems[3:6])
+    scatter_y = Scatter(line, pieces, y_part, y_left, y_right, *sems[6:10], trim=1)
+    scatter_x = Scatter(line, pieces, x_part, x_left, x_right, *sems[10:14], trim=1)
+
+    def w_copy(k, f):
+        return pltpu.make_async_copy(
+            w_ref.at[f, k], w_v.at[k, pl.ds(f * shard, shard)], w_sem.at[k, f]
+        )
+
+    own = (pltpu.make_async_copy(x_ref, xv.at[z], own_sem.at[0]),
+           pltpu.make_async_copy(g_ref, gbuf.at[z], own_sem.at[1]))
+    line.barrier()
+    gather_x.start(x_ref)
+    gather_g.start(g_ref)
+    for c in own:
+        c.start()
+    for k in range(3):
+        for f in range(owners):
+            w_copy(k, f).start()
+    for c in own:
+        c.wait()
+    for k in range(3):
+        for f in range(owners):
+            w_copy(k, f).wait()
+
+    def add_to(ref):
+        def add_own(p, value):
+            cols = slice(p * piece, (p + 1) * piece)
+            ref[:, cols] = ref[:, cols] + value
+        return add_own
+
+    add_y, add_x = add_to(y_ref), add_to(dx_ref)
+
+    def give(b, p, out, ref, part, scatter):
+        @pl.when(b == z)
+        def _():
+            ref[:, p * piece:(p + 1) * piece] = out
+
+        @pl.when(b != z)
+        def _():
+            part[b, p] = out.astype(BF)
+
+        scatter.computed(b, p)
+
+    @pl.loop(0, n)
+    def _(i):
+        b = line.order(i)
+
+        @pl.when(i > 0)
+        def _():
+            gather_x.arrive(b)
+
+        @pl.loop(0, width // tile)
+        def _(j):
+            cols = pl.ds(pl.multiple_of(j * tile, tile), tile)
+            xb = xv[b]
+            gate = dot_nn(xb, w_v[0, :, cols])
+            up = dot_nn(xb, w_v[1, :, cols])
+            gate_v[b, :, cols] = gate.astype(BF)
+            up_v[b, :, cols] = up.astype(BF)
+            hid_v[b, :, cols] = (gate * jax.nn.sigmoid(gate) * up).astype(BF)
+
+        for p in range(pieces):
+            out = dot_nt(hid_v[b], w_v[2, pl.ds(p * piece, piece)])
+            give(b, p, out, y_ref, y_part, scatter_y)
+
+        @pl.when(i > 0)
+        def _():
+            gather_g.arrive(b)
+
+        @pl.when(i == n - 1)
+        def _():
+            for t in range(1, n):
+                scatter_y.step(t, add_y)
+
+        @pl.loop(0, width // tile)
+        def _(j):
+            cols = pl.ds(pl.multiple_of(j * tile, tile), tile)
+            d_hidden = dot_nn(gbuf[b], w_v[2, :, cols])
+            gate = gate_v[b, :, cols].astype(F32)
+            up = up_v[b, :, cols].astype(F32)
+            sig = jax.nn.sigmoid(gate)
+            act = gate * sig
+            gate_v[b, :, cols] = (d_hidden * up * (sig + act * (1.0 - sig))).astype(BF)
+            up_v[b, :, cols] = (d_hidden * act).astype(BF)
+
+        for p in range(pieces):
+            sl = pl.ds(p * piece, piece)
+            out = dot_nt(gate_v[b], w_v[0, sl]) + dot_nt(up_v[b], w_v[1, sl])
+            give(b, p, out, dx_ref, x_part, scatter_x)
+
+    group = d_model // groups
+    per = group // shard
+
+    def dw_copies(k, q, slot):
+        return [
+            pltpu.make_async_copy(
+                stage.at[slot, pl.ds(s * shard, shard)], dw_ref.at[q * per + s, k],
+                out_sem.at[slot, s])
+            for s in range(per)
+        ]
+
+    def weight_unit(unit):
+        k, q = unit // groups, unit % groups
+        slot = unit % 2
+        left = (xv, xv, gbuf)[k]
+        right = (gate_v, up_v, hid_v)[k]
+        if unit >= 2:
+            for c in dw_copies((unit - 2) // groups, (unit - 2) % groups, slot):
+                c.wait()
+        lt = left[:, :, q * group:(q + 1) * group].reshape(n * rows, group)
+
+        @pl.loop(0, width // tile)
+        def _(j):
+            cols = pl.ds(pl.multiple_of(j * tile, tile), tile)
+            stage[slot, :, cols] = dot_tn(
+                lt, right[:, :, cols].reshape(n * rows, tile)
+            ).astype(BF)
+
+        for c in dw_copies(k, q, slot):
+            c.start()
+
+    units = 3 * groups
+    steps = list(scatter_x.steps())
+    done = 0
+    for index, t in enumerate(steps):
+        if t >= n:
+            scatter_y.step(t, add_y)
+        scatter_x.step(t, add_x)
+        until = units * (index + 1) // len(steps)
+        while done < until:
+            weight_unit(done)
+            done += 1
+    for unit in range(units - 2, units):
+        for c in dw_copies(unit // groups, unit % groups, unit % 2):
+            c.wait()
+    gather_x.finish()
+    gather_g.finish()
+    scatter_y.finish()
+    scatter_x.finish()
+
+
+def ffn_both(x, g, w, n):
+    rows, d_model = g.shape
+    owners, _, shard, width = w.shape
+    pieces, groups = 3, 4
+    piece = d_model // pieces
+    per = d_model // groups // shard
+    part = [pltpu.VMEM((n, pieces, rows, piece), BF)]
+    part += [pltpu.VMEM((n - 1, pieces, rows, piece), BF)] * 2
+    return pl.pallas_call(
+        functools.partial(ffn_both_kernel, n, pieces, groups),
+        out_shape=(
+            jax.ShapeDtypeStruct((owners, 3, shard, width), BF),
+            jax.ShapeDtypeStruct((rows, d_model), F32),
+            jax.ShapeDtypeStruct((rows, d_model), F32),
+        ),
+        in_specs=[ANY, ANY, ANY],
+        out_specs=[ANY, VM, VM],
+        scratch_shapes=[
+            pltpu.VMEM((3, d_model, width), BF),
+            pltpu.VMEM((n, rows, d_model), BF),
+            pltpu.VMEM((n, rows, d_model), BF),
+            pltpu.VMEM((n, rows, width), BF),
+            pltpu.VMEM((n, rows, width), BF),
+            pltpu.VMEM((n, rows, width), BF),
+        ] + part + part + [
+            pltpu.VMEM((2, d_model // groups, width), BF),
+            pltpu.SemaphoreType.DMA((3, owners)),
+            pltpu.SemaphoreType.DMA((2,)),
+            pltpu.SemaphoreType.DMA((2, per)),
+        ] + gather_sems(n) * 2 + scatter_sems(n, pieces) * 2,
+        compiler_params=params(10),
+        cost_estimate=pl.CostEstimate(
+            flops=18 * n * rows * d_model * width, transcendentals=2 * n * rows * width,
+            bytes_accessed=80 << 20),
+        name="ffn_both",
+    )(x, g, w)
 
 
 def half_turn(x):
@@ -1262,6 +1459,7 @@
         biases.append(small[:, start:start + bias_shard].reshape(-1))
 
     stream = hidden_in[0].astype(F32)
+    gradient = cotangent[0].astype(F32) * my_valid[:, None].astype(F32)
     kept = []
     for l in range(LAYERS):
         qkv_w, ffn_w = qkv_weights[l], ffn_weights[l]
@@ -1282,20 +1480,20 @@
             qkv_weights.append(next_qkv.reshape(d_model, -1))
             out_weights.append(next_out.reshape(Q_WIDTH, d_model))
         else:
-            xall, gate, up, y = ffn_forward(normed_two, ffn_w, n)
+            dw, dx, y = ffn_both(normed_two, gradient.astype(BF), ffn_w, n)
+            xall, gate, up = None, None, None
         kept.append((stream, normed, q, kvall, lse, mixed, middle, xall, gate, up,
                      qkv_w, out_w, ffn_w))
         stream = middle + y
     layer_out = stream.astype(BF)[None]
 
-    gradient = cotangent[0].astype(F32) * my_valid[:, None].astype(F32)
     small_grads = [None] * LAYERS
     big_grads = [None] * LAYERS
     for l in reversed(range(LAYERS)):
         (stream, normed, q, kvall, lse, mixed, middle, xall, gate, up,
          qkv_w, out_w, ffn_w) = kept[l]
-        dw, dx = ffn_backward(gradient.astype(BF), ffn_w, xall, gate, up, n)
         if l < LAYERS - 1:
+            dw, dx = ffn_backward(gradient.astype(BF), ffn_w, xall, gate, up, n)
             out_sum, qkv_sum, dw_sum = big_grads[l + 1]
             dx, dw_sum = lax.optimization_barrier((dx, dw_sum))
         back, gain_two = normalize_back(dx, middle, gains_mlp[l])

time: 1010 us -> 987 us (0.977)
  Pallas kernels: 837 us -> 814 us
    pallas_call x0 -> x1, Pallas kernels: none -> 187 us  [ffn_both(): pl.pallas_call(functools.partial(ffn_both_kernel, n, pieces, groups), out...]
    pallas_call x2 -> x1, Pallas kernels: 235 us -> 120 us  [ffn_backward(): pl.pallas_call(functools.partial(ffn_backward_kernel, n, pieces, groups),...]
    pallas_call x2 -> x1, Pallas kernels: 215 us -> 116 us  [ffn_forward(): pl.pallas_call(functools.partial(ffn_forward_kernel, n, pieces, count), o...]
  transfers between devices with their start and end apart: 5 -> 5, of which waited for: 2 -> 1; matrix products, arithmetic and copies ran while one was open for 10% -> 11% of each run, Pallas kernels for 45% -> 47%
where the time goes in v8:
time: 987 us; the launch traced here: 982 us
  Pallas kernels  814 us (82%)
  matrix products  64.4 us (7%)
  other arithmetic  42 us (4%)
  local copies, waits for them, and re-layouts  32.6 us (3%)
  between operations  15.4 us (2%)
  waiting for transfers between devices  13.7 us (1%)
    pallas_call x1, Pallas kernels, ffn_both(): pl.pallas_call(functools.partial(ffn_both_kernel, n, pieces, groups), out...  187 us
    pallas_call x1, Pallas kernels, reduce_all(): pl.pallas_call(functools.partial(reduce_kernel, n, owners), out_shape=(ja...  165 us
    pallas_call x1, Pallas kernels, ffn_backward(): pl.pallas_call(functools.partial(ffn_backward_kernel, n, pieces, groups),...  120 us
    pallas_call x1, Pallas kernels, ffn_forward(): pl.pallas_call(functools.partial(ffn_forward_kernel, n, pieces, count), o...  116 us
    pallas_call x2, Pallas kernels, attention_forward(): pl.pallas_call(functools.partial(attention_forward_kernel, n, owners, cou...  85 us
    pallas_call x2, Pallas kernels, attention_backward(): pl.pallas_call(functools.partial(attention_backward_kernel, n), out_shape...  82.1 us
    pallas_call x1, Pallas kernels, spread_all(): pl.pallas_call(functools.partial(spread_kernel, owners, count), out_shape...  59 us
  transfers between devices with their start and end apart: 5, of which 1 were waited for; matrix products, arithmetic and copies ran while one was open for 11% of the time, Pallas kernels for 47%

profile of v8, /device:TPU:0, one launch (start us, length us, event | category | flops | bytes accessed | tf_op | source)
XLA Modules:
  0.0 982.1 jit_solution(7278925198740064000)
XLA Ops:
  9.4 1.5 slice_bitcast_fusion.4
  11.1 1.4 copy-done.23
  12.6 1.4 copy-done.24
  14.8 1.8 pad_maximum_fusion
  16.9 1.8 pad_maximum_fusion.1
  21.8 1.2 slice_bitcast_fusion.8
  23.1 59.0 %spread_all.1 = (f32[8,16,128]{2,1,0:T(8,128)}, bf16[8,192,2048]{2,1,0:T(8,128)(2,1)}) custom-call(f32[16,128]{1,0:T(8,128)} %fusion.51.refs_0_, bf16[192,2048]{1,0:T(8,128)(2,1)} %get-tuple-element.107.refs_1_), custom_call_target="tpu_custom_call" | custom-call | flops 1048576 | bytes 157286400 | tf_op jit(solution)/shard_map/spread_all/pallas_call | solution.py:421
  87.1 1.3 fusion.57
  91.5 1.1 slice_bitcast_fusion.10
  92.6 5.9 convolution_add_fusion.3.proj_ref
  98.6 50.3 %attention_forward.2 = (bf16[256,1536]{1,0:T(8,128)(2,1)}, f32[16,256]{1,0:T(8,128)}, bf16[4,256,512]{2,1,0:T(8,128)(2,1)}, bf16[256,1536]{1,0:T(8,128)(2,1)}, bf16[8,192,1536]{2,1,0:T(8,128)(2,1)}) custom-call(f32[256,2048]{1,0:T(8,128)} %convolution_add_fusion.3.proj_ref, f32[256,128]{1,0:T(8,128)} %get-tuple-element.139.cos_ref, ...), custom_call_target="tpu_custom_call" | custom-call | flops 1610612736 | bytes 16777216 | tf_op jit(solution)/shard_map/attention_forward/pallas_call | solution.py:1024
  149.0 4.3 multiply_reduce_fusion.8
  155.0 1.1 multiply_convert_fusion.2.refs_0_
  156.1 13.6 %all-gather.5.cloned.1.call-done = bf16[24,192,2304]{2,1,0:T(8,128)(2,1)} async-done(((bf16[3,192,2304]{2,1,0:T(8,128)(2,1)}), bf16[24,192,2304]{2,1,0:T(8,128)(2,1)}) %all-gather.5.cloned.1.call-update) | async-done | bytes 21233680 | tf_op jit(solution)/shard_map/all_gather | solution.py:1449
  169.7 115.9 %ffn_forward.1 = (bf16[4,256,1536]{2,1,0:T(8,128)(2,1)}, bf16[4,256,2304]{2,1,0:T(8,128)(2,1)}, bf16[4,256,2304]{2,1,0:T(8,128)(2,1)}, f32[256,1536]{1,0:T(8,128...) custom-call(bf16[256,1536]{1,0:T(8,128)(2,1)} %multiply_convert_fusion.2.refs_0_, ...), custom_call_target="tpu_custom_call" | custom-call | flops 21743271936 | bytes 62914560 | tf_op jit(solution)/shard_map/ffn_forward/pallas_call | solution.py:557
  285.6 2.3 multiply_reduce_fusion.7
  289.1 6.0 convolution_add_fusion.2.proj_ref
  295.1 34.7 %attention_forward.3 = (bf16[256,1536]{1,0:T(8,128)(2,1)}, f32[16,256]{1,0:T(8,128)}, bf16[4,256,512]{2,1,0:T(8,128)(2,1)}, bf16[256,1536]{1,0:T(8,128)(2,1)}) custom-call(f32[256,2048]{1,0:T(8,128)} %convolution_add_fusion.2.proj_ref, f32[256,128]{1,0:T(8,128)} %get-tuple-element.139.cos_ref, f32[256,128]{1,0:T(8,128)} %get-tuple-element.140.sin_ref, ...), custom_call_target="tpu_custom_call" | custom-call | flops 1610612736 | bytes 16777216 | tf_op jit(solution)/shard_map/attention_forward/pallas_call | solution.py:1024
  329.8 4.5 multiply_reduce_fusion.6
  335.5 1.1 multiply_convert_fusion.x_ref
  336.6 187.3 %ffn_both.1 = (bf16[8,3,192,2304]{3,2,1,0:T(8,128)(2,1)}, f32[256,1536]{1,0:T(8,128)}, f32[256,1536]{1,0:T(8,128)}) custom-call(bf16[256,1536]{1,0:T(8,128)(2,1)} %multiply_convert_fusion.x_ref, bf16[256,1536]{1,0:T(8,128)(2,1)} %fusion.19.g_ref, bf16[8,3,192,2304]{3,2,1,0:T(8,128)(2,1)} %bitcast.176), custom_call_target="tpu_custom_call" | custom-call | flops 65229815808 | bytes 83886080 | tf_op jit(solution)/shard_map/ffn_both/pallas_call | solution.py:923
  524.0 1.3 copy-done.7
  527.4 2.8 fusion.18
  530.2 3.6 convolution_convert_fusion.3
  534.6 5.7 convolution_convert_fusion.5.dm_ref
  540.3 43.8 %attention_backward.2 = bf16[256,2048]{1,0:T(8,128)(2,1)} custom-call(bf16[256,1536]{1,0:T(8,128)(2,1)} %get-tuple-element.56.q_ref, bf16[4,256,512]{2,1,0:T(8,128)(2,1)} %get-tuple-element.57.kvall_ref, f32[16,256]{1,0:T(8,128)} %get-tuple-element.58.lse_ref, bf16[256,1536]{1,0:T(8,128)(2,1)} %convolution_convert_fusion.5.dm_ref, ...), custom_call_target="tpu_custom_call" | custom-call | flops 4026531840 | bytes 16777216 | tf_op jit(solution)/shard_map/attention_backward/pallas_call | solution.py:1118
  584.1 6.3 convolution_convert_fusion
  590.5 1.4 copy-done.3
  591.9 6.7 multiply_reduce_fusion.2
  599.2 1.4 convert_reduce_fusion
  601.2 3.3 fusion.56
  604.5 119.6 %ffn_backward.1 = (bf16[8,3,192,2304]{3,2,1,0:T(8,128)(2,1)}, f32[256,1536]{1,0:T(8,128)}) custom-call(bf16[256,1536]{1,0:T(8,128)(2,1)} %get-tuple-element.86.g_ref, bf16[8,3,192,2304]{3,2,1,0:T(8,128)(2,1)} %bitcast.175, bf16[4,256,1536]{2,1,0:T(8,128)(2,1)} %get-tuple-element.59.xall_ref, bf16[4,256,2304]{2,1,0:T(8,128)(2,1)} %get-tuple-element.60.gate_ref, ...), custom_call_target="tpu_custom_call" | custom-call | flops 43486543872 | bytes 104857600 | tf_op jit(solution)/shard_map/ffn_backward/pallas_call | solution.py:732
  724.2 2.4 multiply_reduce_fusion.1
  727.4 2.2 multiply_add_fusion
  729.6 5.9 convolution_convert_fusion.4.dm_ref
  735.6 38.2 %attention_backward.3 = bf16[256,2048]{1,0:T(8,128)(2,1)} custom-call(bf16[256,1536]{1,0:T(8,128)(2,1)} %get-tuple-element.65.q_ref, bf16[4,256,512]{2,1,0:T(8,128)(2,1)} %get-tuple-element.66.kvall_ref, f32[16,256]{1,0:T(8,128)} %get-tuple-element.67.lse_ref, bf16[256,1536]{1,0:T(8,128)(2,1)} %convolution_convert_fusion.4.dm_ref, ...), custom_call_target="tpu_custom_call" | custom-call | flops 4026531840 | bytes 16777216 | tf_op jit(solution)/shard_map/attention_backward/pallas_call | solution.py:1118
  773.9 7.2 fusion.13
  782.2 3.6 convolution_convert_fusion.2
  785.8 4.6 convolution_convert_fusion.1
  790.4 164.8 %reduce_all.1 = (f32[16,128]{1,0:T(8,128)}, bf16[192,1536]{1,0:T(8,128)(2,1)}, bf16[192,2048]{1,0:T(8,128)(2,1)}, bf16[3,192,2304]{2,1,0:T(8,128)(2,1)}, bf16[19...) custom-call(f32[8,16,128]{2,1,0:T(8,128)} %bitcast.160, bf16[8,192,1536]{2,1,0:T(8,128)(2,1)} %bitcast.154, ...), custom_call_target="tpu_custom_call" | custom-call | flops 1048576 | bytes 314572800 | tf_op jit(solution)/shard_map/reduce_all/pallas_call | solution.py:1369
  956.7 1.9 slice_bitcast_fusion
  960.5 2.0 slice_bitcast_fusion.1
  962.7 1.9 maximum_convert_fusion.3
  964.5 1.6 maximum_convert_fusion.4
  966.1 2.0 maximum_convert_fusion.2
  968.1 2.0 maximum_convert_fusion.1
  970.2 2.0 maximum_convert_fusion
  973.6 1.7 fusion.10
  (193 shorter events, 29.1 us)
Async XLA Ops:
  7.2 162.5 %all-gather.5.cloned.1.call-start = ((), (), s32[]{:S(2)}) async-start(), calls=%async_computation.6 | async-start | bytes 23887872 | tf_op jit(solution)/shard_map/all_gather | solution.py:1449
  16.6 320.0 %all-gather.7.cloned.1.call-start = ((), (), s32[]{:S(2)}) async-start(), calls=%async_computation.7 | async-start | bytes 23887872 | tf_op jit(solution)/shard_map/all_gather | solution.py:1467
  18.7 3.1 copy-start.25
  18.7 705.5 %reduce-scatter.4.cloned.1.call-start = ((), (), s32[]{:S(2)}) async-start(), calls=%async_computation.3 | async-start | bytes 23887872 | tf_op jit(solution)/shard_map/reduce_scatter | solution.py:1520
  82.0 7.8 copy-start.11
  82.1 8.6 copy-start.22
  83.0 8.5 copy-start.27
  85.1 7.5 copy-start.38
  90.6 2.0 copy-start.50
  148.9 5.0 copy-start.18
  148.9 5.0 copy-start.55
  285.6 3.5 copy-start.34
  285.6 3.5 copy-start.57
  329.8 5.7 copy-start.36
  523.9 1.9 copy-start.15
  523.9 1.9 copy-start.37
  523.9 249.9 %reduce-scatter.6.cloned.1.call-start = ((), (), s32[]{:S(2)}) async-start(), calls=%async_computation.4 | async-start | bytes 5308416 | tf_op jit(solution)/shard_map/reduce_scatter | solution.py:1518
  527.4 2.8 copy-start.21
  530.2 4.4 copy-start.4
  533.8 256.6 %reduce-scatter.8.cloned.1.call-start = ((), (), s32[]{:S(2)}) async-start(), calls=%async_computation.5 | async-start | bytes 7077888 | tf_op jit(solution)/shard_map/reduce_scatter | solution.py:1519
  591.9 9.4 copy-start.5
  591.9 9.4 copy-start.59
  724.2 3.2 copy-start.1
  724.2 3.2 copy-start.14
  724.2 3.1 copy-start.33
  724.2 3.1 copy-start.47
  724.2 3.1 copy-start.58
  729.6 5.9 copy-start.8
  773.8 7.3 copy-start.17
  773.8 7.5 copy-start.42
  773.8 7.5 copy-start.43
  773.8 7.5 copy-start.44
  773.8 7.5 copy-start.45
  773.9 8.2 copy-start.9
  782.2 3.6 copy-start.12
  782.2 3.6 copy-start.39
  782.2 3.6 copy-start.51
  956.7 1.9 copy-start.62
  960.5 2.0 copy-start.28
  960.5 2.2 copy-start.29
  962.7 1.9 copy-start.30
  962.7 1.9 copy-start.31
  970.2 2.1 copy-start.10
  970.2 2.7 copy-start.13
  970.2 3.4 copy-start.26
  970.2 3.4 copy-start.40
  970.2 3.4 copy-start.52
  970.2 3.4 copy-start.61
  (21 other events, 27.2 us)
Sparse Core Ops, SparseCore 0:
  16.7 152.8 all-gather.4
  172.1 137.0 all-gather.6
  524.1 138.5 reduce-scatter.3
  666.0 53.7 reduce-scatter.5
  723.0 61.7 reduce-scatter.7
